TPU v7x, 32 devices: a whole 2x2x4 slice. The times are simulated.
32 devices in a mesh: shard: 2 (over core), ctx: 4 (over z), tp: 4 (over y, x).
Axes of the slice: x: 2, y: 2, z: 4, core: 2. Of those that a mesh axis runs over, the one named last changes fastest.
Arguments:
- inputs: bfloat16 [2, 1024, 1152], P('shard', 'ctx'), may hold values from -6 to 6
- positions: int32 [2, 1024], P('shard', 'ctx'), may hold values from 0 to 1023, as said below
- cotangent: bfloat16 [2, 1024, 1152], P('shard', 'ctx'), may hold values from -6 to 6
- w_query: bfloat16 [1152, 1024], P(('shard', 'ctx'), 'tp'), may hold values from -0.1875 to 0.1875
- w_keyval: bfloat16 [1152, 512], P(('shard', 'ctx'), 'tp'), may hold values from -0.1875 to 0.1875
- w_out: bfloat16 [1152, 1024], P(('shard', 'ctx'), 'tp'), may hold values from -0.1875 to 0.1875
- w_gate: bfloat16 [1152, 6912], P(('shard', 'ctx'), 'tp'), may hold values from -0.1875 to 0.1875
- w_up: bfloat16 [1152, 6912], P(('shard', 'ctx'), 'tp'), may hold values from -0.1875 to 0.1875
- w_down: bfloat16 [1152, 6912], P(('shard', 'ctx'), 'tp'), may hold values from -0.078125 to 0.078125
- gain_input: float32 [1152], replicated, may hold values from 0.5 to 1.5
- gain_query: float32 [256], replicated, may hold values from 0.5 to 1.5
- gain_key: float32 [256], replicated, may hold values from 0.5 to 1.5
- gain_attn: float32 [1152], replicated, may hold values from 0.5 to 1.5
- gain_prefn: float32 [1152], replicated, may hold values from 0.5 to 1.5
- gain_postfn: float32 [1152], replicated, may hold values from 0.5 to 1.5
Outputs:
- block_out: float32 [2, 1024, 1152], P('shard', 'ctx')
- input_grad: float32 [2, 1024, 1152], P('shard', 'ctx')
- query_grad: float32 [1152, 1024], P(('shard', 'ctx'), 'tp')
- keyval_grad: float32 [1152, 512], P(('shard', 'ctx'), 'tp')
- output_grad: float32 [1152, 1024], P(('shard', 'ctx'), 'tp')
- gate_grad: float32 [1152, 6912], P(('shard', 'ctx'), 'tp')
- up_proj_grad: float32 [1152, 6912], P(('shard', 'ctx'), 'tp')
- down_grad: float32 [1152, 6912], P(('shard', 'ctx'), 'tp')
- gain_input_grad: float32 [1152], P(('shard', 'ctx'))
- gain_query_grad: float32 [256], P(('shard', 'ctx'))
- gain_key_grad: float32 [256], P(('shard', 'ctx'))
- gain_attn_grad: float32 [1152], P(('shard', 'ctx'))
- gain_prefn_grad: float32 [1152], P(('shard', 'ctx'))
- gain_postfn_grad: float32 [1152], P(('shard', 'ctx'))
Inputs may be any that keep to these rules, and one draw needn't show every extreme that they name: Each aligned block of 128 rows of a sequence holds 128 consecutive positions in rising order, starting at a multiple of 128; the rows of one sequence hold every position from 0 to 1023 once.
All inputs are finite; a program needn't handle non-finite values.
Results may differ from a plain program's by a relative error of at most 0.025.
Values may be sent and summed in bfloat16 or wider, within the bound.
No kernel may reach another device: no remote copies, remote signals or barrier semaphores. Data moves between devices by JAX's collectives and lax.ppermute only.
A program may use at most 128 MiB of HBM per device.

v0:
```python
import jax
import jax.numpy as jnp
from jax import lax
from jax.experimental import pallas as pl
from jax.experimental.pallas import tpu as pltpu
from jax.sharding import PartitionSpec as P


HD = 256
EPS = 1e-06
THETA = 1000000.0
SCALE = 0.0625
GELU_C = 0.7978845608028654
BF = jnp.bfloat16
F32 = jnp.float32


def rms_parts(values):
    factor = lax.rsqrt(jnp.mean(values * values, axis=-1, keepdims=True) + EPS)
    return (values * factor, factor)


def rms_back(upstream, normed, factor, gain):
    scaled = upstream * gain
    inner = jnp.mean(scaled * normed, axis=-1, keepdims=True)
    return factor * (scaled - normed * inner)


def rotate_half(values):
    half = values.shape[-1] // 2
    return jnp.concatenate([-values[..., half:], values[..., :half]], axis=-1)


def rope_tables(tok_pos):
    half = HD // 2
    freq = THETA ** (-(jnp.arange(half, dtype=F32) * 2.0) / HD)
    angle = tok_pos.astype(F32)[:, None] * freq[None, :]
    cosine = jnp.cos(angle)
    sine = jnp.sin(angle)
    return (jnp.concatenate([cosine, cosine], axis=-1), jnp.concatenate([sine, sine], axis=-1))


def rope(values, cosine, sine):
    return values * cosine + rotate_half(values) * sine


def rope_back(values, cosine, sine):
    return values * cosine - rotate_half(values * sine)


def gelu_parts(gate):
    inner = GELU_C * (gate + 0.044715 * gate * gate * gate)
    tangent = jnp.tanh(inner)
    value = 0.5 * gate * (1.0 + tangent)
    slope = 0.5 * (1.0 + tangent) + 0.5 * gate * (1.0 - tangent * tangent) * GELU_C * (
        1.0 + 3.0 * 0.044715 * gate * gate
    )
    return (value, slope)


def dot(a, b):
    return jnp.dot(a, b, preferred_element_type=F32)


def dot_nt(a, b):
    return jnp.einsum("ik,jk->ij", a, b, preferred_element_type=F32)


def dot_tn(a, b):
    return jnp.einsum("ki,kj->ij", a, b, preferred_element_type=F32)


def xor_swap(x, axis, bit):
    size = lax.axis_size(axis)
    return lax.ppermute(x, axis, [(i, i ^ bit) for i in range(size)])


def after(x, *others):
    return lax.optimization_barrier((x,) + others)[0]


def bits_of(size):
    out = []
    bit = size >> 1
    while bit:
        out.append(bit)
        bit >>= 1
    return out


def xor_order(size):
    order = [0]
    for bit in bits_of(size):
        order = order + [k ^ bit for k in order]
    return order


def gather_doubling(x, hold=None):
    pieces, order = [x], [0]
    for bit in bits_of(lax.axis_size("ctx")):
        news = []
        for k, piece in zip(order, pieces, strict=True):
            if k and hold is not None:
                piece = after(piece, hold)
            news.append(xor_swap(piece, "ctx", bit))
        pieces, order = pieces + news, order + [k ^ bit for k in order]
    return pieces


def gather_direct(x):
    n = lax.axis_size("ctx")
    if n > 4:
        return gather_doubling(x)
    return [x] + [xor_swap(x, "ctx", k) for k in xor_order(n)[1:]]


def with_other_core(pieces):
    return pieces + [xor_swap(p, "shard", 1) for p in pieces]


def natural_index():
    n = lax.axis_size("ctx")
    me = lax.axis_index("ctx")
    shard = lax.axis_index("shard")
    order = jnp.array(xor_order(n), jnp.int32)
    mine = jnp.bitwise_xor(order, me)
    return jnp.concatenate([shard * n + mine, (1 - shard) * n + mine]).astype(jnp.int32)


def in_order(pieces, index):
    rows = pieces[0].shape[0]
    if rows % 16 == 0:
        return pieces
    whole = jnp.zeros((rows * len(pieces),) + pieces[0].shape[1:], pieces[0].dtype)
    for j, piece in enumerate(pieces):
        whole = lax.dynamic_update_slice_in_dim(whole, piece, index[j] * rows, 0)
    return [whole]


def load_pieces(index_ref, refs, target, sems, lanes=None):
    rows = target.shape[0] // len(refs)
    copies = []
    for j, ref in enumerate(refs):
        if len(refs) == 1:
            where = target
        else:
            start = pl.multiple_of(index_ref[j] * rows, 16)
            where = target.at[pl.ds(start, rows)]
        source = ref
        if ref.shape[0] != rows or lanes is not None:
            source = ref.at[pl.ds(0, rows), lanes if lanes is not None else slice(None)]
        copy = pltpu.make_async_copy(source, where, sems.at[j])
        copy.start()
        copies.append(copy)
    return copies


def vmem():
    return pl.BlockSpec(memory_space=pltpu.VMEM)


def smem():
    return pl.BlockSpec(memory_space=pltpu.SMEM)


def anywhere():
    return pl.BlockSpec(memory_space=pl.ANY)


def spans(total, step):
    return [(at, min(step, total - at)) for at in range(0, total, step)]


PARAMS = pltpu.CompilerParams(vmem_limit_bytes=56 * 1024 * 1024)


def qkv_kernel(tokens, gain, index, pieces, qkv_cols):
    rows, width = tokens.shape
    count = len(pieces)
    out_cols = pieces[0].shape[1] - qkv_cols

    def body(index_ref, x_ref, g_ref, *refs):
        ins = refs[:count]
        a_ref, qkv_ref, wq_ref, wo_ref, sem_a, sem_b = refs[count:]
        copies = load_pieces(index_ref, ins, wq_ref, sem_a, pl.ds(0, qkv_cols))
        copies += load_pieces(index_ref, ins, wo_ref, sem_b, pl.ds(qkv_cols, out_cols))
        x = x_ref[...].astype(F32)
        hat, _ = rms_parts(x)
        a = (hat * g_ref[...]).astype(BF)
        a_ref[...] = a
        for copy in copies:
            copy.wait()
        qkv_ref[...] = dot(a, wq_ref[...])

    return pl.pallas_call(
        body,
        out_shape=(
            jax.ShapeDtypeStruct((rows, width), BF),
            jax.ShapeDtypeStruct((rows, qkv_cols), F32),
            jax.ShapeDtypeStruct((width, qkv_cols), BF),
            jax.ShapeDtypeStruct((width, out_cols), BF),
        ),
        in_specs=[smem(), vmem(), vmem()] + [anywhere()] * count,
        out_specs=(vmem(),) * 4,
        scratch_shapes=[pltpu.SemaphoreType.DMA((count,))] * 2,
        compiler_params=PARAMS,
        name="qkv_kernel",
    )(index, tokens, gain[None], *pieces)


def ff_forward(o_proj, tokens, g_attn, g_pre, index, gate_pieces, up_pieces):
    rows, width = tokens.shape
    count = len(gate_pieces)
    ff = gate_pieces[0].shape[1]

    def body(index_ref, o_ref, x_ref, ga_ref, gp_ref, *refs):
        gates, ups = refs[:count], refs[count : 2 * count]
        h1_ref, b_ref, mix_ref, p1_ref, p2_ref, wg, wu, sem_g, sem_u = refs[2 * count :]
        copies = load_pieces(index_ref, gates, wg, sem_g)
        copies += load_pieces(index_ref, ups, wu, sem_u)
        o_hat, _ = rms_parts(o_ref[...].astype(F32))
        h1 = x_ref[...].astype(F32) + o_hat * ga_ref[...]
        h1_ref[...] = h1
        h_hat, _ = rms_parts(h1)
        b_ref[...] = (h_hat * gp_ref[...]).astype(BF)
        for copy in copies:
            copy.wait()

        def chunk(lanes):
            b = b_ref[...]
            gate = dot(b, wg[:, lanes])
            up = dot(b, wu[:, lanes])
            act, slope = gelu_parts(gate)
            mix_ref[:, lanes] = (act * up).astype(BF)
            p1_ref[:, lanes] = (up * slope).astype(BF)
            p2_ref[:, lanes] = act.astype(BF)

        whole = ff // 256

        @pl.loop(0, whole)
        def _(c):
            chunk(pl.ds(pl.multiple_of(c * 256, 256), 256))

        if ff % 256:
            chunk(pl.ds(whole * 256, ff % 256))

    wide = jax.ShapeDtypeStruct((rows, ff), BF)
    return pl.pallas_call(
        body,
        out_shape=(
            jax.ShapeDtypeStruct((rows, width), F32),
            jax.ShapeDtypeStruct((rows, width), BF),
            wide,
            wide,
            wide,
        ),
        in_specs=[smem()] + [vmem()] * 4 + [anywhere()] * (2 * count),
        out_specs=(vmem(),) * 5,
        scratch_shapes=[
            pltpu.VMEM((width, ff), BF),
            pltpu.VMEM((width, ff), BF),
            pltpu.SemaphoreType.DMA((count,)),
            pltpu.SemaphoreType.DMA((count,)),
        ],
        compiler_params=PARAMS,
        name="ff_forward",
    )(index, o_proj, tokens, g_attn[None], g_pre[None], *gate_pieces, *up_pieces)


def ff_down(mixed, index, pieces, width):
    rows, ff = mixed.shape
    count = len(pieces)

    def body(index_ref, mix_ref, *refs):
        ins = refs[:count]
        f_ref, wd, sems = refs[count:]
        for copy in load_pieces(index_ref, ins, wd, sems):
            copy.wait()
        for at, size in spans(width, 384):
            f_ref[:, at : at + size] = dot_nt(mix_ref[...], wd[at : at + size, :]).astype(BF)

    return pl.pallas_call(
        body,
        out_shape=jax.ShapeDtypeStruct((rows, width), BF),
        in_specs=[smem(), vmem()] + [anywhere()] * count,
        out_specs=vmem(),
        scratch_shapes=[pltpu.VMEM((width, ff), BF), pltpu.SemaphoreType.DMA((count,))],
        compiler_params=PARAMS,
        name="ff_down",
    )(index, mixed, *pieces)


def ff_backward(f_sum, h1, cot, g_post, p1, p2, index, gate_pieces, up_pieces, down_pieces):
    rows, width = h1.shape
    ff = p1.shape[1]
    count = len(gate_pieces)

    def body(index_ref, f_ref, h1_ref, cot_ref, gp_ref, p1_ref, p2_ref, *refs):
        gates, ups, downs = refs[:count], refs[count : 2 * count], refs[2 * count : 3 * count]
        (out_ref, df_ref, gpost_ref, dg_ref, du_ref, dff_ref, wg, wu, wd, sem_g, sem_u, sem_d) = refs[
            3 * count :
        ]
        copies_d = load_pieces(index_ref, downs, wd, sem_d)
        copies = load_pieces(index_ref, gates, wg, sem_g)
        copies += load_pieces(index_ref, ups, wu, sem_u)
        f_hat, factor = rms_parts(f_ref[...].astype(F32))
        gain = gp_ref[...]
        out_ref[...] = h1_ref[...] + f_hat * gain
        up_stream = cot_ref[...].astype(F32)
        gpost_ref[...] = jnp.sum(up_stream * f_hat, axis=0, keepdims=True)
        df_ref[...] = rms_back(up_stream, f_hat, factor, gain).astype(BF)
        for copy in copies_d:
            copy.wait()

        def chunk(lanes):
            d_mixed = dot(df_ref[...], wd[:, lanes])
            dg_ref[:, lanes] = (d_mixed * p1_ref[:, lanes].astype(F32)).astype(BF)
            du_ref[:, lanes] = (d_mixed * p2_ref[:, lanes].astype(F32)).astype(BF)

        whole = ff // 256

        @pl.loop(0, whole)
        def _(c):
            chunk(pl.ds(pl.multiple_of(c * 256, 256), 256))

        if ff % 256:
            chunk(pl.ds(whole * 256, ff % 256))
        for copy in copies:
            copy.wait()
        for at, size in spans(width, 384):
            dff_ref[:, at : at + size] = (
                dot_nt(dg_ref[...], wg[at : at + size, :]) + dot_nt(du_ref[...], wu[at : at + size, :])
            ).astype(BF)

    return pl.pallas_call(
        body,
        out_shape=(
            jax.ShapeDtypeStruct((rows, width), F32),
            jax.ShapeDtypeStruct((rows, width), BF),
            jax.ShapeDtypeStruct((1, width), F32),
            jax.ShapeDtypeStruct((rows, ff), BF),
            jax.ShapeDtypeStruct((rows, ff), BF),
            jax.ShapeDtypeStruct((rows, width), BF),
        ),
        in_specs=[smem()] + [vmem()] * 6 + [anywhere()] * (3 * count),
        out_specs=(vmem(),) * 6,
        scratch_shapes=[pltpu.VMEM((width, ff), BF)] * 3 + [pltpu.SemaphoreType.DMA((count,))] * 3,
        compiler_params=PARAMS,
        name="ff_backward",
    )(index, f_sum, h1, cot, g_post[None], p1, p2, *gate_pieces, *up_pieces, *down_pieces)


def weight_grads(index, groups):
    blocks = index.shape[0]
    half = blocks // 2
    rows, width = groups[0][0][0].shape
    size = width // blocks
    lefts, rights, plan = [], [], []
    for group in groups:
        at, places = 0, []
        for left, right in group:
            known = [i for i, seen in enumerate(lefts) if seen is left]
            if not known:
                lefts.append(left)
                known = [len(lefts) - 1]
            places.append((known[0], len(rights), at, right.shape[1]))
            rights.append(right)
            at += right.shape[1]
        plan.append((places, at))
    turned = [left.T.reshape(blocks, size, rows) for left in lefts]
    n_left, n_right, n_group = len(lefts), len(rights), len(groups)

    def body(index_ref, *refs):
        left_refs, right_refs = refs[:n_left], refs[n_left : n_left + n_right]
        outs = refs[n_left + n_right : n_left + n_right + 2 * n_group]
        held = refs[n_left + n_right + 2 * n_group : -n_group]
        sems = refs[-n_group:]

        for g, (places, _) in enumerate(plan):
            for side, first in ((1, half), (0, 0)):

                @pl.loop(0, half)
                def _(j, g=g, places=places, side=side, first=first):
                    for li, ri, at, cols in places:
                        held[g][first + j, :, at : at + cols] = dot(
                            left_refs[li][index_ref[first + j]], right_refs[ri][...]
                        ).astype(BF)
                    pltpu.make_async_copy(
                        held[g].at[first + j], outs[2 * g + side].at[j], sems[g].at[first + j]
                    ).start()

        for g in range(n_group):
            for side, first in ((1, half), (0, 0)):
                for j in range(half):
                    pltpu.make_async_copy(
                        held[g].at[first + j], outs[2 * g + side].at[j], sems[g].at[first + j]
                    ).wait()

    out_shape = []
    for _, cols in plan:
        out_shape += [jax.ShapeDtypeStruct((half, size, cols), BF)] * 2
    outs = pl.pallas_call(
        body,
        out_shape=out_shape,
        in_specs=[smem()] + [vmem()] * (n_left + n_right),
        out_specs=[anywhere()] * (2 * n_group),
        scratch_shapes=[pltpu.VMEM((blocks, size, cols), BF) for _, cols in plan]
        + [pltpu.SemaphoreType.DMA((blocks,))] * n_group,
        compiler_params=PARAMS,
    )(index, *turned, *rights)
    return [(outs[2 * g], outs[2 * g + 1]) for g in range(n_group)]


def scatter_ctx(x):
    bits = bits_of(lax.axis_size("ctx"))
    for place, bit in enumerate(reversed(bits)):
        half = x.shape[0] // 2
        got = xor_swap(x[half:].astype(BF), "ctx", bit)
        x = x[:half].astype(F32) + got.astype(F32)
        if place + 1 < len(bits):
            x = x.astype(BF)
    return x


def scatter_pair(keep, send):
    got = xor_swap(send, "shard", 1)
    bits = bits_of(lax.axis_size("ctx"))
    half = keep.shape[0] // 2
    low = keep[:half].astype(F32) + got[:half].astype(F32)
    high = (keep[half:].astype(F32) + got[half:].astype(F32)).astype(BF)
    for place, bit in enumerate(reversed(bits)):
        got = xor_swap(high, "ctx", bit)
        if place + 1 == len(bits):
            return (low + got.astype(F32))[0]
        low = low.astype(BF).astype(F32)
        half = half // 2
        high = (low[half:] + got[half:].astype(F32)).astype(BF)
        low = low[:half] + got[:half].astype(F32)


def all_reduce_tp(part):
    n = lax.axis_size("tp")
    rows = part.shape[0]
    sent = part.astype(BF).reshape((n, rows // n) + part.shape[1:])
    got = lax.all_to_all(sent, "tp", 0, 0)
    summed = jnp.sum(got.astype(F32), axis=0).astype(BF)
    return lax.all_gather(summed, "tp", axis=0, tiled=True)


def layer(
    inputs,
    positions,
    cotangent,
    w_query,
    w_keyval,
    w_out,
    w_gate,
    w_up,
    w_down,
    gain_input,
    gain_query,
    gain_key,
    gain_attn,
    gain_prefn,
    gain_postfn,
):
    tokens = inputs[0]
    cot = cotangent[0]
    tok_pos = positions[0]
    n_ctx = lax.axis_size("ctx")
    n_tp = lax.axis_size("tp")
    count, width = tokens.shape
    qc = w_query.shape[1]
    kc = w_keyval.shape[1]
    heads = qc // HD
    index = natural_index()
    rows = w_query.shape[0]

    group = 128
    cols = qc + kc + w_out.shape[1]
    starts = (tok_pos[::group] // group).astype(BF)
    tail = jnp.zeros((16, cols), BF).at[0, : count // group].set(starts)
    first = jnp.concatenate([jnp.concatenate([w_query, w_keyval, w_out], axis=1), tail], axis=0)
    first_mine = gather_direct(first)
    first_all = with_other_core(first_mine)
    block_starts = jnp.stack([p[rows, : count // group] for p in first_mine]).astype(jnp.int32)
    pos_all = (block_starts.reshape(-1, 1) * group + jnp.arange(group, dtype=jnp.int32)[None]).reshape(-1)
    if rows % 16:
        first_all = [p[:rows] for p in first_all]
    first_all = in_order(first_all, index)
    normed_in, qkv, wqkv, wo = qkv_kernel(tokens, gain_input, index, first_all, qc + kc)

    cos_all, sin_all = rope_tables(pos_all)
    cosine, sine = cos_all[:count], sin_all[:count]
    q_raw = qkv[:, :qc].reshape(count, heads, HD)
    kv_part = qkv[:, qc:].astype(BF)

    kv_cols = jnp.concatenate(gather_direct(kv_part), axis=0)
    spread = jnp.broadcast_to(kv_cols[None], (n_tp,) + kv_cols.shape)
    kv_stack = lax.all_to_all(spread, "tp", 0, 0)
    kv_raw = jnp.concatenate([kv_stack[i] for i in range(n_tp)], axis=1)
    k_hat_all, k_factor_all = rms_parts(kv_raw[:, :HD].astype(F32))
    keys = rope(k_hat_all * gain_key, cos_all, sin_all).astype(BF)
    values = kv_raw[:, HD:]

    q_hat, q_factor = rms_parts(q_raw)
    queries = rope(q_hat * gain_query, cosine[:, None, :], sine[:, None, :]).astype(BF)
    visible = pos_all[None, :] <= tok_pos[:, None]

    scores, lses, outs = [], [], []
    for h in range(heads):
        s = dot_nt(queries[:, h], keys) * SCALE
        s = jnp.where(visible, s, -1e30)
        top = jnp.max(s, axis=-1, keepdims=True)
        w = jnp.exp(s - top)
        tot = jnp.sum(w, axis=-1, keepdims=True)
        outs.append((dot(w.astype(BF), values) / tot).astype(BF))
        lses.append(top + jnp.log(tot))
        scores.append(s)
    attn = jnp.concatenate(outs, axis=1)

    o_part = dot_nt(attn, wo).astype(BF)
    gate_mine = gather_doubling(w_gate, kv_cols)
    up_mine = gather_doubling(w_up, kv_stack)
    o_bf = all_reduce_tp(o_part)
    down_mine = gather_doubling(w_down, o_bf)
    gate_all = in_order(with_other_core([after(p, o_bf) for p in gate_mine]), index)
    up_all = in_order(with_other_core([after(p, o_bf) for p in up_mine]), index)
    resid, normed_ff, mixed, p1, p2 = ff_forward(
        o_bf, tokens, gain_attn, gain_prefn, index, gate_all, up_all
    )
    down_all = in_order(with_other_core([after(p, o_bf) for p in down_mine]), index)
    f_bf = all_reduce_tp(ff_down(mixed, index, down_all, width))
    block_out, d_f, grad_postfn, d_gate, d_up, d_ff_part = ff_backward(
        f_bf, resid, cot, gain_postfn, p1, p2, index, gate_all, up_all, down_all
    )
    d_ff = all_reduce_tp(d_ff_part).astype(F32)
    (pair,) = weight_grads(index, [[(d_f, mixed)]])
    grad_down = scatter_pair(*pair)
    left = after(normed_ff, d_ff)
    pairs = weight_grads(index, [[(left, d_gate)], [(left, d_up)]])
    grad_gate = scatter_pair(*pairs[0])
    grad_up = scatter_pair(*pairs[1])

    o_hat, o_factor = rms_parts(o_bf.astype(F32))
    h_hat, h_factor = rms_parts(resid)
    upstream = cot.astype(F32)
    grad_prefn = jnp.sum(d_ff * h_hat, axis=0)
    d_resid = upstream + rms_back(d_ff, h_hat, h_factor, gain_prefn)
    grad_attn = jnp.sum(d_resid * o_hat, axis=0)
    d_o = rms_back(d_resid, o_hat, o_factor, gain_attn).astype(BF)
    d_attn = dot(d_o, wo).astype(BF)
    delta = jnp.sum(
        (d_attn.astype(F32) * attn.astype(F32)).reshape(count, heads, HD), axis=-1, keepdims=True
    )

    d_keys = jnp.zeros(keys.shape, F32)
    d_values = jnp.zeros(values.shape, F32)
    d_queries = []
    for h in range(heads):
        dah = d_attn[:, h * HD : (h + 1) * HD]
        probs = jnp.exp(scores[h] - lses[h])
        d_probs = dot_nt(dah, values)
        d_scores = (probs * (d_probs - delta[:, h])).astype(BF)
        d_queries.append(dot(d_scores, keys))
        d_keys = d_keys + dot_tn(d_scores, queries[:, h])
        d_values = d_values + dot_tn(probs.astype(BF), dah)

    quarter = count // n_tp
    dkv = jnp.concatenate([d_keys, d_values], axis=1).astype(BF)
    dkv = dkv.reshape(n_ctx, n_tp, quarter, 2 * HD).transpose(1, 0, 2, 3)
    dkv = lax.all_to_all(dkv, "tp", 0, 0)
    dkv = jnp.sum(dkv.astype(F32), axis=0).reshape(n_ctx * quarter, 2 * HD)
    dkv = scatter_ctx(dkv)
    at = lax.axis_index("tp") * quarter
    cos_q = lax.dynamic_slice_in_dim(cosine, at, quarter, 0)
    sin_q = lax.dynamic_slice_in_dim(sine, at, quarter, 0)
    khat_q = lax.dynamic_slice_in_dim(k_hat_all[:count], at, quarter, 0)
    kfac_q = lax.dynamic_slice_in_dim(k_factor_all[:count], at, quarter, 0)
    d_knorm = rope_back(dkv[:, :HD] * SCALE, cos_q, sin_q)
    grad_key_part = jnp.sum(d_knorm * khat_q, axis=0)
    d_kraw = rms_back(d_knorm, khat_q, kfac_q, gain_key)
    dkv_raw = jnp.concatenate([d_kraw, dkv[:, HD:]], axis=1).astype(BF)

    d_qnorm = rope_back(
        jnp.stack(d_queries, axis=1) * SCALE, cosine[:, None, :], sine[:, None, :]
    )
    grad_query_part = jnp.sum(d_qnorm * q_hat, axis=(0, 1))
    d_qraw = rms_back(d_qnorm, q_hat, q_factor, gain_query).astype(BF).reshape(count, qc)

    tail = jnp.concatenate([grad_query_part, grad_key_part])[None].astype(BF)
    tail = jnp.concatenate([tail, jnp.zeros((15, 2 * HD), BF)], axis=0)
    dkv_all = lax.all_gather(jnp.concatenate([dkv_raw, tail], axis=0), "tp", axis=0)
    dkv_full = dkv_all[:, :quarter].reshape(count, 2 * HD)
    gain_sums = jnp.sum(dkv_all[:, quarter].astype(F32), axis=0)
    dkv_cols = lax.dynamic_slice_in_dim(dkv_full, lax.axis_index("tp") * kc, kc, 1)
    d_qkv = jnp.concatenate([d_qraw, dkv_cols], axis=1)
    (pair,) = weight_grads(index, [[(normed_in, d_qkv), (d_o, attn)]])
    grad_heads = scatter_pair(*pair)
    d_in = all_reduce_tp(dot_nt(d_qkv, wqkv)).astype(F32)
    x_hat, x_factor = rms_parts(tokens.astype(F32))
    grad_input = jnp.sum(d_in * x_hat, axis=0)
    input_grad = d_resid + rms_back(d_in, x_hat, x_factor, gain_input)

    blocks = 2 * n_ctx
    wide = jnp.stack([grad_input, grad_attn, grad_prefn, grad_postfn[0]])
    both = jnp.concatenate(
        [
            wide.reshape(4, blocks, -1).transpose(1, 0, 2).reshape(blocks, -1),
            gain_sums.reshape(2, blocks, -1).transpose(1, 0, 2).reshape(blocks, -1),
        ],
        axis=1,
    )
    both = jnp.take(both, index, axis=0)[:, None]
    mine = scatter_pair(both[:n_ctx], both[n_ctx:].astype(BF))[0]
    small = HD // blocks
    size = width // blocks
    base = 4 * size
    return (
        block_out[None],
        input_grad[None],
        grad_heads[:, :qc],
        grad_heads[:, qc : qc + kc],
        grad_heads[:, qc + kc :],
        grad_gate,
        grad_up,
        grad_down,
        mine[:size],
        mine[base : base + small],
        mine[base + small :],
        mine[size : 2 * size],
        mine[2 * size : 3 * size],
        mine[3 * size : 4 * size],
    )


def solution(mesh):
    rows = P(("shard", "ctx"), "tp")
    tokens = P("shard", "ctx", None)
    gain = P(("shard", "ctx"))
    return jax.shard_map(
        layer,
        mesh=mesh,
        in_specs=(tokens, P("shard", "ctx"), tokens) + (rows,) * 6 + (P(),) * 6,
        out_specs=(tokens, tokens) + (rows,) * 6 + (gain,) * 6,
        check_vma=False,
    )
```

profile of v0, /device:TPU:0, one launch (start us, length us, event | category | flops | bytes accessed | tf_op | source)
XLA Modules:
  0.0 490.9 jit_solution(2815738887838897698)
XLA Ops:
  3.0 4.7 collective-permute-start.2
  8.3 2.3 collective-permute-start.10
  10.6 1.3 broadcast_in_dim.27.g_ref
  13.6 5.2 %collective-permute-done.1.refs_2_ = bf16[160,640]{1,0:T(8,128)(2,1)S(1)} collective-permute-done((bf16[160,640]{1,0:T(8,128)(2,1)S(1)}, bf16[160,640]{1,0:T(8,128)(2,1)S(1)}, u32[]{:S(2)}, u32[]{:S(2)}) %collective-permute-start.1) | collective-permute-done | bytes 204832 | tf_op jit(solution)/shard_map/ppermute | solution.py:75
  18.8 18.4 %collective-permute-done.refs_1_ = bf16[160,640]{1,0:T(8,128)(2,1)S(1)} collective-permute-done((bf16[160,640]{1,0:T(8,128)(2,1)S(1)}, bf16[160,640]{1,0:T(8,128)(2,1)S(1)}, u32[]{:S(2)}, u32[]{:S(2)}) %collective-permute-start) | collective-permute-done | bytes 204832 | tf_op jit(solution)/shard_map/ppermute | solution.py:75
  37.9 1.9 multiply_sine_fusion
  40.8 4.2 qkv_kernel.1
  46.0 2.5 collective-permute-start.9
  51.5 5.1 %collective-permute-done.9 = bf16[256,128]{1,0:T(8,128)(2,1)S(1)} collective-permute-done((bf16[256,128]{1,0:T(8,128)(2,1)S(1)}, bf16[256,128]{1,0:T(8,128)(2,1)S(1)}, u32[]{:S(2)}, u32[]{:S(2)}) %collective-permute-start.9) | collective-permute-done | bytes 65568 | tf_op jit(solution)/shard_map/ppermute | solution.py:75
  56.7 18.8 %collective-permute-done.7 = bf16[256,128]{1,0:T(8,128)(2,1)S(1)} collective-permute-done((bf16[256,128]{1,0:T(8,128)(2,1)S(1)}, bf16[256,128]{1,0:T(8,128)(2,1)S(1)}, u32[]{:S(2)}, u32[]{:S(2)}) %collective-permute-start.7) | collective-permute-done | bytes 65568 | tf_op jit(solution)/shard_map/ppermute | solution.py:75
  76.6 3.8 all-to-all-start
  81.5 12.4 %all-to-all-done = bf16[4,1024,128]{2,1,0:T(8,128)(2,1)S(1)} async-done(((bf16[4,1024,128]{2,1,0:T(8,128)(2,1)}), bf16[4,1024,128]{2,1,0:T(8,128)(2,1)S(1)}, u32[]{:S(2)}, u32[]{:S(2)}) %all-to-all-start) | async-done | bytes 1048608 | tf_op jit(solution)/shard_map/all_to_all | solution.py:500
  98.9 3.6 all-to-all-start.1
  102.8 2.9 collective-permute-start.11
  105.7 2.0 collective-permute-start.12
  107.7 3.0 all-to-all-done.1
  110.8 11.3 %all_gather.18.o_ref = bf16[256,1152]{1,0:T(8,128)(2,1)} all-gather(bf16[64,1152]{1,0:T(8,128)(2,1)S(1)} %reduce_sum.222), channel_id=1, replica_groups=mesh['shard'=2,'ctx'=4,'tp'=4] {'tp'}, dimensions={0}, use_global_device_ids=true | all-gather | bytes 737280 | tf_op jit(solution)/shard_map/all_gather | solution.py:447
  122.1 5.1 %collective-permute-done.24.refs_1_.refs_17_ = bf16[144,1728]{1,0:T(8,128)(2,1)S(1)} collective-permute-done((bf16[144,1728]{1,0:T(8,128)(2,1)S(1)}, bf16[144,1728]{1,0:T(8,128)(2,1)S(1)}, u32[]{:S(2)}, u32[]{:S(2)}) %collective-permute-start.24) | collective-permute-done | bytes 497696 | tf_op jit(solution)/shard_map/ppermute | solution.py:75
  127.2 2.1 collective-permute-done.11.refs_2_
  129.3 11.1 %collective-permute-done.18.refs_10_ = bf16[144,1728]{1,0:T(8,128)(2,1)} collective-permute-done((bf16[144,1728]{1,0:T(8,128)(2,1)}, bf16[144,1728]{1,0:T(8,128)(2,1)}, u32[]{:S(2)}, u32[]{:S(2)}) %collective-permute-start.18) | collective-permute-done | bytes 497696 | tf_op jit(solution)/shard_map/ppermute | solution.py:75
  140.3 11.1 %collective-permute-done.12.refs_3_ = bf16[144,1728]{1,0:T(8,128)(2,1)} collective-permute-done((bf16[144,1728]{1,0:T(8,128)(2,1)}, bf16[144,1728]{1,0:T(8,128)(2,1)}, u32[]{:S(2)}, u32[]{:S(2)}) %collective-permute-start.12) | collective-permute-done | bytes 497696 | tf_op jit(solution)/shard_map/ppermute | solution.py:75
  151.4 11.1 %collective-permute-done.25.refs_2_.refs_18_ = bf16[144,1728]{1,0:T(8,128)(2,1)} collective-permute-done((bf16[144,1728]{1,0:T(8,128)(2,1)S(1)}, bf16[144,1728]{1,0:T(8,128)(2,1)}, u32[]{:S(2)}, u32[]{:S(2)}) %collective-permute-start.25) | collective-permute-done | bytes 497696 | tf_op jit(solution)/shard_map/ppermute | solution.py:75
  162.5 11.0 %collective-permute-done.19.refs_11_ = bf16[144,1728]{1,0:T(8,128)(2,1)S(1)} collective-permute-done((bf16[144,1728]{1,0:T(8,128)(2,1)}, bf16[144,1728]{1,0:T(8,128)(2,1)S(1)}, u32[]{:S(2)}, u32[]{:S(2)}) %collective-permute-start.19) | collective-permute-done | bytes 497696 | tf_op jit(solution)/shard_map/ppermute | solution.py:75
  174.0 8.7 %collective-permute-done.26.refs_3_.refs_19_ = bf16[144,1728]{1,0:T(8,128)(2,1)} collective-permute-done((bf16[144,1728]{1,0:T(8,128)(2,1)S(1)}, bf16[144,1728]{1,0:T(8,128)(2,1)}, u32[]{:S(2)}, u32[]{:S(2)}) %collective-permute-start.26) | collective-permute-done | bytes 497696 | tf_op jit(solution)/shard_map/ppermute | solution.py:75
  188.0 10.8 %ff_forward.1 = (f32[256,1152]{1,0:T(8,128)}, bf16[256,1152]{1,0:T(8,128)(2,1)}, bf16[256,1728]{1,0:T(8,128)(2,1)}, bf16[256,1728]{1,0:T(8,128)(2,1)}, bf16[256,1728]{1,0:T(8,128)(2,1)}) custom-call(s32[8]{0:T(128)} %get-tuple-element.113.index_ref, bf16[256,1152]{1,0:T(8,128)(2,1)} %all_gather.18.o_ref, bf16[256,1152]{1,0:T(8,128)(2,1)} %bitcast.114, ...), custom_call_target="tpu_custom_call" | custom-call | tf_op jit(solution)/shard_map/ff_forward/pallas_call | solution.py:248
  198.9 5.8 %ff_down.1 = bf16[256,1152]{1,0:T(8,128)(2,1)} custom-call(s32[8]{0:T(128)} %get-tuple-element.113.index_ref, bf16[256,1728]{1,0:T(8,128)(2,1)} %get-tuple-element.76.mix_ref.refs_1_, bf16[144,1728]{1,0:T(8,128)(2,1)} %refs_16_, bf16[144,1728]{1,0:T(8,128)(2,1)} %copy-done.16, bf16[144,1728]{1,0:T(8,128)(2,1)} %collective-permute-done.25.refs_2_.refs_18_, ...), custom_call_target="tpu_custom_call" | custom-call | tf_op jit(solution)/shard_map/ff_down/pallas_call | solution.py:282
  204.7 3.9 all-to-all-start.2
  208.7 1.7 slice.418
  210.7 7.2 %all-to-all-done.2 = bf16[4,64,1152]{2,1,0:T(8,128)(2,1)S(1)} async-done(((bf16[4,64,1152]{2,1,0:T(8,128)(2,1)}), bf16[4,64,1152]{2,1,0:T(8,128)(2,1)S(1)}, u32[]{:S(2)}, u32[]{:S(2)}) %all-to-all-start.2) | async-done | bytes 589856 | tf_op jit(solution)/shard_map/all_to_all | solution.py:445
  218.0 10.9 %all_gather.19.f_ref = bf16[256,1152]{1,0:T(8,128)(2,1)} all-gather(bf16[64,1152]{1,0:T(8,128)(2,1)S(1)} %reduce_sum.223), channel_id=1, replica_groups=mesh['shard'=2,'ctx'=4,'tp'=4] {'tp'}, dimensions={0}, use_global_device_ids=true | all-gather | bytes 737280 | tf_op jit(solution)/shard_map/all_gather | solution.py:447
  228.9 12.9 %ff_backward.1 = (f32[256,1152]{1,0:T(8,128)}, bf16[256,1152]{1,0:T(8,128)(2,1)}, f32[1,1152]{1,0:T(1,128)}, bf16[256,1728]{1,0:T(8,128)(2,1)}, bf16[256,1728]{1,0:T(8,128)(2,1)}, /*index=5*/bf16[256,1152]{1,0:T(8,128)(2,1)}) custom-call(s32[8]{0:T(128)} %get-tuple-element.113.index_ref, bf16[256,1152]{1,0:T(8,128)(2,1)} %all_gather.19.f_ref, ...), custom_call_target="tpu_custom_call" | custom-call | tf_op jit(solution)/shard_map/ff_backward/pallas_call | solution.py:335
  241.8 3.6 all-to-all-start.3
  245.7 6.7 %all-to-all-done.3 = bf16[4,64,1152]{2,1,0:T(8,128)(2,1)S(1)} async-done(((bf16[4,64,1152]{2,1,0:T(8,128)(2,1)}), bf16[4,64,1152]{2,1,0:T(8,128)(2,1)S(1)}, u32[]{:S(2)}, u32[]{:S(2)}) %all-to-all-start.3) | async-done | bytes 589856 | tf_op jit(solution)/shard_map/all_to_all | solution.py:445
  252.5 10.4 %all_gather.20 = bf16[256,1152]{1,0:T(8,128)(2,1)S(1)} all-gather(bf16[64,1152]{1,0:T(8,128)(2,1)S(1)} %reduce_sum.225), channel_id=1, replica_groups=mesh['shard'=2,'ctx'=4,'tp'=4] {'tp'}, dimensions={0}, use_global_device_ids=true | all-gather | bytes 737280 | tf_op jit(solution)/shard_map/all_gather | solution.py:447
  269.3 4.3 all-to-all-start.4
  273.6 1.4 convolution_multiply_fusion.1
  275.3 7.8 %all-to-all-done.4 = bf16[4,4,64,512]{3,2,1,0:T(8,128)(2,1)} async-done(((bf16[4,4,64,512]{3,2,1,0:T(8,128)(2,1)}), bf16[4,4,64,512]{3,2,1,0:T(8,128)(2,1)}, u32[]{:S(2)}, u32[]{:S(2)}) %all-to-all-start.4) | async-done | bytes 1048608 | tf_op jit(solution)/shard_map/all_to_all | solution.py:572
  283.0 1.4 convert_reduce_fusion
  284.6 4.9 collective-permute-done.31
  290.1 4.8 collective-permute-done.32
  297.1 10.7 %all-gather = bf16[320,512]{1,0:T(8,128)(2,1)S(1)} all-gather(bf16[80,512]{1,0:T(8,128)(2,1)S(1)} %maximum_maximum_fusion), channel_id=2, replica_groups=mesh['shard'=2,'ctx'=4,'tp'=4] {'tp'}, dimensions={0}, use_global_device_ids=true | all-gather | bytes 409600 | tf_op jit(solution)/shard_map/all_gather | solution.py:593
  307.9 1.4 convolution_convert_fusion.1
  309.2 3.7 all-to-all-start.5
  314.0 2.2 copy.54
  317.4 4.7 shard_map.265
  322.3 7.6 %shard_map.264 = (bf16[4,144,1728]{2,1,0:T(8,128)(2,1)}, bf16[4,144,1728]{2,1,0:T(8,128)(2,1)}, bf16[4,144,1728]{2,1,0:T(8,128)(2,1)}, bf16[4,144,1728]{2,1,0:T(8,128)(2,1)}) custom-call(s32[8]{0:T(128)} %get-tuple-element.113.index_ref, bf16[8,144,256]{2,1,0:T(8,128)(2,1)} %bitcast.121, bf16[256,1728]{1,0:T(8,128)(2,1)} %get-tuple-element.92.refs_1_, ...), custom_call_target="tpu_custom_call" | custom-call | tf_op jit(solution)/shard_map/pallas_call | solution.py:402
  332.0 11.2 %all_gather.23 = bf16[256,1152]{1,0:T(8,128)(2,1)S(1)} all-gather(bf16[64,1152]{1,0:T(8,128)(2,1)S(1)} %reduce_sum.236), channel_id=1, replica_groups=mesh['shard'=2,'ctx'=4,'tp'=4] {'tp'}, dimensions={0}, use_global_device_ids=true | all-gather | bytes 737280 | tf_op jit(solution)/shard_map/all_gather | solution.py:447
  345.6 3.8 shard_map.263
  350.0 3.6 collective-permute-done.46
  353.7 1.4 fusion.11
  355.1 3.0 collective-permute-done.47
  359.4 2.1 add_convert_fusion
  361.8 2.1 collective-permute-start.34
  363.9 2.2 add_convert_fusion.4
  366.0 1.4 collective-permute-start.37
  367.4 29.7 %collective-permute-done.34 = bf16[2,144,640]{2,1,0:T(8,128)(2,1)S(1)} collective-permute-done((bf16[2,144,640]{2,1,0:T(8,128)(2,1)S(1)}, bf16[2,144,640]{2,1,0:T(8,128)(2,1)S(1)}, u32[]{:S(2)}, u32[]{:S(2)}) %collective-permute-start.34) | collective-permute-done | bytes 368672 | tf_op jit(solution)/shard_map/ppermute | solution.py:75
  397.3 2.0 add_convert_fusion.2
  399.3 2.1 collective-permute-start.40
  401.5 17.3 %collective-permute-done.35 = bf16[1,144,640]{2,1,0:T(8,128)(2,1)S(1)} collective-permute-done((bf16[1,144,640]{2,1,0:T(8,128)(2,1)S(1)}, bf16[1,144,640]{2,1,0:T(8,128)(2,1)S(1)}, u32[]{:S(2)}, u32[]{:S(2)}) %collective-permute-start.35) | collective-permute-done | bytes 184352 | tf_op jit(solution)/shard_map/ppermute | solution.py:75
  420.3 3.4 collective-permute-start.44
  423.7 14.1 %collective-permute-done.37 = bf16[2,144,1728]{2,1,0:T(8,128)(2,1)S(1)} collective-permute-done((bf16[2,144,1728]{2,1,0:T(8,128)(2,1)S(1)}, bf16[2,144,1728]{2,1,0:T(8,128)(2,1)S(1)}, u32[]{:S(2)}, u32[]{:S(2)}) %collective-permute-start.37) | collective-permute-done | bytes 995360 | tf_op jit(solution)/shard_map/ppermute | solution.py:75
  438.0 19.0 %collective-permute-done.40 = bf16[2,144,1728]{2,1,0:T(8,128)(2,1)S(1)} collective-permute-done((bf16[2,144,1728]{2,1,0:T(8,128)(2,1)S(1)}, bf16[2,144,1728]{2,1,0:T(8,128)(2,1)S(1)}, u32[]{:S(2)}, u32[]{:S(2)}) %collective-permute-start.40) | collective-permute-done | bytes 995360 | tf_op jit(solution)/shard_map/ppermute | solution.py:75
  458.3 25.6 %collective-permute-done.38 = bf16[1,144,1728]{2,1,0:T(8,128)(2,1)S(1)} collective-permute-done((bf16[1,144,1728]{2,1,0:T(8,128)(2,1)S(1)}, bf16[1,144,1728]{2,1,0:T(8,128)(2,1)S(1)}, u32[]{:S(2)}, u32[]{:S(2)}) %collective-permute-start.38) | collective-permute-done | bytes 497696 | tf_op jit(solution)/shard_map/ppermute | solution.py:75
  485.0 4.7 collective-permute-done.41
  (296 shorter events, 47.9 us)
Async XLA Ops:
  2.4 37.6 %copy-start.29 = (bf16[160,640]{1,0:T(8,128)(2,1)}, bf16[160,640]{1,0:T(8,128)(2,1)S(1)}, u32[]{:S(2)}) copy-start(bf16[160,640]{1,0:T(8,128)(2,1)S(1)} %fusion.56.refs_0_) | copy-start | bytes 614404
  2.4 37.4 %collective-permute-start.3 = (bf16[160,640]{1,0:T(8,128)(2,1)S(1)}, bf16[160,640]{1,0:T(8,128)(2,1)S(1)}, u32[]{:S(2)}, u32[]{:S(2)}) collective-permute-start(bf16[160,640]{1,0:T(8,128)(2,1)S(1)} %fusion.56.refs_0_), channel_id=1, source_target_pairs={{0,16},{16,0},{1,17},{17,1},{2,18},{18,2},{3,19},{19,3},{4,20},{20... | collective-permute-start | bytes 614408 | tf_op jit(solution)/shard_map/ppermute | solution.py:75
  3.0 10.7 %collective-permute-start.2 = (bf16[160,640]{1,0:T(8,128)(2,1)S(1)}, bf16[160,640]{1,0:T(8,128)(2,1)S(1)}, u32[]{:S(2)}, u32[]{:S(2)}) collective-permute-start(bf16[160,640]{1,0:T(8,128)(2,1)S(1)} %fusion.56.refs_0_), channel_id=1, source_target_pairs={{0,12},{4,8},{8,4},{12,0},{1,13},{5,9},{9,5},{13,1},{2,14},{6,10},... | collective-permute-start | bytes 614408 | tf_op jit(solution)/shard_map/ppermute | solution.py:75
  7.6 11.2 %collective-permute-start.1 = (bf16[160,640]{1,0:T(8,128)(2,1)S(1)}, bf16[160,640]{1,0:T(8,128)(2,1)S(1)}, u32[]{:S(2)}, u32[]{:S(2)}) collective-permute-start(bf16[160,640]{1,0:T(8,128)(2,1)S(1)} %fusion.56.refs_0_), channel_id=1, source_target_pairs={{0,4},{4,0},{8,12},{12,8},{1,5},{5,1},{9,13},{13,9},{2,6},{6,2},{1... | collective-permute-start | bytes 614408 | tf_op jit(solution)/shard_map/ppermute | solution.py:75
  7.6 29.6 %collective-permute-start = (bf16[160,640]{1,0:T(8,128)(2,1)S(1)}, bf16[160,640]{1,0:T(8,128)(2,1)S(1)}, u32[]{:S(2)}, u32[]{:S(2)}) collective-permute-start(bf16[160,640]{1,0:T(8,128)(2,1)S(1)} %fusion.56.refs_0_), channel_id=1, source_target_pairs={{0,8},{4,12},{8,0},{12,4},{1,9},{5,13},{9,1},{13,5},{2,10},{6,14},... | collective-permute-start | bytes 614408 | tf_op jit(solution)/shard_map/ppermute | solution.py:75
  8.3 97.4 %collective-permute-start.10 = (bf16[144,1728]{1,0:T(8,128)(2,1)}, bf16[144,1728]{1,0:T(8,128)(2,1)}, u32[]{:S(2)}, u32[]{:S(2)}) collective-permute-start(bf16[144,1728]{1,0:T(8,128)(2,1)} %refs_0_.2), channel_id=1, source_target_pairs={{0,8},{4,12},{8,0},{12,4},{1,9},{5,13},{9,1},{13,5},{2,10},{6,14},... | collective-permute-start | bytes 1493000 | tf_op jit(solution)/shard_map/ppermute | solution.py:75
  13.6 26.4 %copy-start.41 = (bf16[160,640]{1,0:T(8,128)(2,1)}, bf16[160,640]{1,0:T(8,128)(2,1)S(1)}, u32[]{:S(2)}) copy-start(bf16[160,640]{1,0:T(8,128)(2,1)S(1)} %collective-permute-done.2.refs_3_) | copy-start | bytes 614404
  18.8 21.2 %copy-start.42 = (bf16[160,640]{1,0:T(8,128)(2,1)}, bf16[160,640]{1,0:T(8,128)(2,1)S(1)}, u32[]{:S(2)}) copy-start(bf16[160,640]{1,0:T(8,128)(2,1)S(1)} %collective-permute-done.1.refs_2_) | copy-start | bytes 614404
  37.4 2.5 collective-permute-start.6
  37.4 2.6 collective-permute-start.5
  37.9 2.1 collective-permute-start.4
  39.9 67.8 %collective-permute-start.17 = (bf16[144,1728]{1,0:T(8,128)(2,1)}, bf16[144,1728]{1,0:T(8,128)(2,1)}, u32[]{:S(2)}, u32[]{:S(2)}) collective-permute-start(bf16[144,1728]{1,0:T(8,128)(2,1)} %refs_8_.1), channel_id=1, source_target_pairs={{0,8},{4,12},{8,0},{12,4},{1,9},{5,13},{9,1},{13,5},{2,10},{6,14},... | collective-permute-start | bytes 1493000 | tf_op jit(solution)/shard_map/ppermute | solution.py:75
  46.0 10.7 %collective-permute-start.9 = (bf16[256,128]{1,0:T(8,128)(2,1)S(1)}, bf16[256,128]{1,0:T(8,128)(2,1)S(1)}, u32[]{:S(2)}, u32[]{:S(2)}) collective-permute-start(bf16[256,128]{1,0:T(8,128)(2,1)S(1)} %slice.602), channel_id=1, source_target_pairs={{0,12},{4,8},{8,4},{12,0},{1,13},{5,9},{9,5},{13,1},{2,14},{6,10},... | collective-permute-start | bytes 196616 | tf_op jit(solution)/shard_map/ppermute | solution.py:75
  48.4 8.2 %collective-permute-start.8 = (bf16[256,128]{1,0:T(8,128)(2,1)S(1)}, bf16[256,128]{1,0:T(8,128)(2,1)S(1)}, u32[]{:S(2)}, u32[]{:S(2)}) collective-permute-start(bf16[256,128]{1,0:T(8,128)(2,1)S(1)} %slice.602), channel_id=1, source_target_pairs={{0,4},{4,0},{8,12},{12,8},{1,5},{5,1},{9,13},{13,9},{2,6},{6,2},{1... | collective-permute-start | bytes 196616 | tf_op jit(solution)/shard_map/ppermute | solution.py:75
  49.4 26.0 %collective-permute-start.7 = (bf16[256,128]{1,0:T(8,128)(2,1)S(1)}, bf16[256,128]{1,0:T(8,128)(2,1)S(1)}, u32[]{:S(2)}, u32[]{:S(2)}) collective-permute-start(bf16[256,128]{1,0:T(8,128)(2,1)S(1)} %slice.602), channel_id=1, source_target_pairs={{0,8},{4,12},{8,0},{12,4},{1,9},{5,13},{9,1},{13,5},{2,10},{6,14},... | collective-permute-start | bytes 196616 | tf_op jit(solution)/shard_map/ppermute | solution.py:75
  76.6 17.3 %all-to-all-start = ((bf16[4,1024,128]{2,1,0:T(8,128)(2,1)}), bf16[4,1024,128]{2,1,0:T(8,128)(2,1)S(1)}, u32[]{:S(2)}, u32[]{:S(2)}) async-start(bf16[4,1024,128]{2,1,0:T(8,128)(2,1)} %broadcast_in_dim.28), calls=%async_computation | async-start | bytes 2097152 | tf_op jit(solution)/shard_map/all_to_all | solution.py:500
  97.3 167.3 %copy-start.27 = (bf16[256,256]{1,0:T(8,128)(2,1)}, bf16[256,256]{1,0:T(8,128)(2,1)S(1)}, u32[]{:S(2)}) copy-start(bf16[256,256]{1,0:T(8,128)(2,1)S(1)} %fusion.21.refs_3_) | copy-start | bytes 393220
  98.9 87.1 %copy-start.52 = (f32[1152]{0:T(1024)S(1)}, f32[1152]{0:T(1024)}, u32[]{:S(2)}) copy-start(f32[1152]{0:T(1024)} %param.32) | copy-start | bytes 13828
  98.9 87.6 %copy-start.48 = (f32[1152]{0:T(1024)S(1)}, f32[1152]{0:T(1024)}, u32[]{:S(2)}) copy-start(f32[1152]{0:T(1024)} %param.30) | copy-start | bytes 13828
  98.9 88.2 %copy-start.47 = (f32[1152]{0:T(1024)S(1)}, f32[1152]{0:T(1024)}, u32[]{:S(2)}) copy-start(f32[1152]{0:T(1024)} %param.31) | copy-start | bytes 13828
  98.9 88.9 %copy-start.2 = (bf16[1,256,1152]{2,1,0:T(8,128)(2,1)S(1)}, bf16[1,256,1152]{2,1,0:T(8,128)(2,1)}, u32[]{:S(2)}) copy-start(bf16[1,256,1152]{2,1,0:T(8,128)(2,1)} %param.18) | copy-start | bytes 1769476
  98.9 11.8 %all-to-all-start.1 = ((bf16[4,64,1152]{2,1,0:T(8,128)(2,1)}), bf16[4,64,1152]{2,1,0:T(8,128)(2,1)S(1)}, u32[]{:S(2)}, u32[]{:S(2)}) async-start(bf16[4,64,1152]{2,1,0:T(8,128)(2,1)} %bitcast.11), calls=%async_computation.1 | async-start | bytes 1179648 | tf_op jit(solution)/shard_map/all_to_all | solution.py:445
  102.5 24.7 %collective-permute-start.24 = (bf16[144,1728]{1,0:T(8,128)(2,1)S(1)}, bf16[144,1728]{1,0:T(8,128)(2,1)S(1)}, u32[]{:S(2)}, u32[]{:S(2)}) collective-permute-start(bf16[144,1728]{1,0:T(8,128)(2,1)S(1)} %copy-done.15), channel_id=1, source_target_pairs={{0,8},{4,12},{8,0},{12,4},{1,9},{5,13},{9,1},{13,5},{2,10},{6,14},... | collective-permute-start | bytes 1493000 | tf_op jit(solution)/shard_map/ppermute | solution.py:75
  102.8 26.5 %collective-permute-start.11 = (bf16[144,1728]{1,0:T(8,128)(2,1)S(1)}, bf16[144,1728]{1,0:T(8,128)(2,1)}, u32[]{:S(2)}, u32[]{:S(2)}) collective-permute-start(bf16[144,1728]{1,0:T(8,128)(2,1)S(1)} %copy-done.14), channel_id=1, source_target_pairs={{0,4},{4,0},{8,12},{12,8},{1,5},{5,1},{9,13},{13,9},{2,6},{6,2},{1... | collective-permute-start | bytes 1493000 | tf_op jit(solution)/shard_map/ppermute | solution.py:75
  105.6 34.7 %collective-permute-start.18 = (bf16[144,1728]{1,0:T(8,128)(2,1)}, bf16[144,1728]{1,0:T(8,128)(2,1)}, u32[]{:S(2)}, u32[]{:S(2)}) collective-permute-start(bf16[144,1728]{1,0:T(8,128)(2,1)} %refs_8_.1), channel_id=1, source_target_pairs={{0,4},{4,0},{8,12},{12,8},{1,5},{5,1},{9,13},{13,9},{2,6},{6,2},{1... | collective-permute-start | bytes 1493000 | tf_op jit(solution)/shard_map/ppermute | solution.py:75
  105.7 45.8 %collective-permute-start.12 = (bf16[144,1728]{1,0:T(8,128)(2,1)}, bf16[144,1728]{1,0:T(8,128)(2,1)}, u32[]{:S(2)}, u32[]{:S(2)}) collective-permute-start(bf16[144,1728]{1,0:T(8,128)(2,1)} %collective-permute-done.10.refs_1_), channel_id=1, source_target_pairs={{0,4},{4,0},{8,12},{12,8},{1,5},{5,1},{9,13},{13,9},{2,6},{6,2},{1... | collective-permute-start | bytes 1493000 | tf_op jit(solution)/shard_map/ppermute | solution.py:75
  107.7 54.8 %collective-permute-start.25 = (bf16[144,1728]{1,0:T(8,128)(2,1)S(1)}, bf16[144,1728]{1,0:T(8,128)(2,1)}, u32[]{:S(2)}, u32[]{:S(2)}) collective-permute-start(bf16[144,1728]{1,0:T(8,128)(2,1)S(1)} %copy-done.15), channel_id=1, source_target_pairs={{0,4},{4,0},{8,12},{12,8},{1,5},{5,1},{9,13},{13,9},{2,6},{6,2},{1... | collective-permute-start | bytes 1493000 | tf_op jit(solution)/shard_map/ppermute | solution.py:75
  127.2 71.6 %copy-start.16 = (bf16[144,1728]{1,0:T(8,128)(2,1)}, bf16[144,1728]{1,0:T(8,128)(2,1)S(1)}, u32[]{:S(2)}) copy-start(bf16[144,1728]{1,0:T(8,128)(2,1)S(1)} %collective-permute-done.24.refs_1_.refs_17_) | copy-start | bytes 1492996
  127.2 46.2 %collective-permute-start.19 = (bf16[144,1728]{1,0:T(8,128)(2,1)}, bf16[144,1728]{1,0:T(8,128)(2,1)S(1)}, u32[]{:S(2)}, u32[]{:S(2)}) collective-permute-start(bf16[144,1728]{1,0:T(8,128)(2,1)} %collective-permute-done.17.refs_9_), channel_id=1, source_target_pairs={{0,4},{4,0},{8,12},{12,8},{1,5},{5,1},{9,13},{13,9},{2,6},{6,2},{1... | collective-permute-start | bytes 1493000 | tf_op jit(solution)/shard_map/ppermute | solution.py:75
  129.3 44.1 %collective-permute-start.13 = (bf16[144,1728]{1,0:T(8,128)(2,1)S(1)}, bf16[144,1728]{1,0:T(8,128)(2,1)S(1)}, u32[]{:S(2)}, u32[]{:S(2)}) collective-permute-start(bf16[144,1728]{1,0:T(8,128)(2,1)S(1)} %copy-done.14), channel_id=1, source_target_pairs={{0,16},{16,0},{1,17},{17,1},{2,18},{18,2},{3,19},{19,3},{4,20},{20... | collective-permute-start | bytes 1493000 | tf_op jit(solution)/shard_map/ppermute | solution.py:75
  140.3 33.6 %collective-permute-start.14 = (bf16[144,1728]{1,0:T(8,128)(2,1)}, bf16[144,1728]{1,0:T(8,128)(2,1)S(1)}, u32[]{:S(2)}, u32[]{:S(2)}) collective-permute-start(bf16[144,1728]{1,0:T(8,128)(2,1)} %collective-permute-done.10.refs_1_), channel_id=1, source_target_pairs={{0,16},{16,0},{1,17},{17,1},{2,18},{18,2},{3,19},{19,3},{4,20},{20... | collective-permute-start | bytes 1493000 | tf_op jit(solution)/shard_map/ppermute | solution.py:75
  151.4 31.4 %collective-permute-start.26 = (bf16[144,1728]{1,0:T(8,128)(2,1)S(1)}, bf16[144,1728]{1,0:T(8,128)(2,1)}, u32[]{:S(2)}, u32[]{:S(2)}) collective-permute-start(bf16[144,1728]{1,0:T(8,128)(2,1)S(1)} %collective-permute-done.24.refs_1_.refs_17_), channel_id=1, source_target_pairs={{0,4},{4,0},{8,12},{12,8},{1,5},{5,1},{9,13},{13,9},{2,6},{6,2},{1... | collective-permute-start | bytes 1493000 | tf_op jit(solution)/shard_map/ppermute | solution.py:75
  162.5 20.3 %collective-permute-start.15 = (bf16[144,1728]{1,0:T(8,128)(2,1)}, bf16[144,1728]{1,0:T(8,128)(2,1)S(1)}, u32[]{:S(2)}, u32[]{:S(2)}) collective-permute-start(bf16[144,1728]{1,0:T(8,128)(2,1)} %collective-permute-done.11.refs_2_), channel_id=1, source_target_pairs={{0,16},{16,0},{1,17},{17,1},{2,18},{18,2},{3,19},{19,3},{4,20},{20... | collective-permute-start | bytes 1493000 | tf_op jit(solution)/shard_map/ppermute | solution.py:75
  173.4 9.9 %collective-permute-start.16 = (bf16[144,1728]{1,0:T(8,128)(2,1)}, bf16[144,1728]{1,0:T(8,128)(2,1)S(1)}, u32[]{:S(2)}, u32[]{:S(2)}) collective-permute-start(bf16[144,1728]{1,0:T(8,128)(2,1)} %collective-permute-done.12.refs_3_), channel_id=1, source_target_pairs={{0,16},{16,0},{1,17},{17,1},{2,18},{18,2},{3,19},{19,3},{4,20},{20... | collective-permute-start | bytes 1493000 | tf_op jit(solution)/shard_map/ppermute | solution.py:75
  173.4 9.9 %collective-permute-start.20 = (bf16[144,1728]{1,0:T(8,128)(2,1)}, bf16[144,1728]{1,0:T(8,128)(2,1)S(1)}, u32[]{:S(2)}, u32[]{:S(2)}) collective-permute-start(bf16[144,1728]{1,0:T(8,128)(2,1)} %refs_8_.1), channel_id=1, source_target_pairs={{0,16},{16,0},{1,17},{17,1},{2,18},{18,2},{3,19},{19,3},{4,20},{20... | collective-permute-start | bytes 1493000 | tf_op jit(solution)/shard_map/ppermute | solution.py:75
  173.9 10.0 %collective-permute-start.21 = (bf16[144,1728]{1,0:T(8,128)(2,1)}, bf16[144,1728]{1,0:T(8,128)(2,1)S(1)}, u32[]{:S(2)}, u32[]{:S(2)}) collective-permute-start(bf16[144,1728]{1,0:T(8,128)(2,1)} %collective-permute-done.17.refs_9_), channel_id=1, source_target_pairs={{0,16},{16,0},{1,17},{17,1},{2,18},{18,2},{3,19},{19,3},{4,20},{20... | collective-permute-start | bytes 1493000 | tf_op jit(solution)/shard_map/ppermute | solution.py:75
  182.8 2.1 collective-permute-start.22
  182.8 16.1 %collective-permute-start.28 = (bf16[144,1728]{1,0:T(8,128)(2,1)S(1)}, bf16[144,1728]{1,0:T(8,128)(2,1)}, u32[]{:S(2)}, u32[]{:S(2)}) collective-permute-start(bf16[144,1728]{1,0:T(8,128)(2,1)S(1)} %collective-permute-done.24.refs_1_.refs_17_), channel_id=1, source_target_pairs={{0,16},{16,0},{1,17},{17,1},{2,18},{18,2},{3,19},{19,3},{4,20},{20... | collective-permute-start | bytes 1493000 | tf_op jit(solution)/shard_map/ppermute | solution.py:75
  183.3 15.5 %collective-permute-start.27 = (bf16[144,1728]{1,0:T(8,128)(2,1)S(1)}, bf16[144,1728]{1,0:T(8,128)(2,1)}, u32[]{:S(2)}, u32[]{:S(2)}) collective-permute-start(bf16[144,1728]{1,0:T(8,128)(2,1)S(1)} %copy-done.15), channel_id=1, source_target_pairs={{0,16},{16,0},{1,17},{17,1},{2,18},{18,2},{3,19},{19,3},{4,20},{20... | collective-permute-start | bytes 1493000 | tf_op jit(solution)/shard_map/ppermute | solution.py:75
  183.4 4.6 collective-permute-start.23
  184.1 14.8 %collective-permute-start.29 = (bf16[144,1728]{1,0:T(8,128)(2,1)}, bf16[144,1728]{1,0:T(8,128)(2,1)}, u32[]{:S(2)}, u32[]{:S(2)}) collective-permute-start(bf16[144,1728]{1,0:T(8,128)(2,1)} %collective-permute-done.25.refs_2_.refs_18_), channel_id=1, source_target_pairs={{0,16},{16,0},{1,17},{17,1},{2,18},{18,2},{3,19},{19,3},{4,20},{20... | collective-permute-start | bytes 1493000 | tf_op jit(solution)/shard_map/ppermute | solution.py:75
  185.8 13.1 %collective-permute-start.30 = (bf16[144,1728]{1,0:T(8,128)(2,1)}, bf16[144,1728]{1,0:T(8,128)(2,1)}, u32[]{:S(2)}, u32[]{:S(2)}) collective-permute-start(bf16[144,1728]{1,0:T(8,128)(2,1)} %collective-permute-done.26.refs_3_.refs_19_), channel_id=1, source_target_pairs={{0,16},{16,0},{1,17},{17,1},{2,18},{18,2},{3,19},{19,3},{4,20},{20... | collective-permute-start | bytes 1493000 | tf_op jit(solution)/shard_map/ppermute | solution.py:75
  204.7 13.2 %all-to-all-start.2 = ((bf16[4,64,1152]{2,1,0:T(8,128)(2,1)}), bf16[4,64,1152]{2,1,0:T(8,128)(2,1)S(1)}, u32[]{:S(2)}, u32[]{:S(2)}) async-start(bf16[4,64,1152]{2,1,0:T(8,128)(2,1)} %bitcast.117), calls=%async_computation.2 | async-start | bytes 1179648 | tf_op jit(solution)/shard_map/all_to_all | solution.py:445
  241.8 10.6 %all-to-all-start.3 = ((bf16[4,64,1152]{2,1,0:T(8,128)(2,1)}), bf16[4,64,1152]{2,1,0:T(8,128)(2,1)S(1)}, u32[]{:S(2)}, u32[]{:S(2)}) async-start(bf16[4,64,1152]{2,1,0:T(8,128)(2,1)} %bitcast.129), calls=%async_computation.3 | async-start | bytes 1179648 | tf_op jit(solution)/shard_map/all_to_all | solution.py:445
  269.3 13.8 %all-to-all-start.4 = ((bf16[4,4,64,512]{3,2,1,0:T(8,128)(2,1)}), bf16[4,4,64,512]{3,2,1,0:T(8,128)(2,1)}, u32[]{:S(2)}, u32[]{:S(2)}) async-start(bf16[4,4,64,512]{3,2,1,0:T(8,128)(2,1)} %copy_bitcast_fusion), calls=%async_computation.4 | async-start | bytes 2097152 | tf_op jit(solution)/shard_map/all_to_all | solution.py:572
  284.5 5.0 %collective-permute-start.31 = (bf16[128,512]{1,0:T(8,128)(2,1)S(1)}, bf16[128,512]{1,0:T(8,128)(2,1)S(1)}, u32[]{:S(2)}, u32[]{:S(2)}) collective-permute-start(bf16[128,512]{1,0:T(8,128)(2,1)S(1)} %bitcast.131), channel_id=1, source_target_pairs={{0,4},{4,0},{8,12},{12,8},{1,5},{5,1},{9,13},{13,9},{2,6},{6,2},{1... | collective-permute-start | bytes 393224 | tf_op jit(solution)/shard_map/ppermute | solution.py:75
  289.6 5.4 %collective-permute-start.32 = (bf16[64,512]{1,0:T(8,128)(2,1)S(1)}, bf16[64,512]{1,0:T(8,128)(2,1)S(1)}, u32[]{:S(2)}, u32[]{:S(2)}) collective-permute-start(bf16[64,512]{1,0:T(8,128)(2,1)S(1)} %slice.414), channel_id=1, source_target_pairs={{0,8},{4,12},{8,0},{12,4},{1,9},{5,13},{9,1},{13,5},{2,10},{6,14},... | collective-permute-start | bytes 196616 | tf_op jit(solution)/shard_map/ppermute | solution.py:75
  309.2 22.7 %all-to-all-start.5 = ((bf16[4,64,1152]{2,1,0:T(8,128)(2,1)}), bf16[4,64,1152]{2,1,0:T(8,128)(2,1)S(1)}, u32[]{:S(2)}, u32[]{:S(2)}) async-start(bf16[4,64,1152]{2,1,0:T(8,128)(2,1)} %bitcast.26), calls=%async_computation.5 | async-start | bytes 1179648 | tf_op jit(solution)/shard_map/all_to_all | solution.py:445
  322.2 37.2 %collective-permute-start.42 = (bf16[4,144,1728]{2,1,0:T(8,128)(2,1)}, bf16[4,144,1728]{2,1,0:T(8,128)(2,1)}, u32[]{:S(2)}, u32[]{:S(2)}) collective-permute-start(bf16[4,144,1728]{2,1,0:T(8,128)(2,1)} %get-tuple-element.100), channel_id=1, source_target_pairs={{0,16},{16,0},{1,17},{17,1},{2,18},{18,2},{3,19},{19,3},{4,20},{20... | collective-permute-start | bytes 5971976 | tf_op jit(solution)/shard_map/ppermute | solution.py:75
  329.8 34.0 %collective-permute-start.36 = (bf16[4,144,1728]{2,1,0:T(8,128)(2,1)}, bf16[4,144,1728]{2,1,0:T(8,128)(2,1)}, u32[]{:S(2)}, u32[]{:S(2)}) collective-permute-start(bf16[4,144,1728]{2,1,0:T(8,128)(2,1)} %get-tuple-element.95), channel_id=1, source_target_pairs={{0,16},{16,0},{1,17},{17,1},{2,18},{18,2},{3,19},{19,3},{4,20},{20... | collective-permute-start | bytes 5971976 | tf_op jit(solution)/shard_map/ppermute | solution.py:75
  330.4 66.8 %collective-permute-start.39 = (bf16[4,144,1728]{2,1,0:T(8,128)(2,1)}, bf16[4,144,1728]{2,1,0:T(8,128)(2,1)}, u32[]{:S(2)}, u32[]{:S(2)}) collective-permute-start(bf16[4,144,1728]{2,1,0:T(8,128)(2,1)} %get-tuple-element.97), channel_id=1, source_target_pairs={{0,16},{16,0},{1,17},{17,1},{2,18},{18,2},{3,19},{19,3},{4,20},{20... | collective-permute-start | bytes 5971976 | tf_op jit(solution)/shard_map/ppermute | solution.py:75
  344.8 5.1 %collective-permute-start.45 = (bf16[4,1,640]{2,0,1:T(4,128)(2,1)S(1)}, bf16[4,1,640]{2,0,1:T(4,128)(2,1)S(1)}, u32[]{:S(2)}, u32[]{:S(2)}) collective-permute-start(bf16[4,1,640]{2,0,1:T(4,128)(2,1)S(1)} %fusion.60), channel_id=1, source_target_pairs={{0,16},{16,0},{1,17},{17,1},{2,18},{18,2},{3,19},{19,3},{4,20},{20... | collective-permute-start | bytes 15368 | tf_op jit(solution)/shard_map/ppermute | solution.py:75
  349.3 12.3 %collective-permute-start.33 = (bf16[4,144,640]{2,1,0:T(8,128)(2,1)}, bf16[4,144,640]{2,1,0:T(8,128)(2,1)S(1)}, u32[]{:S(2)}, u32[]{:S(2)}) collective-permute-start(bf16[4,144,640]{2,1,0:T(8,128)(2,1)} %get-tuple-element.89), channel_id=1, source_target_pairs={{0,16},{16,0},{1,17},{17,1},{2,18},{18,2},{3,19},{19,3},{4,20},{20... | collective-permute-start | bytes 2211848 | tf_op jit(solution)/shard_map/ppermute | solution.py:75
  349.9 3.7 collective-permute-start.46
  353.6 4.6 collective-permute-start.47
  361.5 58.7 %collective-permute-start.43 = (bf16[2,144,1728]{2,1,0:T(8,128)(2,1)S(1)}, bf16[2,144,1728]{2,1,0:T(8,128)(2,1)S(1)}, u32[]{:S(2)}, u32[]{:S(2)}) collective-permute-start(bf16[2,144,1728]{2,1,0:T(8,128)(2,1)S(1)} %get-tuple-element.120), channel_id=1, source_target_pairs={{0,4},{4,0},{8,12},{12,8},{1,5},{5,1},{9,13},{13,9},{2,6},{6,2},{1... | collective-permute-start | bytes 2985992 | tf_op jit(solution)/shard_map/ppermute | solution.py:75
  361.8 35.3 %collective-permute-start.34 = (bf16[2,144,640]{2,1,0:T(8,128)(2,1)S(1)}, bf16[2,144,640]{2,1,0:T(8,128)(2,1)S(1)}, u32[]{:S(2)}, u32[]{:S(2)}) collective-permute-start(bf16[2,144,640]{2,1,0:T(8,128)(2,1)S(1)} %get-tuple-element.126), channel_id=1, source_target_pairs={{0,4},{4,0},{8,12},{12,8},{1,5},{5,1},{9,13},{13,9},{2,6},{6,2},{1... | collective-permute-start | bytes 1105928 | tf_op jit(solution)/shard_map/ppermute | solution.py:75
  363.9 33.4 %copy-start.11 = (bf16[4,144,1728]{2,1,0:T(8,128)(2,1)S(1)}, bf16[4,144,1728]{2,1,0:T(8,128)(2,1)}, u32[]{:S(2)}) copy-start(bf16[4,144,1728]{2,1,0:T(8,128)(2,1)} %get-tuple-element.96) | copy-start | bytes 5971972
  366.0 71.8 %collective-permute-start.37 = (bf16[2,144,1728]{2,1,0:T(8,128)(2,1)S(1)}, bf16[2,144,1728]{2,1,0:T(8,128)(2,1)S(1)}, u32[]{:S(2)}, u32[]{:S(2)}) collective-permute-start(bf16[2,144,1728]{2,1,0:T(8,128)(2,1)S(1)} %get-tuple-element.124), channel_id=1, source_target_pairs={{0,4},{4,0},{8,12},{12,8},{1,5},{5,1},{9,13},{13,9},{2,6},{6,2},{1... | collective-permute-start | bytes 2985992 | tf_op jit(solution)/shard_map/ppermute | solution.py:75
  397.2 21.6 %collective-permute-start.35 = (bf16[1,144,640]{2,1,0:T(8,128)(2,1)S(1)}, bf16[1,144,640]{2,1,0:T(8,128)(2,1)S(1)}, u32[]{:S(2)}, u32[]{:S(2)}) collective-permute-start(bf16[1,144,640]{2,1,0:T(8,128)(2,1)S(1)} %fusion.48), channel_id=1, source_target_pairs={{0,8},{4,12},{8,0},{12,4},{1,9},{5,13},{9,1},{13,5},{2,10},{6,14},... | collective-permute-start | bytes 552968 | tf_op jit(solution)/shard_map/ppermute | solution.py:75
  399.3 57.7 %collective-permute-start.40 = (bf16[2,144,1728]{2,1,0:T(8,128)(2,1)S(1)}, bf16[2,144,1728]{2,1,0:T(8,128)(2,1)S(1)}, u32[]{:S(2)}, u32[]{:S(2)}) collective-permute-start(bf16[2,144,1728]{2,1,0:T(8,128)(2,1)S(1)} %get-tuple-element.122), channel_id=1, source_target_pairs={{0,4},{4,0},{8,12},{12,8},{1,5},{5,1},{9,13},{13,9},{2,6},{6,2},{1... | collective-permute-start | bytes 2985992 | tf_op jit(solution)/shard_map/ppermute | solution.py:75
  420.3 36.9 %collective-permute-start.44 = (bf16[1,144,1728]{2,1,0:T(8,128)(2,1)S(1)}, bf16[1,144,1728]{2,1,0:T(8,128)(2,1)S(1)}, u32[]{:S(2)}, u32[]{:S(2)}) collective-permute-start(bf16[1,144,1728]{2,1,0:T(8,128)(2,1)S(1)} %fusion.30), channel_id=1, source_target_pairs={{0,8},{4,12},{8,0},{12,4},{1,9},{5,13},{9,1},{13,5},{2,10},{6,14},... | collective-permute-start | bytes 1493000 | tf_op jit(solution)/shard_map/ppermute | solution.py:75
  437.9 46.0 %collective-permute-start.38 = (bf16[1,144,1728]{2,1,0:T(8,128)(2,1)S(1)}, bf16[1,144,1728]{2,1,0:T(8,128)(2,1)S(1)}, u32[]{:S(2)}, u32[]{:S(2)}) collective-permute-start(bf16[1,144,1728]{2,1,0:T(8,128)(2,1)S(1)} %fusion.36), channel_id=1, source_target_pairs={{0,8},{4,12},{8,0},{12,4},{1,9},{5,13},{9,1},{13,5},{2,10},{6,14},... | collective-permute-start | bytes 1493000 | tf_op jit(solution)/shard_map/ppermute | solution.py:75
  457.1 32.7 %collective-permute-start.41 = (bf16[1,144,1728]{2,1,0:T(8,128)(2,1)S(1)}, bf16[1,144,1728]{2,1,0:T(8,128)(2,1)S(1)}, u32[]{:S(2)}, u32[]{:S(2)}) collective-permute-start(bf16[1,144,1728]{2,1,0:T(8,128)(2,1)S(1)} %fusion.33), channel_id=1, source_target_pairs={{0,8},{4,12},{8,0},{12,4},{1,9},{5,13},{9,1},{13,5},{2,10},{6,14},... | collective-permute-start | bytes 1493000 | tf_op jit(solution)/shard_map/ppermute | solution.py:75
  (45 other events, 208.4 us)
where the time goes:
time: 492 us; the launch traced here: 491 us
  waiting for transfers between devices  272 us (55%)
  starting transfers between devices  54.8 us (11%)
  blocking collectives  54.5 us (11%)
  Pallas kernels  49.9 us (10%)
  other arithmetic  28.9 us (6%)
  local copies, waits for them, and re-layouts  22.5 us (5%)
  matrix products  6.25 us (1%)
    ppermute x48, waiting for transfers between devices, xor_swap(): return lax.ppermute(x, axis, [(i, i ^ bit) for i in range(size)])  235 us
    all_gather x4, blocking collectives, all_reduce_tp(): return lax.all_gather(summed, 'tp', axis=0, tiled=True)  43.8 us
    ppermute x48, starting transfers between devices, xor_swap(): return lax.ppermute(x, axis, [(i, i ^ bit) for i in range(size)])  31.8 us
    all_to_all x4, waiting for transfers between devices, all_reduce_tp(): got = lax.all_to_all(sent, 'tp', 0, 0)  16.9 us
    pallas_call x3, Pallas kernels, weight_grads(): pl.pallas_call(body, out_shape=out_shape, in_specs=[smem()] + [vmem()] *...  16.1 us
    all_to_all x4, starting transfers between devices, all_reduce_tp(): got = lax.all_to_all(sent, 'tp', 0, 0)  14.9 us
    pallas_call x1, Pallas kernels, ff_backward(): pl.pallas_call(body, out_shape=(jax.ShapeDtypeStruct((rows, width), F32),...  12.9 us
    all_to_all x1, waiting for transfers between devices, layer(): kv_stack = lax.all_to_all(spread, 'tp', 0, 0)  12.4 us
  transfers between devices with their start and end apart: 54, of which 27 were waited for; matrix products, arithmetic and copies ran while one was open for 8% of the time, Pallas kernels for 6%

commit v1 on v0

--- a/solution.py
+++ b/solution.py
@@ -107,10 +107,10 @@
     return pieces
 
 
-def gather_direct(x):
+def gather_direct(x, hold=None):
     n = lax.axis_size("ctx")
     if n > 4:
-        return gather_doubling(x)
+        return gather_doubling(x, hold)
     return [x] + [xor_swap(x, "ctx", k) for k in xor_order(n)[1:]]
 
 
@@ -367,7 +367,8 @@
             rights.append(right)
             at += right.shape[1]
         plan.append((places, at))
-    turned = [left.T.reshape(blocks, size, rows) for left in lefts]
+    tiled = size % 16 == 0
+    turned = lefts if tiled else [left.T.reshape(blocks, size, rows) for left in lefts]
     n_left, n_right, n_group = len(lefts), len(rights), len(groups)
 
     def body(index_ref, *refs):
@@ -376,25 +377,38 @@
         held = refs[n_left + n_right + 2 * n_group : -n_group]
         sems = refs[-n_group:]
 
+        def copy(g, side, j):
+            block = half * side + j
+            if tiled:
+                start = pl.multiple_of(index_ref[block] * size, 16)
+                source = held[g].at[pl.ds(start, size)]
+            else:
+                source = held[g].at[block]
+            return pltpu.make_async_copy(source, outs[2 * g + side].at[j], sems[g].at[block])
+
         for g, (places, _) in enumerate(plan):
-            for side, first in ((1, half), (0, 0)):
-
-                @pl.loop(0, half)
-                def _(j, g=g, places=places, side=side, first=first):
+            if tiled:
+                for li, ri, at, cols in places:
+                    for row, step in spans(width, 384):
+                        held[g][row : row + step, at : at + cols] = dot_tn(
+                            left_refs[li][:, row : row + step], right_refs[ri][...]
+                        ).astype(BF)
+            else:
+
+                @pl.loop(0, blocks)
+                def _(j, g=g, places=places):
                     for li, ri, at, cols in places:
-                        held[g][first + j, :, at : at + cols] = dot(
-                            left_refs[li][index_ref[first + j]], right_refs[ri][...]
+                        held[g][j, :, at : at + cols] = dot(
+                            left_refs[li][index_ref[j]], right_refs[ri][...]
                         ).astype(BF)
-                    pltpu.make_async_copy(
-                        held[g].at[first + j], outs[2 * g + side].at[j], sems[g].at[first + j]
-                    ).start()
-
+
+            for side in (1, 0):
+                for j in range(half):
+                    copy(g, side, j).start()
         for g in range(n_group):
-            for side, first in ((1, half), (0, 0)):
+            for side in (1, 0):
                 for j in range(half):
-                    pltpu.make_async_copy(
-                        held[g].at[first + j], outs[2 * g + side].at[j], sems[g].at[first + j]
-                    ).wait()
+                    copy(g, side, j).wait()
 
     out_shape = []
     for _, cols in plan:
@@ -404,11 +418,68 @@
         out_shape=out_shape,
         in_specs=[smem()] + [vmem()] * (n_left + n_right),
         out_specs=[anywhere()] * (2 * n_group),
-        scratch_shapes=[pltpu.VMEM((blocks, size, cols), BF) for _, cols in plan]
+        scratch_shapes=[
+            pltpu.VMEM((width, cols) if tiled else (blocks, size, cols), BF) for _, cols in plan
+        ]
         + [pltpu.SemaphoreType.DMA((blocks,))] * n_group,
         compiler_params=PARAMS,
     )(index, *turned, *rights)
     return [(outs[2 * g], outs[2 * g + 1]) for g in range(n_group)]
+
+
+def input_kernel(gathered, lead, quarter, wqkv, peers, peers_other, qc, d_resid, tokens, gain):
+    rows, width = tokens.shape
+    cols = wqkv.shape[1]
+    kc = cols - qc
+    n_tp = gathered.shape[0]
+    order = xor_order(n_tp)
+    count = len(peers)
+    half = width // 2
+    place = jnp.stack([lax.axis_index("shard"), lax.axis_index("tp")]).astype(jnp.int32)
+
+    def body(place_ref, got_ref, own_ref, resid_ref, x_ref, gain_ref, *refs):
+        mine, other = refs[:count], refs[count : 2 * count]
+        out_ref, sum_ref, held, sem_a, sem_b = refs[2 * count :]
+        shard, me = place_ref[0], place_ref[1]
+        copies = []
+        for refs_of, sems, side in ((mine, sem_a, shard), (other, sem_b, 1 - shard)):
+            for i, ref in enumerate(refs_of):
+                start = pl.multiple_of(side * half, 16)
+                copy = pltpu.make_async_copy(ref, held.at[i, pl.ds(start, half)], sems.at[i])
+                copy.start()
+                copies.append(copy)
+
+        def left(peer):
+            lanes = pl.ds(pl.multiple_of(peer * kc, kc), kc)
+            packed = got_ref[peer, :lead, :].reshape(rows // 2, 2 * qc)
+            queries = jnp.concatenate([packed[:, :qc], packed[:, qc:]], axis=0)
+            keys = jnp.concatenate(
+                [got_ref[q, lead : lead + quarter, lanes] for q in range(n_tp)], axis=0
+            )
+            return jnp.concatenate([queries, keys], axis=1)
+
+        total = dot_nt(left(me), own_ref[...])
+        for copy in copies:
+            copy.wait()
+        for i in range(count):
+            total = total + dot_nt(left(jnp.bitwise_xor(me, order[i + 1])), held[i])
+        hat, factor = rms_parts(x_ref[...].astype(F32))
+        sum_ref[...] = jnp.sum(total * hat, axis=0, keepdims=True)
+        out_ref[...] = resid_ref[...] + rms_back(total, hat, factor, gain_ref[...])
+
+    return pl.pallas_call(
+        body,
+        out_shape=(jax.ShapeDtypeStruct((rows, width), F32), jax.ShapeDtypeStruct((1, width), F32)),
+        in_specs=[smem()] + [vmem()] * 5 + [anywhere()] * (2 * count),
+        out_specs=(vmem(), vmem()),
+        scratch_shapes=[
+            pltpu.VMEM((count, width, cols), BF),
+            pltpu.SemaphoreType.DMA((count,)),
+            pltpu.SemaphoreType.DMA((count,)),
+        ],
+        compiler_params=PARAMS,
+        name="input_kernel",
+    )(place, gathered, wqkv, d_resid, tokens, gain[None], *peers, *peers_other)
 
 
 def scatter_ctx(x):
@@ -423,19 +494,16 @@
 
 
 def scatter_pair(keep, send):
-    got = xor_swap(send, "shard", 1)
-    bits = bits_of(lax.axis_size("ctx"))
-    half = keep.shape[0] // 2
-    low = keep[:half].astype(F32) + got[:half].astype(F32)
-    high = (keep[half:].astype(F32) + got[half:].astype(F32)).astype(BF)
-    for place, bit in enumerate(reversed(bits)):
-        got = xor_swap(high, "ctx", bit)
-        if place + 1 == len(bits):
-            return (low + got.astype(F32))[0]
-        low = low.astype(BF).astype(F32)
-        half = half // 2
-        high = (low[half:] + got[half:].astype(F32)).astype(BF)
-        low = low[:half] + got[:half].astype(F32)
+    parts = [keep, xor_swap(send, "shard", 1)]
+
+    def total(first, last):
+        return sum(part[first:last].astype(F32) for part in parts)
+
+    end = keep.shape[0]
+    for bit in reversed(bits_of(lax.axis_size("ctx"))):
+        parts.append(xor_swap(total(end // 2, end).astype(BF), "ctx", bit))
+        end = end // 2
+    return total(0, 1)[0]
 
 
 def all_reduce_tp(part):
@@ -490,6 +558,13 @@
     first_all = in_order(first_all, index)
     normed_in, qkv, wqkv, wo = qkv_kernel(tokens, gain_input, index, first_all, qc + kc)
 
+    shard_rows = lax.dynamic_slice_in_dim(
+        wqkv, lax.axis_index("shard") * (width // 2), width // 2, 0
+    )
+    tp_order = xor_order(n_tp)
+    peers = [xor_swap(shard_rows, "tp", k) for k in tp_order[1:]]
+    peers_other = [xor_swap(p, "shard", 1) for p in peers]
+
     cos_all, sin_all = rope_tables(pos_all)
     cosine, sine = cos_all[:count], sin_all[:count]
     q_raw = qkv[:, :qc].reshape(count, heads, HD)
@@ -521,9 +596,9 @@
 
     o_part = dot_nt(attn, wo).astype(BF)
     gate_mine = gather_doubling(w_gate, kv_cols)
-    up_mine = gather_doubling(w_up, kv_stack)
+    up_mine = gather_doubling(w_up, o_part)
     o_bf = all_reduce_tp(o_part)
-    down_mine = gather_doubling(w_down, o_bf)
+    down_mine = gather_direct(w_down, o_bf)
     gate_all = in_order(with_other_core([after(p, o_bf) for p in gate_mine]), index)
     up_all = in_order(with_other_core([after(p, o_bf) for p in up_mine]), index)
     resid, normed_ff, mixed, p1, p2 = ff_forward(
@@ -537,10 +612,10 @@
     d_ff = all_reduce_tp(d_ff_part).astype(F32)
     (pair,) = weight_grads(index, [[(d_f, mixed)]])
     grad_down = scatter_pair(*pair)
-    left = after(normed_ff, d_ff)
-    pairs = weight_grads(index, [[(left, d_gate)], [(left, d_up)]])
-    grad_gate = scatter_pair(*pairs[0])
-    grad_up = scatter_pair(*pairs[1])
+    (pair,) = weight_grads(index, [[(normed_ff, d_gate)]])
+    grad_gate = scatter_pair(*pair)
+    (pair,) = weight_grads(index, [[(after(normed_ff, d_ff), d_up)]])
+    grad_up = scatter_pair(*pair)
 
     o_hat, o_factor = rms_parts(o_bf.astype(F32))
     h_hat, h_factor = rms_parts(resid)
@@ -590,17 +665,20 @@
 
     tail = jnp.concatenate([grad_query_part, grad_key_part])[None].astype(BF)
     tail = jnp.concatenate([tail, jnp.zeros((15, 2 * HD), BF)], axis=0)
-    dkv_all = lax.all_gather(jnp.concatenate([dkv_raw, tail], axis=0), "tp", axis=0)
-    dkv_full = dkv_all[:, :quarter].reshape(count, 2 * HD)
-    gain_sums = jnp.sum(dkv_all[:, quarter].astype(F32), axis=0)
-    dkv_cols = lax.dynamic_slice_in_dim(dkv_full, lax.axis_index("tp") * kc, kc, 1)
+    packed = jnp.concatenate([d_qraw[: count // 2], d_qraw[count // 2 :]], axis=1)
+    packed = packed.reshape(-1, 2 * HD)
+    lead = packed.shape[0]
+    gathered = lax.all_gather(jnp.concatenate([packed, dkv_raw, tail], axis=0), "tp", axis=0)
+    gain_sums = jnp.sum(gathered[:, lead + quarter].astype(F32), axis=0)
+    at = lax.axis_index("tp") * kc
+    dkv_cols = lax.dynamic_slice_in_dim(gathered[:, lead : lead + quarter], at, kc, 2).reshape(count, kc)
     d_qkv = jnp.concatenate([d_qraw, dkv_cols], axis=1)
     (pair,) = weight_grads(index, [[(normed_in, d_qkv), (d_o, attn)]])
     grad_heads = scatter_pair(*pair)
-    d_in = all_reduce_tp(dot_nt(d_qkv, wqkv)).astype(F32)
-    x_hat, x_factor = rms_parts(tokens.astype(F32))
-    grad_input = jnp.sum(d_in * x_hat, axis=0)
-    input_grad = d_resid + rms_back(d_in, x_hat, x_factor, gain_input)
+    input_grad, grad_input = input_kernel(
+        gathered, lead, quarter, wqkv, peers, peers_other, qc, d_resid, tokens, gain_input
+    )
+    grad_input = grad_input[0]
 
     blocks = 2 * n_ctx
     wide = jnp.stack([grad_input, grad_attn, grad_prefn, grad_postfn[0]])

time: 492 us -> 450 us (0.915)
  waiting for transfers between devices: 272 us -> 217 us
  starting transfers between devices: 54.8 us -> 76 us
  blocking collectives: 54.5 us -> 45.9 us
  Pallas kernels: 49.9 us -> 57.7 us
    ppermute x48 -> x54, waiting for transfers between devices: 235 us -> 183 us  [xor_swap(): return lax.ppermute(x, axis, [(i, i ^ bit) for i in range(size)])]
    ppermute x48 -> x54, starting transfers between devices: 31.8 us -> 57.6 us  [xor_swap(): return lax.ppermute(x, axis, [(i, i ^ bit) for i in range(size)])]
    all_gather x4 -> x3, blocking collectives: 43.8 us -> 32.8 us  [all_reduce_tp(): return lax.all_gather(summed, 'tp', axis=0, tiled=True)]
    all_to_all x4 -> x3, waiting for transfers between devices: 16.9 us -> 9.88 us  [all_reduce_tp(): got = lax.all_to_all(sent, 'tp', 0, 0)]
    pallas_call x0 -> x1, Pallas kernels: none -> 6.58 us  [input_kernel(): pl.pallas_call(body, out_shape=(jax.ShapeDtypeStruct((rows, width), F32),...]
    transpose x4 -> x0, local copies, waits for them, and re-layouts: 5.4 us -> none  [weight_grads(): turned = [left.T.reshape(blocks, size, rows) for left in lefts]]
    all_to_all x4 -> x3, starting transfers between devices: 14.9 us -> 11 us  [all_reduce_tp(): got = lax.all_to_all(sent, 'tp', 0, 0)]
    pallas_call x3 -> x4, Pallas kernels: 16.1 us -> 17.3 us  [weight_grads(): pl.pallas_call(body, out_shape=out_shape, in_specs=[smem()] + [vmem()] *...]
  transfers between devices with their start and end apart: 54 -> 59, of which waited for: 27 -> 25; matrix products, arithmetic and copies ran while one was open for 8% -> 9% of each run, Pallas kernels for 6% -> 13%
where the time goes in v1:
time: 450 us; the launch traced here: 449 us
  waiting for transfers between devices  217 us (48%)
  starting transfers between devices  76 us (17%)
  Pallas kernels  57.7 us (13%)
  blocking collectives  45.9 us (10%)
  other arithmetic  25.8 us (6%)
  local copies, waits for them, and re-layouts  21.2 us (5%)
    ppermute x54, waiting for transfers between devices, xor_swap(): return lax.ppermute(x, axis, [(i, i ^ bit) for i in range(size)])  183 us
    ppermute x54, starting transfers between devices, xor_swap(): return lax.ppermute(x, axis, [(i, i ^ bit) for i in range(size)])  57.6 us
    all_gather x3, blocking collectives, all_reduce_tp(): return lax.all_gather(summed, 'tp', axis=0, tiled=True)  32.8 us
    pallas_call x4, Pallas kernels, weight_grads(): pl.pallas_call(body, out_shape=out_shape, in_specs=[smem()] + [vmem()] *...  17.3 us
    all_to_all x1, waiting for transfers between devices, layer(): kv_stack = lax.all_to_all(spread, 'tp', 0, 0)  13.1 us
    all_gather x1, blocking collectives, layer(): lax.all_gather(jnp.concatenate([packed, dkv_raw, tail], axis=0), 'tp', ax...  13 us
    pallas_call x1, Pallas kernels, ff_backward(): pl.pallas_call(body, out_shape=(jax.ShapeDtypeStruct((rows, width), F32),...  13 us
    all_to_all x3, starting transfers between devices, all_reduce_tp(): got = lax.all_to_all(sent, 'tp', 0, 0)  11 us
  transfers between devices with their start and end apart: 59, of which 25 were waited for; matrix products, arithmetic and copies ran while one was open for 9% of the time, Pallas kernels for 13%

profile of v1, /device:TPU:0, one launch (start us, length us, event | category | flops | bytes accessed | tf_op | source)
XLA Modules:
  0.0 448.6 jit_solution(8663127272491085433)
XLA Ops:
  2.5 4.1 collective-permute-start
  6.6 1.6 collective-permute-start.1
  8.2 1.9 collective-permute-start.10
  10.1 1.3 broadcast_in_dim.27.g_ref.gain_ref
  12.6 5.2 %collective-permute-done.refs_1_ = bf16[160,640]{1,0:T(8,128)(2,1)S(1)} collective-permute-done((bf16[160,640]{1,0:T(8,128)(2,1)S(1)}, bf16[160,640]{1,0:T(8,128)(2,1)S(1)}, u32[]{:S(2)}, u32[]{:S(2)}) %collective-permute-start) | collective-permute-done | bytes 204832 | tf_op jit(solution)/shard_map/ppermute | solution.py:75
  17.9 4.9 %collective-permute-done.2.refs_3_ = bf16[160,640]{1,0:T(8,128)(2,1)S(1)} collective-permute-done((bf16[160,640]{1,0:T(8,128)(2,1)S(1)}, bf16[160,640]{1,0:T(8,128)(2,1)S(1)}, u32[]{:S(2)}, u32[]{:S(2)}) %collective-permute-start.2) | collective-permute-done | bytes 204832 | tf_op jit(solution)/shard_map/ppermute | solution.py:75
  23.5 1.9 multiply_sine_fusion
  25.4 14.7 %collective-permute-start.11 = (bf16[144,1728]{1,0:T(8,128)(2,1)S(1)}, bf16[144,1728]{1,0:T(8,128)(2,1)}, u32[]{:S(2)}, u32[]{:S(2)}) collective-permute-start(bf16[144,1728]{1,0:T(8,128)(2,1)S(1)} %copy-done.11), channel_id=1, source_target_pairs={{0,4},{4,0},{8,12},{12,8},{1,5},{5,1},{9,13},{13,9},{2,6},{6,2},{1... | collective-permute-start | bytes 1493000 | tf_op jit(solution)/shard_map/ppermute | solution.py:75
  40.9 4.2 qkv_kernel.1
  46.0 1.3 collective-permute-start.7
  47.3 2.0 collective-permute-start.8
  51.5 2.1 collective-permute-done.7
  53.6 3.4 collective-permute-start.17
  57.0 6.3 %collective-permute-done.8 = bf16[256,128]{1,0:T(8,128)(2,1)S(1)} collective-permute-done((bf16[256,128]{1,0:T(8,128)(2,1)S(1)}, bf16[256,128]{1,0:T(8,128)(2,1)S(1)}, u32[]{:S(2)}, u32[]{:S(2)}) %collective-permute-start.8) | collective-permute-done | bytes 65568 | tf_op jit(solution)/shard_map/ppermute | solution.py:75
  64.4 3.7 all-to-all-start
  69.2 13.1 %all-to-all-done = bf16[4,1024,128]{2,1,0:T(8,128)(2,1)S(1)} async-done(((bf16[4,1024,128]{2,1,0:T(8,128)(2,1)}), bf16[4,1024,128]{2,1,0:T(8,128)(2,1)S(1)}, u32[]{:S(2)}, u32[]{:S(2)}) %all-to-all-start) | async-done | bytes 1048608 | tf_op jit(solution)/shard_map/all_to_all | solution.py:575
  83.0 1.3 convert_multiply_fusion.2
  87.3 3.5 all-to-all-start.1
  90.9 3.5 collective-permute-start.24
  94.5 1.4 collective-permute-start.26
  96.5 2.8 all-to-all-done.1
  100.0 11.0 %all_gather.15.o_ref = bf16[256,1152]{1,0:T(8,128)(2,1)} all-gather(bf16[64,1152]{1,0:T(8,128)(2,1)} %reduce_sum.183), channel_id=1, replica_groups=mesh['shard'=2,'ctx'=4,'tp'=4] {'tp'}, dimensions={0}, use_global_device_ids=true | all-gather | bytes 737280 | tf_op jit(solution)/shard_map/all_gather | solution.py:515
  111.0 4.8 %collective-permute-done.18.refs_10_ = bf16[144,1728]{1,0:T(8,128)(2,1)S(1)} collective-permute-done((bf16[144,1728]{1,0:T(8,128)(2,1)}, bf16[144,1728]{1,0:T(8,128)(2,1)S(1)}, u32[]{:S(2)}, u32[]{:S(2)}) %collective-permute-start.18) | collective-permute-done | bytes 497696 | tf_op jit(solution)/shard_map/ppermute | solution.py:75
  115.8 2.4 collective-permute-done.24.refs_1_.refs_17_
  118.2 19.2 %collective-permute-done.25.refs_2_.refs_18_ = bf16[144,1728]{1,0:T(8,128)(2,1)} collective-permute-done((bf16[144,1728]{1,0:T(8,128)(2,1)S(1)}, bf16[144,1728]{1,0:T(8,128)(2,1)}, u32[]{:S(2)}, u32[]{:S(2)}) %collective-permute-start.25) | collective-permute-done | bytes 497696 | tf_op jit(solution)/shard_map/ppermute | solution.py:75
  137.3 2.7 collective-permute-done.26.refs_3_.refs_19_
  140.0 8.5 %collective-permute-done.19.refs_11_ = bf16[144,1728]{1,0:T(8,128)(2,1)} collective-permute-done((bf16[144,1728]{1,0:T(8,128)(2,1)}, bf16[144,1728]{1,0:T(8,128)(2,1)}, u32[]{:S(2)}, u32[]{:S(2)}) %collective-permute-start.19) | collective-permute-done | bytes 497696 | tf_op jit(solution)/shard_map/ppermute | solution.py:75
  152.8 1.8 constant_dynamic-slice_fusion.1
  154.6 1.6 collective-permute-start.33
  156.3 1.5 collective-permute-start.34
  160.1 10.8 %ff_forward.1 = (f32[256,1152]{1,0:T(8,128)}, bf16[256,1152]{1,0:T(8,128)(2,1)}, bf16[256,1728]{1,0:T(8,128)(2,1)}, bf16[256,1728]{1,0:T(8,128)(2,1)}, bf16[256,1728]{1,0:T(8,128)(2,1)}) custom-call(s32[8]{0:T(128)} %get-tuple-element.115.index_ref, bf16[256,1152]{1,0:T(8,128)(2,1)} %all_gather.15.o_ref, bf16[256,1152]{1,0:T(8,128)(2,1)} %bitcast.101, ...), custom_call_target="tpu_custom_call" | custom-call | tf_op jit(solution)/shard_map/ff_forward/pallas_call | solution.py:248
  171.7 5.8 %ff_down.1 = bf16[256,1152]{1,0:T(8,128)(2,1)} custom-call(s32[8]{0:T(128)} %get-tuple-element.115.index_ref, bf16[256,1728]{1,0:T(8,128)(2,1)} %get-tuple-element.78.mix_ref.refs_1_, bf16[144,1728]{1,0:T(8,128)(2,1)} %refs_16_, bf16[144,1728]{1,0:T(8,128)(2,1)} %collective-permute-done.24.refs_1_.refs_17_, ...), custom_call_target="tpu_custom_call" | custom-call | tf_op jit(solution)/shard_map/ff_down/pallas_call | solution.py:282
  177.6 3.9 all-to-all-start.2
  182.7 1.7 slice.437
  184.6 5.3 %all-to-all-done.2 = bf16[4,64,1152]{2,1,0:T(8,128)(2,1)S(1)} async-done(((bf16[4,64,1152]{2,1,0:T(8,128)(2,1)}), bf16[4,64,1152]{2,1,0:T(8,128)(2,1)S(1)}, u32[]{:S(2)}, u32[]{:S(2)}) %all-to-all-start.2) | async-done | bytes 589856 | tf_op jit(solution)/shard_map/all_to_all | solution.py:513
  190.0 11.5 %all_gather.16.f_ref = bf16[256,1152]{1,0:T(8,128)(2,1)} all-gather(bf16[64,1152]{1,0:T(8,128)(2,1)S(1)} %reduce_sum.184), channel_id=1, replica_groups=mesh['shard'=2,'ctx'=4,'tp'=4] {'tp'}, dimensions={0}, use_global_device_ids=true | all-gather | bytes 737280 | tf_op jit(solution)/shard_map/all_gather | solution.py:515
  201.5 13.0 %ff_backward.1 = (f32[256,1152]{1,0:T(8,128)}, bf16[256,1152]{1,0:T(8,128)(2,1)}, f32[1,1152]{1,0:T(1,128)}, bf16[256,1728]{1,0:T(8,128)(2,1)}, bf16[256,1728]{1,0:T(8,128)(2,1)}, /*index=5*/bf16[256,1152]{1,0:T(8,128)(2,1)}) custom-call(s32[8]{0:T(128)} %get-tuple-element.115.index_ref, bf16[256,1152]{1,0:T(8,128)(2,1)} %all_gather.16.f_ref, ...), custom_call_target="tpu_custom_call" | custom-call | tf_op jit(solution)/shard_map/ff_backward/pallas_call | solution.py:335
  214.5 3.6 all-to-all-start.3
  218.4 4.7 %shard_map.266 = (bf16[4,144,1728]{2,1,0:T(8,128)(2,1)}, bf16[4,144,1728]{2,1,0:T(8,128)(2,1)}) custom-call(s32[8]{0:T(128)} %get-tuple-element.115.index_ref, bf16[256,1152]{1,0:T(8,128)(2,1)} %get-tuple-element.101.refs_0_, bf16[256,1728]{1,0:T(8,128)(2,1)} %get-tuple-element.78.mix_ref.refs_1_), custom_call_target="tpu_custom_call" | custom-call | tf_op jit(solution)/shard_map/pallas_call | solution.py:416
  223.2 1.9 all-to-all-done.3
  225.8 10.4 %all_gather.17 = bf16[256,1152]{1,0:T(8,128)(2,1)S(1)} all-gather(bf16[64,1152]{1,0:T(8,128)(2,1)} %reduce_sum.187), channel_id=1, replica_groups=mesh['shard'=2,'ctx'=4,'tp'=4] {'tp'}, dimensions={0}, use_global_device_ids=true | all-gather | bytes 737280 | tf_op jit(solution)/shard_map/all_gather | solution.py:515
  243.2 3.6 all-to-all-start.4
  248.0 10.6 %all-to-all-done.4 = bf16[4,4,64,512]{3,2,1,0:T(8,128)(2,1)S(1)} async-done(((bf16[4,4,64,512]{3,2,1,0:T(8,128)(2,1)}), bf16[4,4,64,512]{3,2,1,0:T(8,128)(2,1)S(1)}, u32[]{:S(2)}, u32[]{:S(2)}) %all-to-all-start.4) | async-done | bytes 1048608 | tf_op jit(solution)/shard_map/all_to_all | solution.py:647
  259.4 4.4 collective-permute-done.31
  263.9 1.8 collective-permute-start.32
  265.9 3.9 collective-permute-done.32
  270.2 13.0 %all-gather = bf16[832,512]{1,0:T(8,128)(2,1)} all-gather(bf16[208,512]{1,0:T(8,128)(2,1)S(1)} %maximum_maximum_fusion), channel_id=2, replica_groups=mesh['shard'=2,'ctx'=4,'tp'=4] {'tp'}, dimensions={0}, use_global_device_ids=true | all-gather | bytes 1064960 | tf_op jit(solution)/shard_map/all_gather | solution.py:671
  283.2 6.6 %input_kernel.1 = (f32[256,1152]{1,0:T(8,128)}, f32[1,1152]{1,0:T(1,128)}) custom-call(s32[2]{0:T(128)} %pad_add_fusion.1.place_ref, bf16[4,208,512]{2,1,0:T(8,128)(2,1)} %bitcast.103, bf16[1152,384]{1,0:T(8,128)(2,1)} %get-tuple-element.88.own_ref, f32[256,1152]{1,0:T(8,128)} %copy-done.2, bf16[256,1152]{1,0:T(8,128)(2,1)} %bitcast.102, ...), custom_call_target="tpu_custom_call" | custom-call | tf_op jit(solution)/shard_map/input_kernel/pallas_call | solution.py:470
  292.5 4.7 %shard_map.265 = (bf16[4,144,1728]{2,1,0:T(8,128)(2,1)}, bf16[4,144,1728]{2,1,0:T(8,128)(2,1)}) custom-call(s32[8]{0:T(128)} %get-tuple-element.115.index_ref, bf16[256,1152]{1,0:T(8,128)(2,1)} %get-tuple-element.97.refs_0_, bf16[256,1728]{1,0:T(8,128)(2,1)} %get-tuple-element.98.refs_1_), custom_call_target="tpu_custom_call" | custom-call | tf_op jit(solution)/shard_map/pallas_call | solution.py:416
  297.8 4.7 %shard_map.264 = (bf16[4,144,1728]{2,1,0:T(8,128)(2,1)}, bf16[4,144,1728]{2,1,0:T(8,128)(2,1)}) custom-call(s32[8]{0:T(128)} %get-tuple-element.115.index_ref, bf16[256,1152]{1,0:T(8,128)(2,1)} %get-tuple-element.97.refs_0_, bf16[256,1728]{1,0:T(8,128)(2,1)} %get-tuple-element.94.refs_1_), custom_call_target="tpu_custom_call" | custom-call | tf_op jit(solution)/shard_map/pallas_call | solution.py:416
  304.0 3.4 collective-permute-done.52
  309.4 3.2 shard_map.263
  313.9 1.6 add_convert_fusion
  315.5 2.1 collective-permute-start.49
  318.1 2.1 collective-permute-start.46
  320.1 29.0 %collective-permute-done.40 = bf16[2,144,640]{2,1,0:T(8,128)(2,1)S(1)} collective-permute-done((bf16[2,144,640]{2,1,0:T(8,128)(2,1)S(1)}, bf16[2,144,640]{2,1,0:T(8,128)(2,1)S(1)}, u32[]{:S(2)}, u32[]{:S(2)}) %collective-permute-start.40) | collective-permute-done | bytes 368672 | tf_op jit(solution)/shard_map/ppermute | solution.py:75
  349.2 1.8 collective-permute-start.41
  352.2 22.6 %collective-permute-done.41 = bf16[1,144,640]{2,1,0:T(8,128)(2,1)S(1)} collective-permute-done((bf16[1,144,640]{2,1,0:T(8,128)(2,1)S(1)}, bf16[1,144,640]{2,1,0:T(8,128)(2,1)S(1)}, u32[]{:S(2)}, u32[]{:S(2)}) %collective-permute-start.41) | collective-permute-done | bytes 184352 | tf_op jit(solution)/shard_map/ppermute | solution.py:75
  376.2 1.2 add_convert_fusion.3
  377.5 3.4 collective-permute-start.50
  381.2 33.1 %collective-permute-done.43 = bf16[2,144,1728]{2,1,0:T(8,128)(2,1)S(1)} collective-permute-done((bf16[2,144,1728]{2,1,0:T(8,128)(2,1)S(1)}, bf16[2,144,1728]{2,1,0:T(8,128)(2,1)S(1)}, u32[]{:S(2)}, u32[]{:S(2)}) %collective-permute-start.43) | collective-permute-done | bytes 995360 | tf_op jit(solution)/shard_map/ppermute | solution.py:75
  415.3 2.3 add_bitcast_fusion
  417.6 20.2 %collective-permute-done.47 = bf16[1,144,1728]{2,1,0:T(8,128)(2,1)S(1)} collective-permute-done((bf16[1,144,1728]{2,1,0:T(8,128)(2,1)S(1)}, bf16[1,144,1728]{2,1,0:T(8,128)(2,1)S(1)}, u32[]{:S(2)}, u32[]{:S(2)}) %collective-permute-start.47) | collective-permute-done | bytes 497696 | tf_op jit(solution)/shard_map/ppermute | solution.py:75
  439.0 8.3 %collective-permute-done.44 = bf16[1,144,1728]{2,1,0:T(8,128)(2,1)S(1)} collective-permute-done((bf16[1,144,1728]{2,1,0:T(8,128)(2,1)S(1)}, bf16[1,144,1728]{2,1,0:T(8,128)(2,1)S(1)}, u32[]{:S(2)}, u32[]{:S(2)}) %collective-permute-start.44) | collective-permute-done | bytes 497696 | tf_op jit(solution)/shard_map/ppermute | solution.py:75
  (292 shorter events, 49.1 us)
Async XLA Ops:
  2.5 15.4 %collective-permute-start = (bf16[160,640]{1,0:T(8,128)(2,1)S(1)}, bf16[160,640]{1,0:T(8,128)(2,1)S(1)}, u32[]{:S(2)}, u32[]{:S(2)}) collective-permute-start(bf16[160,640]{1,0:T(8,128)(2,1)S(1)} %fusion.31.refs_0_), channel_id=1, source_target_pairs={{0,8},{4,12},{8,0},{12,4},{1,9},{5,13},{9,1},{13,5},{2,10},{6,14},... | collective-permute-start | bytes 614408 | tf_op jit(solution)/shard_map/ppermute | solution.py:75
  6.6 11.2 %collective-permute-start.1 = (bf16[160,640]{1,0:T(8,128)(2,1)S(1)}, bf16[160,640]{1,0:T(8,128)(2,1)S(1)}, u32[]{:S(2)}, u32[]{:S(2)}) collective-permute-start(bf16[160,640]{1,0:T(8,128)(2,1)S(1)} %fusion.31.refs_0_), channel_id=1, source_target_pairs={{0,4},{4,0},{8,12},{12,8},{1,5},{5,1},{9,13},{13,9},{2,6},{6,2},{1... | collective-permute-start | bytes 614408 | tf_op jit(solution)/shard_map/ppermute | solution.py:75
  8.2 14.6 %collective-permute-start.2 = (bf16[160,640]{1,0:T(8,128)(2,1)S(1)}, bf16[160,640]{1,0:T(8,128)(2,1)S(1)}, u32[]{:S(2)}, u32[]{:S(2)}) collective-permute-start(bf16[160,640]{1,0:T(8,128)(2,1)S(1)} %fusion.31.refs_0_), channel_id=1, source_target_pairs={{0,12},{4,8},{8,4},{12,0},{1,13},{5,9},{9,5},{13,1},{2,14},{6,10},... | collective-permute-start | bytes 614408 | tf_op jit(solution)/shard_map/ppermute | solution.py:75
  8.2 17.2 %collective-permute-start.3 = (bf16[160,640]{1,0:T(8,128)(2,1)S(1)}, bf16[160,640]{1,0:T(8,128)(2,1)S(1)}, u32[]{:S(2)}, u32[]{:S(2)}) collective-permute-start(bf16[160,640]{1,0:T(8,128)(2,1)S(1)} %fusion.31.refs_0_), channel_id=1, source_target_pairs={{0,16},{16,0},{1,17},{17,1},{2,18},{18,2},{3,19},{19,3},{4,20},{20... | collective-permute-start | bytes 614408 | tf_op jit(solution)/shard_map/ppermute | solution.py:75
  8.2 61.0 %collective-permute-start.10 = (bf16[144,1728]{1,0:T(8,128)(2,1)}, bf16[144,1728]{1,0:T(8,128)(2,1)}, u32[]{:S(2)}, u32[]{:S(2)}) collective-permute-start(bf16[144,1728]{1,0:T(8,128)(2,1)} %refs_0_.2), channel_id=1, source_target_pairs={{0,8},{4,12},{8,0},{12,4},{1,9},{5,13},{9,1},{13,5},{2,10},{6,14},... | collective-permute-start | bytes 1493000 | tf_op jit(solution)/shard_map/ppermute | solution.py:75
  22.9 17.1 %collective-permute-start.4 = (bf16[160,640]{1,0:T(8,128)(2,1)S(1)}, bf16[160,640]{1,0:T(8,128)(2,1)S(1)}, u32[]{:S(2)}, u32[]{:S(2)}) collective-permute-start(bf16[160,640]{1,0:T(8,128)(2,1)S(1)} %collective-permute-done.refs_1_), channel_id=1, source_target_pairs={{0,16},{16,0},{1,17},{17,1},{2,18},{18,2},{3,19},{19,3},{4,20},{20... | collective-permute-start | bytes 614408 | tf_op jit(solution)/shard_map/ppermute | solution.py:75
  22.9 17.1 %collective-permute-start.5 = (bf16[160,640]{1,0:T(8,128)(2,1)S(1)}, bf16[160,640]{1,0:T(8,128)(2,1)S(1)}, u32[]{:S(2)}, u32[]{:S(2)}) collective-permute-start(bf16[160,640]{1,0:T(8,128)(2,1)S(1)} %collective-permute-done.1.refs_2_), channel_id=1, source_target_pairs={{0,16},{16,0},{1,17},{17,1},{2,18},{18,2},{3,19},{19,3},{4,20},{20... | collective-permute-start | bytes 614408 | tf_op jit(solution)/shard_map/ppermute | solution.py:75
  23.4 16.7 %collective-permute-start.6 = (bf16[160,640]{1,0:T(8,128)(2,1)S(1)}, bf16[160,640]{1,0:T(8,128)(2,1)S(1)}, u32[]{:S(2)}, u32[]{:S(2)}) collective-permute-start(bf16[160,640]{1,0:T(8,128)(2,1)S(1)} %collective-permute-done.2.refs_3_), channel_id=1, source_target_pairs={{0,16},{16,0},{1,17},{17,1},{2,18},{18,2},{3,19},{19,3},{4,20},{20... | collective-permute-start | bytes 614408 | tf_op jit(solution)/shard_map/ppermute | solution.py:75
  25.4 69.1 %collective-permute-start.11 = (bf16[144,1728]{1,0:T(8,128)(2,1)S(1)}, bf16[144,1728]{1,0:T(8,128)(2,1)}, u32[]{:S(2)}, u32[]{:S(2)}) collective-permute-start(bf16[144,1728]{1,0:T(8,128)(2,1)S(1)} %copy-done.11), channel_id=1, source_target_pairs={{0,4},{4,0},{8,12},{12,8},{1,5},{5,1},{9,13},{13,9},{2,6},{6,2},{1... | collective-permute-start | bytes 1493000 | tf_op jit(solution)/shard_map/ppermute | solution.py:75
  46.0 7.6 %collective-permute-start.7 = (bf16[256,128]{1,0:T(8,128)(2,1)S(1)}, bf16[256,128]{1,0:T(8,128)(2,1)S(1)}, u32[]{:S(2)}, u32[]{:S(2)}) collective-permute-start(bf16[256,128]{1,0:T(8,128)(2,1)S(1)} %slice.599), channel_id=1, source_target_pairs={{0,8},{4,12},{8,0},{12,4},{1,9},{5,13},{9,1},{13,5},{2,10},{6,14},... | collective-permute-start | bytes 196616 | tf_op jit(solution)/shard_map/ppermute | solution.py:75
  47.3 16.0 %collective-permute-start.8 = (bf16[256,128]{1,0:T(8,128)(2,1)S(1)}, bf16[256,128]{1,0:T(8,128)(2,1)S(1)}, u32[]{:S(2)}, u32[]{:S(2)}) collective-permute-start(bf16[256,128]{1,0:T(8,128)(2,1)S(1)} %slice.599), channel_id=1, source_target_pairs={{0,4},{4,0},{8,12},{12,8},{1,5},{5,1},{9,13},{13,9},{2,6},{6,2},{1... | collective-permute-start | bytes 196616 | tf_op jit(solution)/shard_map/ppermute | solution.py:75
  49.3 14.0 %collective-permute-start.9 = (bf16[256,128]{1,0:T(8,128)(2,1)S(1)}, bf16[256,128]{1,0:T(8,128)(2,1)S(1)}, u32[]{:S(2)}, u32[]{:S(2)}) collective-permute-start(bf16[256,128]{1,0:T(8,128)(2,1)S(1)} %slice.599), channel_id=1, source_target_pairs={{0,12},{4,8},{8,4},{12,0},{1,13},{5,9},{9,5},{13,1},{2,14},{6,10},... | collective-permute-start | bytes 196616 | tf_op jit(solution)/shard_map/ppermute | solution.py:75
  53.6 40.8 %collective-permute-start.17 = (bf16[144,1728]{1,0:T(8,128)(2,1)}, bf16[144,1728]{1,0:T(8,128)(2,1)}, u32[]{:S(2)}, u32[]{:S(2)}) collective-permute-start(bf16[144,1728]{1,0:T(8,128)(2,1)} %refs_8_.1), channel_id=1, source_target_pairs={{0,8},{4,12},{8,0},{12,4},{1,9},{5,13},{9,1},{13,5},{2,10},{6,14},... | collective-permute-start | bytes 1493000 | tf_op jit(solution)/shard_map/ppermute | solution.py:75
  64.4 17.9 %all-to-all-start = ((bf16[4,1024,128]{2,1,0:T(8,128)(2,1)}), bf16[4,1024,128]{2,1,0:T(8,128)(2,1)S(1)}, u32[]{:S(2)}, u32[]{:S(2)}) async-start(bf16[4,1024,128]{2,1,0:T(8,128)(2,1)} %broadcast_in_dim.28), calls=%async_computation | async-start | bytes 2097152 | tf_op jit(solution)/shard_map/all_to_all | solution.py:575
  69.2 26.8 %collective-permute-start.12 = (bf16[144,1728]{1,0:T(8,128)(2,1)}, bf16[144,1728]{1,0:T(8,128)(2,1)}, u32[]{:S(2)}, u32[]{:S(2)}) collective-permute-start(bf16[144,1728]{1,0:T(8,128)(2,1)} %collective-permute-done.10.refs_1_), channel_id=1, source_target_pairs={{0,4},{4,0},{8,12},{12,8},{1,5},{5,1},{9,13},{13,9},{2,6},{6,2},{1... | collective-permute-start | bytes 1493000 | tf_op jit(solution)/shard_map/ppermute | solution.py:75
  85.7 152.2 %copy-start.27 = (bf16[256,256]{1,0:T(8,128)(2,1)}, bf16[256,256]{1,0:T(8,128)(2,1)S(1)}, u32[]{:S(2)}) copy-start(bf16[256,256]{1,0:T(8,128)(2,1)S(1)} %fusion.12.refs_3_) | copy-start | bytes 393220
  87.3 12.0 %all-to-all-start.1 = ((bf16[4,64,1152]{2,1,0:T(8,128)(2,1)}), bf16[4,64,1152]{2,1,0:T(8,128)(2,1)S(1)}, u32[]{:S(2)}, u32[]{:S(2)}) async-start(bf16[4,64,1152]{2,1,0:T(8,128)(2,1)} %bitcast.11), calls=%async_computation.1 | async-start | bytes 1179648 | tf_op jit(solution)/shard_map/all_to_all | solution.py:513
  90.8 67.3 %copy-start.45 = (f32[1152]{0:T(1024)S(1)}, f32[1152]{0:T(1024)}, u32[]{:S(2)}) copy-start(f32[1152]{0:T(1024)} %param.30) | copy-start | bytes 13828
  90.8 67.9 %copy-start.44 = (f32[1152]{0:T(1024)S(1)}, f32[1152]{0:T(1024)}, u32[]{:S(2)}) copy-start(f32[1152]{0:T(1024)} %param.31) | copy-start | bytes 13828
  90.8 68.5 %copy-start.48 = (f32[1152]{0:T(1024)S(1)}, f32[1152]{0:T(1024)}, u32[]{:S(2)}) copy-start(f32[1152]{0:T(1024)} %param.32) | copy-start | bytes 13828
  90.8 25.0 %collective-permute-start.18 = (bf16[144,1728]{1,0:T(8,128)(2,1)}, bf16[144,1728]{1,0:T(8,128)(2,1)S(1)}, u32[]{:S(2)}, u32[]{:S(2)}) collective-permute-start(bf16[144,1728]{1,0:T(8,128)(2,1)} %refs_8_.1), channel_id=1, source_target_pairs={{0,4},{4,0},{8,12},{12,8},{1,5},{5,1},{9,13},{13,9},{2,6},{6,2},{1... | collective-permute-start | bytes 1493000 | tf_op jit(solution)/shard_map/ppermute | solution.py:75
  90.9 27.2 %collective-permute-start.24 = (bf16[144,1728]{1,0:T(8,128)(2,1)S(1)}, bf16[144,1728]{1,0:T(8,128)(2,1)}, u32[]{:S(2)}, u32[]{:S(2)}) collective-permute-start(bf16[144,1728]{1,0:T(8,128)(2,1)S(1)} %copy-done.12), channel_id=1, source_target_pairs={{0,8},{4,12},{8,0},{12,4},{1,9},{5,13},{9,1},{13,5},{2,10},{6,14},... | collective-permute-start | bytes 1493000 | tf_op jit(solution)/shard_map/ppermute | solution.py:75
  94.4 42.9 %collective-permute-start.25 = (bf16[144,1728]{1,0:T(8,128)(2,1)S(1)}, bf16[144,1728]{1,0:T(8,128)(2,1)}, u32[]{:S(2)}, u32[]{:S(2)}) collective-permute-start(bf16[144,1728]{1,0:T(8,128)(2,1)S(1)} %copy-done.12), channel_id=1, source_target_pairs={{0,4},{4,0},{8,12},{12,8},{1,5},{5,1},{9,13},{13,9},{2,6},{6,2},{1... | collective-permute-start | bytes 1493000 | tf_op jit(solution)/shard_map/ppermute | solution.py:75
  94.5 45.5 %collective-permute-start.26 = (bf16[144,1728]{1,0:T(8,128)(2,1)S(1)}, bf16[144,1728]{1,0:T(8,128)(2,1)}, u32[]{:S(2)}, u32[]{:S(2)}) collective-permute-start(bf16[144,1728]{1,0:T(8,128)(2,1)S(1)} %copy-done.12), channel_id=1, source_target_pairs={{0,12},{4,8},{8,4},{12,0},{1,13},{5,9},{9,5},{13,1},{2,14},{6,10},... | collective-permute-start | bytes 1493000 | tf_op jit(solution)/shard_map/ppermute | solution.py:75
  96.0 52.5 %collective-permute-start.19 = (bf16[144,1728]{1,0:T(8,128)(2,1)}, bf16[144,1728]{1,0:T(8,128)(2,1)}, u32[]{:S(2)}, u32[]{:S(2)}) collective-permute-start(bf16[144,1728]{1,0:T(8,128)(2,1)} %collective-permute-done.17.refs_9_), channel_id=1, source_target_pairs={{0,4},{4,0},{8,12},{12,8},{1,5},{5,1},{9,13},{13,9},{2,6},{6,2},{1... | collective-permute-start | bytes 1493000 | tf_op jit(solution)/shard_map/ppermute | solution.py:75
  115.8 44.3 %copy-start.13 = (bf16[144,1728]{1,0:T(8,128)(2,1)}, bf16[144,1728]{1,0:T(8,128)(2,1)S(1)}, u32[]{:S(2)}) copy-start(bf16[144,1728]{1,0:T(8,128)(2,1)S(1)} %collective-permute-done.18.refs_10_) | copy-start | bytes 1492996
  115.8 32.7 %collective-permute-start.16 = (bf16[144,1728]{1,0:T(8,128)(2,1)}, bf16[144,1728]{1,0:T(8,128)(2,1)S(1)}, u32[]{:S(2)}, u32[]{:S(2)}) collective-permute-start(bf16[144,1728]{1,0:T(8,128)(2,1)} %collective-permute-done.12.refs_3_), channel_id=1, source_target_pairs={{0,16},{16,0},{1,17},{17,1},{2,18},{18,2},{3,19},{19,3},{4,20},{20... | collective-permute-start | bytes 1493000 | tf_op jit(solution)/shard_map/ppermute | solution.py:75
  118.2 30.8 %collective-permute-start.14 = (bf16[144,1728]{1,0:T(8,128)(2,1)}, bf16[144,1728]{1,0:T(8,128)(2,1)S(1)}, u32[]{:S(2)}, u32[]{:S(2)}) collective-permute-start(bf16[144,1728]{1,0:T(8,128)(2,1)} %collective-permute-done.10.refs_1_), channel_id=1, source_target_pairs={{0,16},{16,0},{1,17},{17,1},{2,18},{18,2},{3,19},{19,3},{4,20},{20... | collective-permute-start | bytes 1493000 | tf_op jit(solution)/shard_map/ppermute | solution.py:75
  137.3 11.7 %collective-permute-start.15 = (bf16[144,1728]{1,0:T(8,128)(2,1)}, bf16[144,1728]{1,0:T(8,128)(2,1)S(1)}, u32[]{:S(2)}, u32[]{:S(2)}) collective-permute-start(bf16[144,1728]{1,0:T(8,128)(2,1)} %collective-permute-done.11.refs_2_), channel_id=1, source_target_pairs={{0,16},{16,0},{1,17},{17,1},{2,18},{18,2},{3,19},{19,3},{4,20},{20... | collective-permute-start | bytes 1493000 | tf_op jit(solution)/shard_map/ppermute | solution.py:75
  140.0 9.5 %collective-permute-start.21 = (bf16[144,1728]{1,0:T(8,128)(2,1)}, bf16[144,1728]{1,0:T(8,128)(2,1)S(1)}, u32[]{:S(2)}, u32[]{:S(2)}) collective-permute-start(bf16[144,1728]{1,0:T(8,128)(2,1)} %collective-permute-done.17.refs_9_), channel_id=1, source_target_pairs={{0,16},{16,0},{1,17},{17,1},{2,18},{18,2},{3,19},{19,3},{4,20},{20... | collective-permute-start | bytes 1493000 | tf_op jit(solution)/shard_map/ppermute | solution.py:75
  148.5 1.9 collective-permute-start.22
  148.5 2.6 collective-permute-start.13
  149.0 2.9 collective-permute-start.20
  149.1 5.6 %collective-permute-start.28 = (bf16[144,1728]{1,0:T(8,128)(2,1)}, bf16[144,1728]{1,0:T(8,128)(2,1)}, u32[]{:S(2)}, u32[]{:S(2)}) collective-permute-start(bf16[144,1728]{1,0:T(8,128)(2,1)} %collective-permute-done.24.refs_1_.refs_17_), channel_id=1, source_target_pairs={{0,16},{16,0},{1,17},{17,1},{2,18},{18,2},{3,19},{19,3},{4,20},{20... | collective-permute-start | bytes 1493000 | tf_op jit(solution)/shard_map/ppermute | solution.py:75
  149.5 6.8 %collective-permute-start.29 = (bf16[144,1728]{1,0:T(8,128)(2,1)}, bf16[144,1728]{1,0:T(8,128)(2,1)}, u32[]{:S(2)}, u32[]{:S(2)}) collective-permute-start(bf16[144,1728]{1,0:T(8,128)(2,1)} %collective-permute-done.25.refs_2_.refs_18_), channel_id=1, source_target_pairs={{0,16},{16,0},{1,17},{17,1},{2,18},{18,2},{3,19},{19,3},{4,20},{20... | collective-permute-start | bytes 1493000 | tf_op jit(solution)/shard_map/ppermute | solution.py:75
  150.4 7.4 %collective-permute-start.23 = (bf16[144,1728]{1,0:T(8,128)(2,1)}, bf16[144,1728]{1,0:T(8,128)(2,1)}, u32[]{:S(2)}, u32[]{:S(2)}) collective-permute-start(bf16[144,1728]{1,0:T(8,128)(2,1)} %collective-permute-done.19.refs_11_), channel_id=1, source_target_pairs={{0,16},{16,0},{1,17},{17,1},{2,18},{18,2},{3,19},{19,3},{4,20},{20... | collective-permute-start | bytes 1493000 | tf_op jit(solution)/shard_map/ppermute | solution.py:75
  151.1 19.8 %collective-permute-start.30 = (bf16[144,1728]{1,0:T(8,128)(2,1)}, bf16[144,1728]{1,0:T(8,128)(2,1)S(1)}, u32[]{:S(2)}, u32[]{:S(2)}) collective-permute-start(bf16[144,1728]{1,0:T(8,128)(2,1)} %collective-permute-done.26.refs_3_.refs_19_), channel_id=1, source_target_pairs={{0,16},{16,0},{1,17},{17,1},{2,18},{18,2},{3,19},{19,3},{4,20},{20... | collective-permute-start | bytes 1493000 | tf_op jit(solution)/shard_map/ppermute | solution.py:75
  152.7 18.3 %collective-permute-start.27 = (bf16[144,1728]{1,0:T(8,128)(2,1)S(1)}, bf16[144,1728]{1,0:T(8,128)(2,1)}, u32[]{:S(2)}, u32[]{:S(2)}) collective-permute-start(bf16[144,1728]{1,0:T(8,128)(2,1)S(1)} %copy-done.12), channel_id=1, source_target_pairs={{0,16},{16,0},{1,17},{17,1},{2,18},{18,2},{3,19},{19,3},{4,20},{20... | collective-permute-start | bytes 1493000 | tf_op jit(solution)/shard_map/ppermute | solution.py:75
  154.6 27.4 %collective-permute-start.33 = (bf16[576,384]{1,0:T(8,128)(2,1)}, bf16[576,384]{1,0:T(8,128)(2,1)}, u32[]{:S(2)}, u32[]{:S(2)}) collective-permute-start(bf16[576,384]{1,0:T(8,128)(2,1)} %constant_dynamic-slice_fusion.1), channel_id=1, source_target_pairs={{0,2},{1,3},{2,0},{3,1},{4,6},{5,7},{6,4},{7,5},{8,10},{9,11},{10,... | collective-permute-start | bytes 1327112 | tf_op jit(solution)/shard_map/ppermute | solution.py:75
  156.3 25.8 %collective-permute-start.34 = (bf16[576,384]{1,0:T(8,128)(2,1)}, bf16[576,384]{1,0:T(8,128)(2,1)}, u32[]{:S(2)}, u32[]{:S(2)}) collective-permute-start(bf16[576,384]{1,0:T(8,128)(2,1)} %constant_dynamic-slice_fusion.1), channel_id=1, source_target_pairs={{0,1},{1,0},{2,3},{3,2},{4,5},{5,4},{6,7},{7,6},{8,9},{9,8},{10,11... | collective-permute-start | bytes 1327112 | tf_op jit(solution)/shard_map/ppermute | solution.py:75
  157.7 24.9 %collective-permute-start.35 = (bf16[576,384]{1,0:T(8,128)(2,1)}, bf16[576,384]{1,0:T(8,128)(2,1)}, u32[]{:S(2)}, u32[]{:S(2)}) collective-permute-start(bf16[576,384]{1,0:T(8,128)(2,1)} %constant_dynamic-slice_fusion.1), channel_id=1, source_target_pairs={{0,3},{1,2},{2,1},{3,0},{4,7},{5,6},{6,5},{7,4},{8,11},{9,10},{10,... | collective-permute-start | bytes 1327112 | tf_op jit(solution)/shard_map/ppermute | solution.py:75
  177.6 12.3 %all-to-all-start.2 = ((bf16[4,64,1152]{2,1,0:T(8,128)(2,1)}), bf16[4,64,1152]{2,1,0:T(8,128)(2,1)S(1)}, u32[]{:S(2)}, u32[]{:S(2)}) async-start(bf16[4,64,1152]{2,1,0:T(8,128)(2,1)} %bitcast.107), calls=%async_computation.2 | async-start | bytes 1179648 | tf_op jit(solution)/shard_map/all_to_all | solution.py:513
  182.1 101.1 %collective-permute-start.36 = (bf16[576,384]{1,0:T(8,128)(2,1)}, bf16[576,384]{1,0:T(8,128)(2,1)}, u32[]{:S(2)}, u32[]{:S(2)}) collective-permute-start(bf16[576,384]{1,0:T(8,128)(2,1)} %collective-permute-done.33.refs_0_), channel_id=1, source_target_pairs={{0,16},{16,0},{1,17},{17,1},{2,18},{18,2},{3,19},{19,3},{4,20},{20... | collective-permute-start | bytes 1327112 | tf_op jit(solution)/shard_map/ppermute | solution.py:75
  182.1 101.1 %collective-permute-start.37 = (bf16[576,384]{1,0:T(8,128)(2,1)}, bf16[576,384]{1,0:T(8,128)(2,1)}, u32[]{:S(2)}, u32[]{:S(2)}) collective-permute-start(bf16[576,384]{1,0:T(8,128)(2,1)} %collective-permute-done.34.refs_1_), channel_id=1, source_target_pairs={{0,16},{16,0},{1,17},{17,1},{2,18},{18,2},{3,19},{19,3},{4,20},{20... | collective-permute-start | bytes 1327112 | tf_op jit(solution)/shard_map/ppermute | solution.py:75
  182.6 100.6 %collective-permute-start.38 = (bf16[576,384]{1,0:T(8,128)(2,1)}, bf16[576,384]{1,0:T(8,128)(2,1)}, u32[]{:S(2)}, u32[]{:S(2)}) collective-permute-start(bf16[576,384]{1,0:T(8,128)(2,1)} %collective-permute-done.35.refs_2_), channel_id=1, source_target_pairs={{0,16},{16,0},{1,17},{17,1},{2,18},{18,2},{3,19},{19,3},{4,20},{20... | collective-permute-start | bytes 1327112 | tf_op jit(solution)/shard_map/ppermute | solution.py:75
  214.5 10.6 %all-to-all-start.3 = ((bf16[4,64,1152]{2,1,0:T(8,128)(2,1)}), bf16[4,64,1152]{2,1,0:T(8,128)(2,1)S(1)}, u32[]{:S(2)}, u32[]{:S(2)}) async-start(bf16[4,64,1152]{2,1,0:T(8,128)(2,1)} %bitcast.110), calls=%async_computation.3 | async-start | bytes 1179648 | tf_op jit(solution)/shard_map/all_to_all | solution.py:513
  223.1 90.8 %collective-permute-start.48 = (bf16[4,144,1728]{2,1,0:T(8,128)(2,1)}, bf16[4,144,1728]{2,1,0:T(8,128)(2,1)}, u32[]{:S(2)}, u32[]{:S(2)}) collective-permute-start(bf16[4,144,1728]{2,1,0:T(8,128)(2,1)} %get-tuple-element.103), channel_id=1, source_target_pairs={{0,16},{16,0},{1,17},{17,1},{2,18},{18,2},{3,19},{19,3},{4,20},{20... | collective-permute-start | bytes 5971976 | tf_op jit(solution)/shard_map/ppermute | solution.py:75
  243.2 15.5 %all-to-all-start.4 = ((bf16[4,4,64,512]{3,2,1,0:T(8,128)(2,1)}), bf16[4,4,64,512]{3,2,1,0:T(8,128)(2,1)S(1)}, u32[]{:S(2)}, u32[]{:S(2)}) async-start(bf16[4,4,64,512]{3,2,1,0:T(8,128)(2,1)} %copy_bitcast_fusion), calls=%async_computation.4 | async-start | bytes 2097152 | tf_op jit(solution)/shard_map/all_to_all | solution.py:647
  258.8 5.0 %collective-permute-start.31 = (bf16[128,512]{1,0:T(8,128)(2,1)S(1)}, bf16[128,512]{1,0:T(8,128)(2,1)S(1)}, u32[]{:S(2)}, u32[]{:S(2)}) collective-permute-start(bf16[128,512]{1,0:T(8,128)(2,1)S(1)} %bitcast.112), channel_id=1, source_target_pairs={{0,4},{4,0},{8,12},{12,8},{1,5},{5,1},{9,13},{13,9},{2,6},{6,2},{1... | collective-permute-start | bytes 393224 | tf_op jit(solution)/shard_map/ppermute | solution.py:75
  263.9 5.8 %collective-permute-start.32 = (bf16[64,512]{1,0:T(8,128)(2,1)S(1)}, bf16[64,512]{1,0:T(8,128)(2,1)S(1)}, u32[]{:S(2)}, u32[]{:S(2)}) collective-permute-start(bf16[64,512]{1,0:T(8,128)(2,1)S(1)} %slice.433), channel_id=1, source_target_pairs={{0,8},{4,12},{8,0},{12,4},{1,9},{5,13},{9,1},{13,5},{2,10},{6,14},... | collective-permute-start | bytes 196616 | tf_op jit(solution)/shard_map/ppermute | solution.py:75
  292.4 11.3 %collective-permute-start.51 = (bf16[4,1,640]{2,0,1:T(4,128)(2,1)S(1)}, bf16[4,1,640]{2,0,1:T(4,128)(2,1)S(1)}, u32[]{:S(2)}, u32[]{:S(2)}) collective-permute-start(bf16[4,1,640]{2,0,1:T(4,128)(2,1)S(1)} %fusion.35), channel_id=1, source_target_pairs={{0,16},{16,0},{1,17},{17,1},{2,18},{18,2},{3,19},{19,3},{4,20},{20... | collective-permute-start | bytes 15368 | tf_op jit(solution)/shard_map/ppermute | solution.py:75
  297.2 20.6 %collective-permute-start.45 = (bf16[4,144,1728]{2,1,0:T(8,128)(2,1)}, bf16[4,144,1728]{2,1,0:T(8,128)(2,1)S(1)}, u32[]{:S(2)}, u32[]{:S(2)}) collective-permute-start(bf16[4,144,1728]{2,1,0:T(8,128)(2,1)} %get-tuple-element.100), channel_id=1, source_target_pairs={{0,16},{16,0},{1,17},{17,1},{2,18},{18,2},{3,19},{19,3},{4,20},{20... | collective-permute-start | bytes 5971976 | tf_op jit(solution)/shard_map/ppermute | solution.py:75
  302.6 48.5 %collective-permute-start.42 = (bf16[4,144,1728]{2,1,0:T(8,128)(2,1)}, bf16[4,144,1728]{2,1,0:T(8,128)(2,1)S(1)}, u32[]{:S(2)}, u32[]{:S(2)}) collective-permute-start(bf16[4,144,1728]{2,1,0:T(8,128)(2,1)} %get-tuple-element.96), channel_id=1, source_target_pairs={{0,16},{16,0},{1,17},{17,1},{2,18},{18,2},{3,19},{19,3},{4,20},{20... | collective-permute-start | bytes 5971976 | tf_op jit(solution)/shard_map/ppermute | solution.py:75
  303.8 3.7 collective-permute-start.52
  307.4 5.2 %collective-permute-start.53 = (bf16[1,1,640]{2,0,1:T(2,128)(2,1)S(1)}, bf16[1,1,640]{2,0,1:T(2,128)(2,1)S(1)}, u32[]{:S(2)}, u32[]{:S(2)}) collective-permute-start(bf16[1,1,640]{2,0,1:T(2,128)(2,1)S(1)} %fusion.39), channel_id=1, source_target_pairs={{0,8},{4,12},{8,0},{12,4},{1,9},{5,13},{9,1},{13,5},{2,10},{6,14},... | collective-permute-start | bytes 3848 | tf_op jit(solution)/shard_map/ppermute | solution.py:75
  312.5 5.1 %collective-permute-start.39 = (bf16[4,144,640]{2,1,0:T(8,128)(2,1)}, bf16[4,144,640]{2,1,0:T(8,128)(2,1)S(1)}, u32[]{:S(2)}, u32[]{:S(2)}) collective-permute-start(bf16[4,144,640]{2,1,0:T(8,128)(2,1)} %get-tuple-element.92), channel_id=1, source_target_pairs={{0,16},{16,0},{1,17},{17,1},{2,18},{18,2},{3,19},{19,3},{4,20},{20... | collective-permute-start | bytes 2211848 | tf_op jit(solution)/shard_map/ppermute | solution.py:75
  315.5 60.7 %collective-permute-start.49 = (bf16[2,144,1728]{2,1,0:T(8,128)(2,1)S(1)}, bf16[2,144,1728]{2,1,0:T(8,128)(2,1)S(1)}, u32[]{:S(2)}, u32[]{:S(2)}) collective-permute-start(bf16[2,144,1728]{2,1,0:T(8,128)(2,1)S(1)} %add_convert_fusion), channel_id=1, source_target_pairs={{0,4},{4,0},{8,12},{12,8},{1,5},{5,1},{9,13},{13,9},{2,6},{6,2},{1... | collective-permute-start | bytes 2985992 | tf_op jit(solution)/shard_map/ppermute | solution.py:75
  317.7 31.5 %collective-permute-start.40 = (bf16[2,144,640]{2,1,0:T(8,128)(2,1)S(1)}, bf16[2,144,640]{2,1,0:T(8,128)(2,1)S(1)}, u32[]{:S(2)}, u32[]{:S(2)}) collective-permute-start(bf16[2,144,640]{2,1,0:T(8,128)(2,1)S(1)} %add_convert_fusion.6), channel_id=1, source_target_pairs={{0,4},{4,0},{8,12},{12,8},{1,5},{5,1},{9,13},{13,9},{2,6},{6,2},{1... | collective-permute-start | bytes 1105928 | tf_op jit(solution)/shard_map/ppermute | solution.py:75
  318.1 62.9 %collective-permute-start.46 = (bf16[2,144,1728]{2,1,0:T(8,128)(2,1)S(1)}, bf16[2,144,1728]{2,1,0:T(8,128)(2,1)S(1)}, u32[]{:S(2)}, u32[]{:S(2)}) collective-permute-start(bf16[2,144,1728]{2,1,0:T(8,128)(2,1)S(1)} %add_convert_fusion.1), channel_id=1, source_target_pairs={{0,4},{4,0},{8,12},{12,8},{1,5},{5,1},{9,13},{13,9},{2,6},{6,2},{1... | collective-permute-start | bytes 2985992 | tf_op jit(solution)/shard_map/ppermute | solution.py:75
  349.2 25.5 %collective-permute-start.41 = (bf16[1,144,640]{2,1,0:T(8,128)(2,1)S(1)}, bf16[1,144,640]{2,1,0:T(8,128)(2,1)S(1)}, u32[]{:S(2)}, u32[]{:S(2)}) collective-permute-start(bf16[1,144,640]{2,1,0:T(8,128)(2,1)S(1)} %add_convert_fusion.7), channel_id=1, source_target_pairs={{0,8},{4,12},{8,0},{12,4},{1,9},{5,13},{9,1},{13,5},{2,10},{6,14},... | collective-permute-start | bytes 552968 | tf_op jit(solution)/shard_map/ppermute | solution.py:75
  351.4 63.0 %collective-permute-start.43 = (bf16[2,144,1728]{2,1,0:T(8,128)(2,1)S(1)}, bf16[2,144,1728]{2,1,0:T(8,128)(2,1)S(1)}, u32[]{:S(2)}, u32[]{:S(2)}) collective-permute-start(bf16[2,144,1728]{2,1,0:T(8,128)(2,1)S(1)} %add_convert_fusion.2), channel_id=1, source_target_pairs={{0,4},{4,0},{8,12},{12,8},{1,5},{5,1},{9,13},{13,9},{2,6},{6,2},{1... | collective-permute-start | bytes 2985992 | tf_op jit(solution)/shard_map/ppermute | solution.py:75
  377.5 37.8 %collective-permute-start.50 = (bf16[1,144,1728]{2,1,0:T(8,128)(2,1)S(1)}, bf16[1,144,1728]{2,1,0:T(8,128)(2,1)S(1)}, u32[]{:S(2)}, u32[]{:S(2)}) collective-permute-start(bf16[1,144,1728]{2,1,0:T(8,128)(2,1)S(1)} %add_convert_fusion.3), channel_id=1, source_target_pairs={{0,8},{4,12},{8,0},{12,4},{1,9},{5,13},{9,1},{13,5},{2,10},{6,14},... | collective-permute-start | bytes 1493000 | tf_op jit(solution)/shard_map/ppermute | solution.py:75
  381.2 56.6 %collective-permute-start.47 = (bf16[1,144,1728]{2,1,0:T(8,128)(2,1)S(1)}, bf16[1,144,1728]{2,1,0:T(8,128)(2,1)S(1)}, u32[]{:S(2)}, u32[]{:S(2)}) collective-permute-start(bf16[1,144,1728]{2,1,0:T(8,128)(2,1)S(1)} %add_convert_fusion.4), channel_id=1, source_target_pairs={{0,8},{4,12},{8,0},{12,4},{1,9},{5,13},{9,1},{13,5},{2,10},{6,14},... | collective-permute-start | bytes 1493000 | tf_op jit(solution)/shard_map/ppermute | solution.py:75
  414.5 32.8 %collective-permute-start.44 = (bf16[1,144,1728]{2,1,0:T(8,128)(2,1)S(1)}, bf16[1,144,1728]{2,1,0:T(8,128)(2,1)S(1)}, u32[]{:S(2)}, u32[]{:S(2)}) collective-permute-start(bf16[1,144,1728]{2,1,0:T(8,128)(2,1)S(1)} %add_convert_fusion.5), channel_id=1, source_target_pairs={{0,8},{4,12},{8,0},{12,4},{1,9},{5,13},{9,1},{13,5},{2,10},{6,14},... | collective-permute-start | bytes 1493000 | tf_op jit(solution)/shard_map/ppermute | solution.py:75
  (46 other events, 316.7 us)

commit v2 on v1

--- a/solution.py
+++ b/solution.py
@@ -501,9 +501,26 @@
 
     end = keep.shape[0]
     for bit in reversed(bits_of(lax.axis_size("ctx"))):
-        parts.append(xor_swap(total(end // 2, end).astype(BF), "ctx", bit))
+        high = total(end // 2, end).astype(BF)
+        parts.append(xor_swap(high, "ctx", bit))
         end = end // 2
     return total(0, 1)[0]
+
+
+def scatter_split(keep, send):
+    got = xor_swap(send, "shard", 1)
+    sums = [[keep[i], got[i]] for i in range(keep.shape[0])]
+
+    def total(parts):
+        return sum(part.astype(F32) for part in parts)
+
+    for bit in reversed(bits_of(lax.axis_size("ctx"))):
+        half = len(sums) // 2
+        for place in reversed(range(half, 2 * half)):
+            block = total(sums[place]).astype(BF)
+            sums[place - half].append(xor_swap(block, "ctx", bit))
+        sums = sums[:half]
+    return total(sums[0])
 
 
 def all_reduce_tp(part):
@@ -599,8 +616,8 @@
     up_mine = gather_doubling(w_up, o_part)
     o_bf = all_reduce_tp(o_part)
     down_mine = gather_direct(w_down, o_bf)
-    gate_all = in_order(with_other_core([after(p, o_bf) for p in gate_mine]), index)
-    up_all = in_order(with_other_core([after(p, o_bf) for p in up_mine]), index)
+    gate_all = in_order(with_other_core([after(p, o_part) for p in gate_mine]), index)
+    up_all = in_order(with_other_core([after(p, o_part) for p in up_mine[:-1]] + [after(up_mine[-1], o_bf)]), index)
     resid, normed_ff, mixed, p1, p2 = ff_forward(
         o_bf, tokens, gain_attn, gain_prefn, index, gate_all, up_all
     )
@@ -611,11 +628,11 @@
     )
     d_ff = all_reduce_tp(d_ff_part).astype(F32)
     (pair,) = weight_grads(index, [[(d_f, mixed)]])
-    grad_down = scatter_pair(*pair)
+    grad_down = scatter_split(*pair)
     (pair,) = weight_grads(index, [[(normed_ff, d_gate)]])
-    grad_gate = scatter_pair(*pair)
+    grad_gate = scatter_split(*pair)
     (pair,) = weight_grads(index, [[(after(normed_ff, d_ff), d_up)]])
-    grad_up = scatter_pair(*pair)
+    grad_up = scatter_split(*pair)
 
     o_hat, o_factor = rms_parts(o_bf.astype(F32))
     h_hat, h_factor = rms_parts(resid)

time: 450 us -> 485 us (1.078)
  waiting for transfers between devices: 217 us -> 237 us
  starting transfers between devices: 76 us -> 82.3 us
  blocking collectives: 45.9 us -> 51.1 us
    ppermute x54 -> x57, waiting for transfers between devices: 183 us -> 207 us  [xor_swap(): return lax.ppermute(x, axis, [(i, i ^ bit) for i in range(size)])]
    ppermute x54 -> x57, starting transfers between devices: 57.6 us -> 63.8 us  [xor_swap(): return lax.ppermute(x, axis, [(i, i ^ bit) for i in range(size)])]
    add x0 -> x3, other arithmetic: none -> 5.77 us  [total(): return sum((part.astype(F32) for part in parts))]
  transfers between devices with their start and end apart: 59 -> 62, of which waited for: 25 -> 19; matrix products, arithmetic and copies ran while one was open for 9% -> 9% of each run, Pallas kernels for 13% -> 12%
where the time goes in v2:
time: 485 us; the launch traced here: 483 us
  waiting for transfers between devices  237 us (49%)
  starting transfers between devices  82.3 us (17%)
  Pallas kernels  57.6 us (12%)
  blocking collectives  51.1 us (11%)
  other arithmetic  29.1 us (6%)
  local copies, waits for them, and re-layouts  20.2 us (4%)
    ppermute x57, waiting for transfers between devices, xor_swap(): return lax.ppermute(x, axis, [(i, i ^ bit) for i in range(size)])  207 us
    ppermute x57, starting transfers between devices, xor_swap(): return lax.ppermute(x, axis, [(i, i ^ bit) for i in range(size)])  63.8 us
    all_gather x3, blocking collectives, all_reduce_tp(): return lax.all_gather(summed, 'tp', axis=0, tiled=True)  37.1 us
    pallas_call x4, Pallas kernels, weight_grads(): pl.pallas_call(body, out_shape=out_shape, in_specs=[smem()] + [vmem()] *...  17.3 us
    all_gather x1, blocking collectives, layer(): lax.all_gather(jnp.concatenate([packed, dkv_raw, tail], axis=0), 'tp', ax...  14.1 us
    pallas_call x1, Pallas kernels, ff_backward(): pl.pallas_call(body, out_shape=(jax.ShapeDtypeStruct((rows, width), F32),...  13 us
    all_to_all x1, waiting for transfers between devices, layer(): kv_stack = lax.all_to_all(spread, 'tp', 0, 0)  12.4 us
    all_to_all x1, waiting for transfers between devices, layer(): dkv = lax.all_to_all(dkv, 'tp', 0, 0)  12.2 us
  transfers between devices with their start and end apart: 62, of which 19 were waited for; matrix products, arithmetic and copies ran while one was open for 9% of the time, Pallas kernels for 12%

profile of v2, /device:TPU:0, one launch (start us, length us, event | category | flops | bytes accessed | tf_op | source)
XLA Modules:
  0.0 483.0 jit_solution(17082108447882027112)
XLA Ops:
  2.5 4.1 collective-permute-start
  6.6 1.6 collective-permute-start.1
  8.2 1.9 collective-permute-start.10
  12.6 5.2 %collective-permute-done.refs_1_ = bf16[160,640]{1,0:T(8,128)(2,1)S(1)} collective-permute-done((bf16[160,640]{1,0:T(8,128)(2,1)S(1)}, bf16[160,640]{1,0:T(8,128)(2,1)S(1)}, u32[]{:S(2)}, u32[]{:S(2)}) %collective-permute-start) | collective-permute-done | bytes 204832 | tf_op jit(solution)/shard_map/ppermute | solution.py:75
  17.9 4.9 %collective-permute-done.2.refs_3_ = bf16[160,640]{1,0:T(8,128)(2,1)S(1)} collective-permute-done((bf16[160,640]{1,0:T(8,128)(2,1)S(1)}, bf16[160,640]{1,0:T(8,128)(2,1)S(1)}, u32[]{:S(2)}, u32[]{:S(2)}) %collective-permute-start.2) | collective-permute-done | bytes 204832 | tf_op jit(solution)/shard_map/ppermute | solution.py:75
  23.5 1.9 multiply_sine_fusion
  25.4 14.7 %collective-permute-start.11 = (bf16[144,1728]{1,0:T(8,128)(2,1)S(1)}, bf16[144,1728]{1,0:T(8,128)(2,1)}, u32[]{:S(2)}, u32[]{:S(2)}) collective-permute-start(bf16[144,1728]{1,0:T(8,128)(2,1)S(1)} %copy-done.11), channel_id=1, source_target_pairs={{0,4},{4,0},{8,12},{12,8},{1,5},{5,1},{9,13},{13,9},{2,6},{6,2},{1... | collective-permute-start | bytes 1493000 | tf_op jit(solution)/shard_map/ppermute | solution.py:75
  40.9 4.2 qkv_kernel.1
  47.3 2.0 collective-permute-start.8
  51.5 2.2 collective-permute-done.7
  53.6 3.4 collective-permute-start.17
  57.0 6.3 %collective-permute-done.8 = bf16[256,128]{1,0:T(8,128)(2,1)S(1)} collective-permute-done((bf16[256,128]{1,0:T(8,128)(2,1)S(1)}, bf16[256,128]{1,0:T(8,128)(2,1)S(1)}, u32[]{:S(2)}, u32[]{:S(2)}) %collective-permute-start.8) | collective-permute-done | bytes 65568 | tf_op jit(solution)/shard_map/ppermute | solution.py:75
  63.3 3.6 collective-permute-start.24
  68.0 3.7 all-to-all-start
  72.9 12.4 %all-to-all-done = bf16[4,1024,128]{2,1,0:T(8,128)(2,1)S(1)} async-done(((bf16[4,1024,128]{2,1,0:T(8,128)(2,1)}), bf16[4,1024,128]{2,1,0:T(8,128)(2,1)S(1)}, u32[]{:S(2)}, u32[]{:S(2)}) %all-to-all-start) | async-done | bytes 1048608 | tf_op jit(solution)/shard_map/all_to_all | solution.py:592
  90.5 1.5 collective-permute-start.26
  92.0 18.4 %collective-permute-done.12.refs_3_ = bf16[144,1728]{1,0:T(8,128)(2,1)} collective-permute-done((bf16[144,1728]{1,0:T(8,128)(2,1)}, bf16[144,1728]{1,0:T(8,128)(2,1)}, u32[]{:S(2)}, u32[]{:S(2)}) %collective-permute-start.12) | collective-permute-done | bytes 497696 | tf_op jit(solution)/shard_map/ppermute | solution.py:75
  110.9 3.8 all-to-all-start.1
  114.7 17.7 %collective-permute-done.25.refs_2_.refs_18_ = bf16[144,1728]{1,0:T(8,128)(2,1)S(1)} collective-permute-done((bf16[144,1728]{1,0:T(8,128)(2,1)}, bf16[144,1728]{1,0:T(8,128)(2,1)S(1)}, u32[]{:S(2)}, u32[]{:S(2)}) %collective-permute-start.25) | collective-permute-done | bytes 497696 | tf_op jit(solution)/shard_map/ppermute | solution.py:75
  132.9 9.9 %collective-permute-done.19.refs_11_ = bf16[144,1728]{1,0:T(8,128)(2,1)} collective-permute-done((bf16[144,1728]{1,0:T(8,128)(2,1)}, bf16[144,1728]{1,0:T(8,128)(2,1)}, u32[]{:S(2)}, u32[]{:S(2)}) %collective-permute-start.19) | collective-permute-done | bytes 497696 | tf_op jit(solution)/shard_map/ppermute | solution.py:75
  144.2 13.3 %all_gather.15.o_ref = bf16[256,1152]{1,0:T(8,128)(2,1)} all-gather(bf16[64,1152]{1,0:T(8,128)(2,1)} %reduce_sum.183), channel_id=1, replica_groups=mesh['shard'=2,'ctx'=4,'tp'=4] {'tp'}, dimensions={0}, use_global_device_ids=true | all-gather | bytes 737280 | tf_op jit(solution)/shard_map/all_gather | solution.py:532
  158.7 1.8 constant_dynamic-slice_fusion.1
  161.1 1.5 collective-permute-start.34
  162.6 1.5 collective-permute-start.35
  166.0 10.8 %ff_forward.1 = (f32[256,1152]{1,0:T(8,128)}, bf16[256,1152]{1,0:T(8,128)(2,1)}, bf16[256,1728]{1,0:T(8,128)(2,1)}, bf16[256,1728]{1,0:T(8,128)(2,1)}, bf16[256,1728]{1,0:T(8,128)(2,1)}) custom-call(s32[8]{0:T(128)} %get-tuple-element.113.index_ref, bf16[256,1152]{1,0:T(8,128)(2,1)} %all_gather.15.o_ref, bf16[256,1152]{1,0:T(8,128)(2,1)} %bitcast.131, ...), custom_call_target="tpu_custom_call" | custom-call | tf_op jit(solution)/shard_map/ff_forward/pallas_call | solution.py:248
  177.7 5.8 %ff_down.1 = bf16[256,1152]{1,0:T(8,128)(2,1)} custom-call(s32[8]{0:T(128)} %get-tuple-element.113.index_ref, bf16[256,1728]{1,0:T(8,128)(2,1)} %get-tuple-element.76.mix_ref.refs_1_, bf16[144,1728]{1,0:T(8,128)(2,1)} %refs_16_, bf16[144,1728]{1,0:T(8,128)(2,1)} %collective-permute-done.24.refs_1_.refs_17_, bf16[144,1728]{1,0:T(8,128)(2,1)} %copy-done.12, ...), custom_call_target="tpu_custom_call" | custom-call | tf_op jit(solution)/shard_map/ff_down/pallas_call | solution.py:282
  183.5 3.8 all-to-all-start.2
  188.5 1.7 slice.437
  190.4 5.4 %all-to-all-done.2 = bf16[4,64,1152]{2,1,0:T(8,128)(2,1)S(1)} async-done(((bf16[4,64,1152]{2,1,0:T(8,128)(2,1)}), bf16[4,64,1152]{2,1,0:T(8,128)(2,1)S(1)}, u32[]{:S(2)}, u32[]{:S(2)}) %all-to-all-start.2) | async-done | bytes 589856 | tf_op jit(solution)/shard_map/all_to_all | solution.py:530
  195.9 11.2 %all_gather.16.f_ref = bf16[256,1152]{1,0:T(8,128)(2,1)} all-gather(bf16[64,1152]{1,0:T(8,128)(2,1)S(1)} %reduce_sum.184), channel_id=1, replica_groups=mesh['shard'=2,'ctx'=4,'tp'=4] {'tp'}, dimensions={0}, use_global_device_ids=true | all-gather | bytes 737280 | tf_op jit(solution)/shard_map/all_gather | solution.py:532
  207.1 13.0 %ff_backward.1 = (f32[256,1152]{1,0:T(8,128)}, bf16[256,1152]{1,0:T(8,128)(2,1)}, f32[1,1152]{1,0:T(1,128)}, bf16[256,1728]{1,0:T(8,128)(2,1)}, bf16[256,1728]{1,0:T(8,128)(2,1)}, /*index=5*/bf16[256,1152]{1,0:T(8,128)(2,1)}) custom-call(s32[8]{0:T(128)} %get-tuple-element.113.index_ref, bf16[256,1152]{1,0:T(8,128)(2,1)} %all_gather.16.f_ref, ...), custom_call_target="tpu_custom_call" | custom-call | tf_op jit(solution)/shard_map/ff_backward/pallas_call | solution.py:335
  220.1 3.6 all-to-all-start.3
  224.1 4.7 shard_map.266
  228.8 4.7 shard_map.265
  234.3 12.6 %all_gather.17 = bf16[256,1152]{1,0:T(8,128)(2,1)S(1)} all-gather(bf16[64,1152]{1,0:T(8,128)(2,1)} %reduce_sum.187), channel_id=1, replica_groups=mesh['shard'=2,'ctx'=4,'tp'=4] {'tp'}, dimensions={0}, use_global_device_ids=true | all-gather | bytes 737280 | tf_op jit(solution)/shard_map/all_gather | solution.py:532
  253.9 3.6 all-to-all-start.4
  258.7 12.2 %all-to-all-done.4 = bf16[4,4,64,512]{3,2,1,0:T(8,128)(2,1)S(1)} async-done(((bf16[4,4,64,512]{3,2,1,0:T(8,128)(2,1)}), bf16[4,4,64,512]{3,2,1,0:T(8,128)(2,1)S(1)}, u32[]{:S(2)}, u32[]{:S(2)}) %all-to-all-start.4) | async-done | bytes 1048608 | tf_op jit(solution)/shard_map/all_to_all | solution.py:664
  271.4 4.8 collective-permute-done.31
  276.2 1.9 collective-permute-start.32
  278.4 3.8 collective-permute-done.32
  282.6 14.1 %all-gather = bf16[832,512]{1,0:T(8,128)(2,1)} all-gather(bf16[208,512]{1,0:T(8,128)(2,1)S(1)} %maximum_maximum_fusion), channel_id=2, replica_groups=mesh['shard'=2,'ctx'=4,'tp'=4] {'tp'}, dimensions={0}, use_global_device_ids=true | all-gather | bytes 1064960 | tf_op jit(solution)/shard_map/all_gather | solution.py:688
  296.7 6.6 %input_kernel.1 = (f32[256,1152]{1,0:T(8,128)}, f32[1,1152]{1,0:T(1,128)}) custom-call(s32[2]{0:T(128)} %pad_add_fusion.1.place_ref, bf16[4,208,512]{2,1,0:T(8,128)(2,1)} %bitcast.133, bf16[1152,384]{1,0:T(8,128)(2,1)} %get-tuple-element.86.own_ref, f32[256,1152]{1,0:T(8,128)} %copy-done.2, bf16[256,1152]{1,0:T(8,128)(2,1)} %bitcast.132, ...), custom_call_target="tpu_custom_call" | custom-call | tf_op jit(solution)/shard_map/input_kernel/pallas_call | solution.py:470
  306.0 4.7 shard_map.264
  312.7 3.2 collective-permute-done.55
  315.9 1.4 collective-permute-start.56
  318.0 3.2 shard_map.263
  322.6 1.6 fusion.35
  324.1 2.1 collective-permute-start.52
  326.6 2.0 collective-permute-start.48
  328.7 1.5 fusion.31
  330.2 2.0 collective-permute-start.44
  332.3 6.5 %collective-permute-done.52 = bf16[144,1728]{1,0:T(8,128)(2,1)S(1)} collective-permute-done((bf16[144,1728]{1,0:T(8,128)(2,1)S(1)}, bf16[144,1728]{1,0:T(8,128)(2,1)S(1)}, u32[]{:S(2)}, u32[]{:S(2)}) %collective-permute-start.52) | collective-permute-done | bytes 497696 | tf_op jit(solution)/shard_map/ppermute | solution.py:75
  338.8 2.0 collective-permute-start.43
  342.1 18.9 %collective-permute-done.48 = bf16[144,1728]{1,0:T(8,128)(2,1)S(1)} collective-permute-done((bf16[144,1728]{1,0:T(8,128)(2,1)S(1)}, bf16[144,1728]{1,0:T(8,128)(2,1)S(1)}, u32[]{:S(2)}, u32[]{:S(2)}) %collective-permute-start.48) | collective-permute-done | bytes 497696 | tf_op jit(solution)/shard_map/ppermute | solution.py:75
  361.0 2.0 collective-permute-start.40
  363.2 38.7 %collective-permute-done.40 = bf16[2,144,640]{2,1,0:T(8,128)(2,1)S(1)} collective-permute-done((bf16[2,144,640]{2,1,0:T(8,128)(2,1)S(1)}, bf16[2,144,640]{2,1,0:T(8,128)(2,1)S(1)}, u32[]{:S(2)}, u32[]{:S(2)}) %collective-permute-start.40) | collective-permute-done | bytes 368672 | tf_op jit(solution)/shard_map/ppermute | solution.py:75
  401.8 1.3 collective-permute-start.53
  403.2 1.7 collective-permute-start.41
  406.2 29.1 %collective-permute-done.41 = bf16[1,144,640]{2,1,0:T(8,128)(2,1)S(1)} collective-permute-done((bf16[1,144,640]{2,1,0:T(8,128)(2,1)S(1)}, bf16[1,144,640]{2,1,0:T(8,128)(2,1)S(1)}, u32[]{:S(2)}, u32[]{:S(2)}) %collective-permute-start.41) | collective-permute-done | bytes 184352 | tf_op jit(solution)/shard_map/ppermute | solution.py:75
  436.7 2.9 collective-permute-start.45
  439.7 2.3 fusion.19
  442.0 27.8 %collective-permute-done.49 = bf16[144,1728]{1,0:T(8,128)(2,1)S(1)} collective-permute-done((bf16[144,1728]{1,0:T(8,128)(2,1)S(1)}, bf16[144,1728]{1,0:T(8,128)(2,1)S(1)}, u32[]{:S(2)}, u32[]{:S(2)}) %collective-permute-start.49) | collective-permute-done | bytes 497696 | tf_op jit(solution)/shard_map/ppermute | solution.py:75
  471.0 9.7 %collective-permute-done.45 = bf16[144,1728]{1,0:T(8,128)(2,1)S(1)} collective-permute-done((bf16[144,1728]{1,0:T(8,128)(2,1)S(1)}, bf16[144,1728]{1,0:T(8,128)(2,1)S(1)}, u32[]{:S(2)}, u32[]{:S(2)}) %collective-permute-start.45) | collective-permute-done | bytes 497696 | tf_op jit(solution)/shard_map/ppermute | solution.py:75
  480.8 2.2 fusion.23
  (286 shorter events, 48.9 us)
Async XLA Ops:
  2.5 15.4 %collective-permute-start = (bf16[160,640]{1,0:T(8,128)(2,1)S(1)}, bf16[160,640]{1,0:T(8,128)(2,1)S(1)}, u32[]{:S(2)}, u32[]{:S(2)}) collective-permute-start(bf16[160,640]{1,0:T(8,128)(2,1)S(1)} %fusion.43.refs_0_), channel_id=1, source_target_pairs={{0,8},{4,12},{8,0},{12,4},{1,9},{5,13},{9,1},{13,5},{2,10},{6,14},... | collective-permute-start | bytes 614408 | tf_op jit(solution)/shard_map/ppermute | solution.py:75
  6.6 11.2 %collective-permute-start.1 = (bf16[160,640]{1,0:T(8,128)(2,1)S(1)}, bf16[160,640]{1,0:T(8,128)(2,1)S(1)}, u32[]{:S(2)}, u32[]{:S(2)}) collective-permute-start(bf16[160,640]{1,0:T(8,128)(2,1)S(1)} %fusion.43.refs_0_), channel_id=1, source_target_pairs={{0,4},{4,0},{8,12},{12,8},{1,5},{5,1},{9,13},{13,9},{2,6},{6,2},{1... | collective-permute-start | bytes 614408 | tf_op jit(solution)/shard_map/ppermute | solution.py:75
  8.2 14.6 %collective-permute-start.2 = (bf16[160,640]{1,0:T(8,128)(2,1)S(1)}, bf16[160,640]{1,0:T(8,128)(2,1)S(1)}, u32[]{:S(2)}, u32[]{:S(2)}) collective-permute-start(bf16[160,640]{1,0:T(8,128)(2,1)S(1)} %fusion.43.refs_0_), channel_id=1, source_target_pairs={{0,12},{4,8},{8,4},{12,0},{1,13},{5,9},{9,5},{13,1},{2,14},{6,10},... | collective-permute-start | bytes 614408 | tf_op jit(solution)/shard_map/ppermute | solution.py:75
  8.2 17.2 %collective-permute-start.3 = (bf16[160,640]{1,0:T(8,128)(2,1)S(1)}, bf16[160,640]{1,0:T(8,128)(2,1)S(1)}, u32[]{:S(2)}, u32[]{:S(2)}) collective-permute-start(bf16[160,640]{1,0:T(8,128)(2,1)S(1)} %fusion.43.refs_0_), channel_id=1, source_target_pairs={{0,16},{16,0},{1,17},{17,1},{2,18},{18,2},{3,19},{19,3},{4,20},{20... | collective-permute-start | bytes 614408 | tf_op jit(solution)/shard_map/ppermute | solution.py:75
  8.2 64.6 %collective-permute-start.10 = (bf16[144,1728]{1,0:T(8,128)(2,1)}, bf16[144,1728]{1,0:T(8,128)(2,1)}, u32[]{:S(2)}, u32[]{:S(2)}) collective-permute-start(bf16[144,1728]{1,0:T(8,128)(2,1)} %refs_0_.2), channel_id=1, source_target_pairs={{0,8},{4,12},{8,0},{12,4},{1,9},{5,13},{9,1},{13,5},{2,10},{6,14},... | collective-permute-start | bytes 1493000 | tf_op jit(solution)/shard_map/ppermute | solution.py:75
  22.9 17.1 %collective-permute-start.4 = (bf16[160,640]{1,0:T(8,128)(2,1)S(1)}, bf16[160,640]{1,0:T(8,128)(2,1)S(1)}, u32[]{:S(2)}, u32[]{:S(2)}) collective-permute-start(bf16[160,640]{1,0:T(8,128)(2,1)S(1)} %collective-permute-done.refs_1_), channel_id=1, source_target_pairs={{0,16},{16,0},{1,17},{17,1},{2,18},{18,2},{3,19},{19,3},{4,20},{20... | collective-permute-start | bytes 614408 | tf_op jit(solution)/shard_map/ppermute | solution.py:75
  22.9 17.1 %collective-permute-start.5 = (bf16[160,640]{1,0:T(8,128)(2,1)S(1)}, bf16[160,640]{1,0:T(8,128)(2,1)S(1)}, u32[]{:S(2)}, u32[]{:S(2)}) collective-permute-start(bf16[160,640]{1,0:T(8,128)(2,1)S(1)} %collective-permute-done.1.refs_2_), channel_id=1, source_target_pairs={{0,16},{16,0},{1,17},{17,1},{2,18},{18,2},{3,19},{19,3},{4,20},{20... | collective-permute-start | bytes 614408 | tf_op jit(solution)/shard_map/ppermute | solution.py:75
  23.4 16.7 %collective-permute-start.6 = (bf16[160,640]{1,0:T(8,128)(2,1)S(1)}, bf16[160,640]{1,0:T(8,128)(2,1)S(1)}, u32[]{:S(2)}, u32[]{:S(2)}) collective-permute-start(bf16[160,640]{1,0:T(8,128)(2,1)S(1)} %collective-permute-done.2.refs_3_), channel_id=1, source_target_pairs={{0,16},{16,0},{1,17},{17,1},{2,18},{18,2},{3,19},{19,3},{4,20},{20... | collective-permute-start | bytes 614408 | tf_op jit(solution)/shard_map/ppermute | solution.py:75
  25.4 65.1 %collective-permute-start.11 = (bf16[144,1728]{1,0:T(8,128)(2,1)S(1)}, bf16[144,1728]{1,0:T(8,128)(2,1)}, u32[]{:S(2)}, u32[]{:S(2)}) collective-permute-start(bf16[144,1728]{1,0:T(8,128)(2,1)S(1)} %copy-done.11), channel_id=1, source_target_pairs={{0,4},{4,0},{8,12},{12,8},{1,5},{5,1},{9,13},{13,9},{2,6},{6,2},{1... | collective-permute-start | bytes 1493000 | tf_op jit(solution)/shard_map/ppermute | solution.py:75
  46.0 7.6 %collective-permute-start.7 = (bf16[256,128]{1,0:T(8,128)(2,1)S(1)}, bf16[256,128]{1,0:T(8,128)(2,1)S(1)}, u32[]{:S(2)}, u32[]{:S(2)}) collective-permute-start(bf16[256,128]{1,0:T(8,128)(2,1)S(1)} %slice.596), channel_id=1, source_target_pairs={{0,8},{4,12},{8,0},{12,4},{1,9},{5,13},{9,1},{13,5},{2,10},{6,14},... | collective-permute-start | bytes 196616 | tf_op jit(solution)/shard_map/ppermute | solution.py:75
  47.3 16.0 %collective-permute-start.8 = (bf16[256,128]{1,0:T(8,128)(2,1)S(1)}, bf16[256,128]{1,0:T(8,128)(2,1)S(1)}, u32[]{:S(2)}, u32[]{:S(2)}) collective-permute-start(bf16[256,128]{1,0:T(8,128)(2,1)S(1)} %slice.596), channel_id=1, source_target_pairs={{0,4},{4,0},{8,12},{12,8},{1,5},{5,1},{9,13},{13,9},{2,6},{6,2},{1... | collective-permute-start | bytes 196616 | tf_op jit(solution)/shard_map/ppermute | solution.py:75
  49.3 14.0 %collective-permute-start.9 = (bf16[256,128]{1,0:T(8,128)(2,1)S(1)}, bf16[256,128]{1,0:T(8,128)(2,1)S(1)}, u32[]{:S(2)}, u32[]{:S(2)}) collective-permute-start(bf16[256,128]{1,0:T(8,128)(2,1)S(1)} %slice.596), channel_id=1, source_target_pairs={{0,12},{4,8},{8,4},{12,0},{1,13},{5,9},{9,5},{13,1},{2,14},{6,10},... | collective-permute-start | bytes 196616 | tf_op jit(solution)/shard_map/ppermute | solution.py:75
  53.6 36.6 %collective-permute-start.17 = (bf16[144,1728]{1,0:T(8,128)(2,1)}, bf16[144,1728]{1,0:T(8,128)(2,1)}, u32[]{:S(2)}, u32[]{:S(2)}) collective-permute-start(bf16[144,1728]{1,0:T(8,128)(2,1)} %refs_8_.1), channel_id=1, source_target_pairs={{0,8},{4,12},{8,0},{12,4},{1,9},{5,13},{9,1},{13,5},{2,10},{6,14},... | collective-permute-start | bytes 1493000 | tf_op jit(solution)/shard_map/ppermute | solution.py:75
  63.3 47.1 %collective-permute-start.18 = (bf16[144,1728]{1,0:T(8,128)(2,1)}, bf16[144,1728]{1,0:T(8,128)(2,1)}, u32[]{:S(2)}, u32[]{:S(2)}) collective-permute-start(bf16[144,1728]{1,0:T(8,128)(2,1)} %refs_8_.1), channel_id=1, source_target_pairs={{0,4},{4,0},{8,12},{12,8},{1,5},{5,1},{9,13},{13,9},{2,6},{6,2},{1... | collective-permute-start | bytes 1493000 | tf_op jit(solution)/shard_map/ppermute | solution.py:75
  63.3 47.1 %collective-permute-start.24 = (bf16[144,1728]{1,0:T(8,128)(2,1)}, bf16[144,1728]{1,0:T(8,128)(2,1)}, u32[]{:S(2)}, u32[]{:S(2)}) collective-permute-start(bf16[144,1728]{1,0:T(8,128)(2,1)} %refs_16_), channel_id=1, source_target_pairs={{0,8},{4,12},{8,0},{12,4},{1,9},{5,13},{9,1},{13,5},{2,10},{6,14},... | collective-permute-start | bytes 1493000 | tf_op jit(solution)/shard_map/ppermute | solution.py:75
  68.0 17.2 %all-to-all-start = ((bf16[4,1024,128]{2,1,0:T(8,128)(2,1)}), bf16[4,1024,128]{2,1,0:T(8,128)(2,1)S(1)}, u32[]{:S(2)}, u32[]{:S(2)}) async-start(bf16[4,1024,128]{2,1,0:T(8,128)(2,1)} %broadcast_in_dim.28), calls=%async_computation | async-start | bytes 2097152 | tf_op jit(solution)/shard_map/all_to_all | solution.py:592
  72.8 37.6 %collective-permute-start.12 = (bf16[144,1728]{1,0:T(8,128)(2,1)}, bf16[144,1728]{1,0:T(8,128)(2,1)}, u32[]{:S(2)}, u32[]{:S(2)}) collective-permute-start(bf16[144,1728]{1,0:T(8,128)(2,1)} %collective-permute-done.10.refs_1_), channel_id=1, source_target_pairs={{0,4},{4,0},{8,12},{12,8},{1,5},{5,1},{9,13},{13,9},{2,6},{6,2},{1... | collective-permute-start | bytes 1493000 | tf_op jit(solution)/shard_map/ppermute | solution.py:75
  88.6 160.0 %copy-start.21 = (bf16[256,256]{1,0:T(8,128)(2,1)}, bf16[256,256]{1,0:T(8,128)(2,1)S(1)}, u32[]{:S(2)}) copy-start(bf16[256,256]{1,0:T(8,128)(2,1)S(1)} %fusion.12.refs_3_) | copy-start | bytes 393220
  90.3 42.2 %collective-permute-start.25 = (bf16[144,1728]{1,0:T(8,128)(2,1)}, bf16[144,1728]{1,0:T(8,128)(2,1)S(1)}, u32[]{:S(2)}, u32[]{:S(2)}) collective-permute-start(bf16[144,1728]{1,0:T(8,128)(2,1)} %refs_16_), channel_id=1, source_target_pairs={{0,4},{4,0},{8,12},{12,8},{1,5},{5,1},{9,13},{13,9},{2,6},{6,2},{1... | collective-permute-start | bytes 1493000 | tf_op jit(solution)/shard_map/ppermute | solution.py:75
  90.5 41.9 %collective-permute-start.26 = (bf16[144,1728]{1,0:T(8,128)(2,1)}, bf16[144,1728]{1,0:T(8,128)(2,1)S(1)}, u32[]{:S(2)}, u32[]{:S(2)}) collective-permute-start(bf16[144,1728]{1,0:T(8,128)(2,1)} %refs_16_), channel_id=1, source_target_pairs={{0,12},{4,8},{8,4},{12,0},{1,13},{5,9},{9,5},{13,1},{2,14},{6,10},... | collective-permute-start | bytes 1493000 | tf_op jit(solution)/shard_map/ppermute | solution.py:75
  110.4 32.4 %collective-permute-start.19 = (bf16[144,1728]{1,0:T(8,128)(2,1)}, bf16[144,1728]{1,0:T(8,128)(2,1)}, u32[]{:S(2)}, u32[]{:S(2)}) collective-permute-start(bf16[144,1728]{1,0:T(8,128)(2,1)} %collective-permute-done.17.refs_9_), channel_id=1, source_target_pairs={{0,4},{4,0},{8,12},{12,8},{1,5},{5,1},{9,13},{13,9},{2,6},{6,2},{1... | collective-permute-start | bytes 1493000 | tf_op jit(solution)/shard_map/ppermute | solution.py:75
  110.4 32.4 %collective-permute-start.16 = (bf16[144,1728]{1,0:T(8,128)(2,1)}, bf16[144,1728]{1,0:T(8,128)(2,1)}, u32[]{:S(2)}, u32[]{:S(2)}) collective-permute-start(bf16[144,1728]{1,0:T(8,128)(2,1)} %collective-permute-done.12.refs_3_), channel_id=1, source_target_pairs={{0,16},{16,0},{1,17},{17,1},{2,18},{18,2},{3,19},{19,3},{4,20},{20... | collective-permute-start | bytes 1493000 | tf_op jit(solution)/shard_map/ppermute | solution.py:75
  110.4 32.9 %collective-permute-start.14 = (bf16[144,1728]{1,0:T(8,128)(2,1)}, bf16[144,1728]{1,0:T(8,128)(2,1)}, u32[]{:S(2)}, u32[]{:S(2)}) collective-permute-start(bf16[144,1728]{1,0:T(8,128)(2,1)} %collective-permute-done.10.refs_1_), channel_id=1, source_target_pairs={{0,16},{16,0},{1,17},{17,1},{2,18},{18,2},{3,19},{19,3},{4,20},{20... | collective-permute-start | bytes 1493000 | tf_op jit(solution)/shard_map/ppermute | solution.py:75
  110.9 32.5 %all-to-all-start.1 = ((bf16[4,64,1152]{2,1,0:T(8,128)(2,1)}), bf16[4,64,1152]{2,1,0:T(8,128)(2,1)S(1)}, u32[]{:S(2)}, u32[]{:S(2)}) async-start(bf16[4,64,1152]{2,1,0:T(8,128)(2,1)} %bitcast.11), calls=%async_computation.1 | async-start | bytes 1179648 | tf_op jit(solution)/shard_map/all_to_all | solution.py:530
  114.7 50.6 %copy-start.42 = (f32[1152]{0:T(1024)S(1)}, f32[1152]{0:T(1024)}, u32[]{:S(2)}) copy-start(f32[1152]{0:T(1024)} %param.32) | copy-start | bytes 13828
  132.4 25.1 %collective-permute-start.15 = (bf16[144,1728]{1,0:T(8,128)(2,1)}, bf16[144,1728]{1,0:T(8,128)(2,1)}, u32[]{:S(2)}, u32[]{:S(2)}) collective-permute-start(bf16[144,1728]{1,0:T(8,128)(2,1)} %collective-permute-done.11.refs_2_), channel_id=1, source_target_pairs={{0,16},{16,0},{1,17},{17,1},{2,18},{18,2},{3,19},{19,3},{4,20},{20... | collective-permute-start | bytes 1493000 | tf_op jit(solution)/shard_map/ppermute | solution.py:75
  132.4 25.1 %collective-permute-start.21 = (bf16[144,1728]{1,0:T(8,128)(2,1)}, bf16[144,1728]{1,0:T(8,128)(2,1)}, u32[]{:S(2)}, u32[]{:S(2)}) collective-permute-start(bf16[144,1728]{1,0:T(8,128)(2,1)} %collective-permute-done.17.refs_9_), channel_id=1, source_target_pairs={{0,16},{16,0},{1,17},{17,1},{2,18},{18,2},{3,19},{19,3},{4,20},{20... | collective-permute-start | bytes 1493000 | tf_op jit(solution)/shard_map/ppermute | solution.py:75
  142.8 15.2 %collective-permute-start.22 = (bf16[144,1728]{1,0:T(8,128)(2,1)}, bf16[144,1728]{1,0:T(8,128)(2,1)}, u32[]{:S(2)}, u32[]{:S(2)}) collective-permute-start(bf16[144,1728]{1,0:T(8,128)(2,1)} %collective-permute-done.18.refs_10_), channel_id=1, source_target_pairs={{0,16},{16,0},{1,17},{17,1},{2,18},{18,2},{3,19},{19,3},{4,20},{20... | collective-permute-start | bytes 1493000 | tf_op jit(solution)/shard_map/ppermute | solution.py:75
  142.8 15.3 %collective-permute-start.13 = (bf16[144,1728]{1,0:T(8,128)(2,1)S(1)}, bf16[144,1728]{1,0:T(8,128)(2,1)}, u32[]{:S(2)}, u32[]{:S(2)}) collective-permute-start(bf16[144,1728]{1,0:T(8,128)(2,1)S(1)} %copy-done.11), channel_id=1, source_target_pairs={{0,16},{16,0},{1,17},{17,1},{2,18},{18,2},{3,19},{19,3},{4,20},{20... | collective-permute-start | bytes 1493000 | tf_op jit(solution)/shard_map/ppermute | solution.py:75
  143.3 15.2 %collective-permute-start.20 = (bf16[144,1728]{1,0:T(8,128)(2,1)}, bf16[144,1728]{1,0:T(8,128)(2,1)}, u32[]{:S(2)}, u32[]{:S(2)}) collective-permute-start(bf16[144,1728]{1,0:T(8,128)(2,1)} %refs_8_.1), channel_id=1, source_target_pairs={{0,16},{16,0},{1,17},{17,1},{2,18},{18,2},{3,19},{19,3},{4,20},{20... | collective-permute-start | bytes 1493000 | tf_op jit(solution)/shard_map/ppermute | solution.py:75
  157.5 3.0 collective-permute-start.28
  157.6 3.6 collective-permute-start.29
  158.1 4.6 collective-permute-start.23
  158.1 18.7 %collective-permute-start.30 = (bf16[144,1728]{1,0:T(8,128)(2,1)S(1)}, bf16[144,1728]{1,0:T(8,128)(2,1)S(1)}, u32[]{:S(2)}, u32[]{:S(2)}) collective-permute-start(bf16[144,1728]{1,0:T(8,128)(2,1)S(1)} %collective-permute-done.26.refs_3_.refs_19_), channel_id=1, source_target_pairs={{0,16},{16,0},{1,17},{17,1},{2,18},{18,2},{3,19},{19,3},{4,20},{20... | collective-permute-start | bytes 1493000 | tf_op jit(solution)/shard_map/ppermute | solution.py:75
  158.6 18.3 %collective-permute-start.27 = (bf16[144,1728]{1,0:T(8,128)(2,1)}, bf16[144,1728]{1,0:T(8,128)(2,1)}, u32[]{:S(2)}, u32[]{:S(2)}) collective-permute-start(bf16[144,1728]{1,0:T(8,128)(2,1)} %refs_16_), channel_id=1, source_target_pairs={{0,16},{16,0},{1,17},{17,1},{2,18},{18,2},{3,19},{19,3},{4,20},{20... | collective-permute-start | bytes 1493000 | tf_op jit(solution)/shard_map/ppermute | solution.py:75
  160.5 27.4 %collective-permute-start.33 = (bf16[576,384]{1,0:T(8,128)(2,1)}, bf16[576,384]{1,0:T(8,128)(2,1)}, u32[]{:S(2)}, u32[]{:S(2)}) collective-permute-start(bf16[576,384]{1,0:T(8,128)(2,1)} %constant_dynamic-slice_fusion.1), channel_id=1, source_target_pairs={{0,2},{1,3},{2,0},{3,1},{4,6},{5,7},{6,4},{7,5},{8,10},{9,11},{10,... | collective-permute-start | bytes 1327112 | tf_op jit(solution)/shard_map/ppermute | solution.py:75
  161.1 26.8 %collective-permute-start.34 = (bf16[576,384]{1,0:T(8,128)(2,1)}, bf16[576,384]{1,0:T(8,128)(2,1)}, u32[]{:S(2)}, u32[]{:S(2)}) collective-permute-start(bf16[576,384]{1,0:T(8,128)(2,1)} %constant_dynamic-slice_fusion.1), channel_id=1, source_target_pairs={{0,1},{1,0},{2,3},{3,2},{4,5},{5,4},{6,7},{7,6},{8,9},{9,8},{10,11... | collective-permute-start | bytes 1327112 | tf_op jit(solution)/shard_map/ppermute | solution.py:75
  162.6 25.8 %collective-permute-start.35 = (bf16[576,384]{1,0:T(8,128)(2,1)}, bf16[576,384]{1,0:T(8,128)(2,1)}, u32[]{:S(2)}, u32[]{:S(2)}) collective-permute-start(bf16[576,384]{1,0:T(8,128)(2,1)} %constant_dynamic-slice_fusion.1), channel_id=1, source_target_pairs={{0,3},{1,2},{2,1},{3,0},{4,7},{5,6},{6,5},{7,4},{8,11},{9,10},{10,... | collective-permute-start | bytes 1327112 | tf_op jit(solution)/shard_map/ppermute | solution.py:75
  183.5 12.3 %all-to-all-start.2 = ((bf16[4,64,1152]{2,1,0:T(8,128)(2,1)}), bf16[4,64,1152]{2,1,0:T(8,128)(2,1)S(1)}, u32[]{:S(2)}, u32[]{:S(2)}) async-start(bf16[4,64,1152]{2,1,0:T(8,128)(2,1)} %bitcast.137), calls=%async_computation.2 | async-start | bytes 1179648 | tf_op jit(solution)/shard_map/all_to_all | solution.py:530
  187.9 108.8 %collective-permute-start.36 = (bf16[576,384]{1,0:T(8,128)(2,1)}, bf16[576,384]{1,0:T(8,128)(2,1)}, u32[]{:S(2)}, u32[]{:S(2)}) collective-permute-start(bf16[576,384]{1,0:T(8,128)(2,1)} %collective-permute-done.33.refs_0_), channel_id=1, source_target_pairs={{0,16},{16,0},{1,17},{17,1},{2,18},{18,2},{3,19},{19,3},{4,20},{20... | collective-permute-start | bytes 1327112 | tf_op jit(solution)/shard_map/ppermute | solution.py:75
  187.9 108.8 %collective-permute-start.37 = (bf16[576,384]{1,0:T(8,128)(2,1)}, bf16[576,384]{1,0:T(8,128)(2,1)}, u32[]{:S(2)}, u32[]{:S(2)}) collective-permute-start(bf16[576,384]{1,0:T(8,128)(2,1)} %collective-permute-done.34.refs_1_), channel_id=1, source_target_pairs={{0,16},{16,0},{1,17},{17,1},{2,18},{18,2},{3,19},{19,3},{4,20},{20... | collective-permute-start | bytes 1327112 | tf_op jit(solution)/shard_map/ppermute | solution.py:75
  188.4 108.3 %collective-permute-start.38 = (bf16[576,384]{1,0:T(8,128)(2,1)}, bf16[576,384]{1,0:T(8,128)(2,1)}, u32[]{:S(2)}, u32[]{:S(2)}) collective-permute-start(bf16[576,384]{1,0:T(8,128)(2,1)} %collective-permute-done.35.refs_2_), channel_id=1, source_target_pairs={{0,16},{16,0},{1,17},{17,1},{2,18},{18,2},{3,19},{19,3},{4,20},{20... | collective-permute-start | bytes 1327112 | tf_op jit(solution)/shard_map/ppermute | solution.py:75
  220.1 13.4 %all-to-all-start.3 = ((bf16[4,64,1152]{2,1,0:T(8,128)(2,1)}), bf16[4,64,1152]{2,1,0:T(8,128)(2,1)S(1)}, u32[]{:S(2)}, u32[]{:S(2)}) async-start(bf16[4,64,1152]{2,1,0:T(8,128)(2,1)} %bitcast.140), calls=%async_computation.3 | async-start | bytes 1179648 | tf_op jit(solution)/shard_map/all_to_all | solution.py:530
  228.8 93.8 %collective-permute-start.50 = (bf16[4,144,1728]{2,1,0:T(8,128)(2,1)}, bf16[4,144,1728]{2,1,0:T(8,128)(2,1)}, u32[]{:S(2)}, u32[]{:S(2)}) collective-permute-start(bf16[4,144,1728]{2,1,0:T(8,128)(2,1)} %get-tuple-element.101), channel_id=1, source_target_pairs={{0,16},{16,0},{1,17},{17,1},{2,18},{18,2},{3,19},{19,3},{4,20},{20... | collective-permute-start | bytes 5971976 | tf_op jit(solution)/shard_map/ppermute | solution.py:75
  253.9 17.0 %all-to-all-start.4 = ((bf16[4,4,64,512]{3,2,1,0:T(8,128)(2,1)}), bf16[4,4,64,512]{3,2,1,0:T(8,128)(2,1)S(1)}, u32[]{:S(2)}, u32[]{:S(2)}) async-start(bf16[4,4,64,512]{3,2,1,0:T(8,128)(2,1)} %copy_bitcast_fusion), calls=%async_computation.4 | async-start | bytes 2097152 | tf_op jit(solution)/shard_map/all_to_all | solution.py:664
  271.1 5.0 %collective-permute-start.31 = (bf16[128,512]{1,0:T(8,128)(2,1)S(1)}, bf16[128,512]{1,0:T(8,128)(2,1)S(1)}, u32[]{:S(2)}, u32[]{:S(2)}) collective-permute-start(bf16[128,512]{1,0:T(8,128)(2,1)S(1)} %bitcast.142), channel_id=1, source_target_pairs={{0,4},{4,0},{8,12},{12,8},{1,5},{5,1},{9,13},{13,9},{2,6},{6,2},{1... | collective-permute-start | bytes 393224 | tf_op jit(solution)/shard_map/ppermute | solution.py:75
  276.2 5.9 %collective-permute-start.32 = (bf16[64,512]{1,0:T(8,128)(2,1)S(1)}, bf16[64,512]{1,0:T(8,128)(2,1)S(1)}, u32[]{:S(2)}, u32[]{:S(2)}) collective-permute-start(bf16[64,512]{1,0:T(8,128)(2,1)S(1)} %slice.433), channel_id=1, source_target_pairs={{0,8},{4,12},{8,0},{12,4},{1,9},{5,13},{9,1},{13,5},{2,10},{6,14},... | collective-permute-start | bytes 196616 | tf_op jit(solution)/shard_map/ppermute | solution.py:75
  282.2 44.2 %collective-permute-start.46 = (bf16[4,144,1728]{2,1,0:T(8,128)(2,1)}, bf16[4,144,1728]{2,1,0:T(8,128)(2,1)S(1)}, u32[]{:S(2)}, u32[]{:S(2)}) collective-permute-start(bf16[4,144,1728]{2,1,0:T(8,128)(2,1)} %get-tuple-element.98), channel_id=1, source_target_pairs={{0,16},{16,0},{1,17},{17,1},{2,18},{18,2},{3,19},{19,3},{4,20},{20... | collective-permute-start | bytes 5971976 | tf_op jit(solution)/shard_map/ppermute | solution.py:75
  305.9 6.4 %collective-permute-start.54 = (bf16[4,1,640]{2,0,1:T(4,128)(2,1)S(1)}, bf16[4,1,640]{2,0,1:T(4,128)(2,1)S(1)}, u32[]{:S(2)}, u32[]{:S(2)}) collective-permute-start(bf16[4,1,640]{2,0,1:T(4,128)(2,1)S(1)} %fusion.47), channel_id=1, source_target_pairs={{0,16},{16,0},{1,17},{17,1},{2,18},{18,2},{3,19},{19,3},{4,20},{20... | collective-permute-start | bytes 15368 | tf_op jit(solution)/shard_map/ppermute | solution.py:75
  310.6 18.0 %collective-permute-start.42 = (bf16[4,144,1728]{2,1,0:T(8,128)(2,1)}, bf16[4,144,1728]{2,1,0:T(8,128)(2,1)}, u32[]{:S(2)}, u32[]{:S(2)}) collective-permute-start(bf16[4,144,1728]{2,1,0:T(8,128)(2,1)} %get-tuple-element.94), channel_id=1, source_target_pairs={{0,16},{16,0},{1,17},{17,1},{2,18},{18,2},{3,19},{19,3},{4,20},{20... | collective-permute-start | bytes 5971976 | tf_op jit(solution)/shard_map/ppermute | solution.py:75
  312.3 3.7 collective-permute-start.55
  315.9 5.4 %collective-permute-start.56 = (bf16[1,1,640]{2,0,1:T(2,128)(2,1)S(1)}, bf16[1,1,640]{2,0,1:T(2,128)(2,1)S(1)}, u32[]{:S(2)}, u32[]{:S(2)}) collective-permute-start(bf16[1,1,640]{2,0,1:T(2,128)(2,1)S(1)} %fusion.51), channel_id=1, source_target_pairs={{0,8},{4,12},{8,0},{12,4},{1,9},{5,13},{9,1},{13,5},{2,10},{6,14},... | collective-permute-start | bytes 3848 | tf_op jit(solution)/shard_map/ppermute | solution.py:75
  321.2 9.0 %collective-permute-start.39 = (bf16[4,144,640]{2,1,0:T(8,128)(2,1)}, bf16[4,144,640]{2,1,0:T(8,128)(2,1)S(1)}, u32[]{:S(2)}, u32[]{:S(2)}) collective-permute-start(bf16[4,144,640]{2,1,0:T(8,128)(2,1)} %get-tuple-element.90), channel_id=1, source_target_pairs={{0,16},{16,0},{1,17},{17,1},{2,18},{18,2},{3,19},{19,3},{4,20},{20... | collective-permute-start | bytes 2211848 | tf_op jit(solution)/shard_map/ppermute | solution.py:75
  324.1 14.7 %collective-permute-start.52 = (bf16[144,1728]{1,0:T(8,128)(2,1)S(1)}, bf16[144,1728]{1,0:T(8,128)(2,1)S(1)}, u32[]{:S(2)}, u32[]{:S(2)}) collective-permute-start(bf16[144,1728]{1,0:T(8,128)(2,1)S(1)} %get-tuple-element.121), channel_id=1, source_target_pairs={{0,4},{4,0},{8,12},{12,8},{1,5},{5,1},{9,13},{13,9},{2,6},{6,2},{1... | collective-permute-start | bytes 1493000 | tf_op jit(solution)/shard_map/ppermute | solution.py:75
  326.2 110.5 %collective-permute-start.51 = (bf16[144,1728]{1,0:T(8,128)(2,1)S(1)}, bf16[144,1728]{1,0:T(8,128)(2,1)S(1)}, u32[]{:S(2)}, u32[]{:S(2)}) collective-permute-start(bf16[144,1728]{1,0:T(8,128)(2,1)S(1)} %get-tuple-element.120), channel_id=1, source_target_pairs={{0,4},{4,0},{8,12},{12,8},{1,5},{5,1},{9,13},{13,9},{2,6},{6,2},{1... | collective-permute-start | bytes 1493000 | tf_op jit(solution)/shard_map/ppermute | solution.py:75
  326.6 34.4 %collective-permute-start.48 = (bf16[144,1728]{1,0:T(8,128)(2,1)S(1)}, bf16[144,1728]{1,0:T(8,128)(2,1)S(1)}, u32[]{:S(2)}, u32[]{:S(2)}) collective-permute-start(bf16[144,1728]{1,0:T(8,128)(2,1)S(1)} %get-tuple-element.123), channel_id=1, source_target_pairs={{0,4},{4,0},{8,12},{12,8},{1,5},{5,1},{9,13},{13,9},{2,6},{6,2},{1... | collective-permute-start | bytes 1493000 | tf_op jit(solution)/shard_map/ppermute | solution.py:75
  328.6 113.4 %collective-permute-start.47 = (bf16[144,1728]{1,0:T(8,128)(2,1)S(1)}, bf16[144,1728]{1,0:T(8,128)(2,1)S(1)}, u32[]{:S(2)}, u32[]{:S(2)}) collective-permute-start(bf16[144,1728]{1,0:T(8,128)(2,1)S(1)} %get-tuple-element.122), channel_id=1, source_target_pairs={{0,4},{4,0},{8,12},{12,8},{1,5},{5,1},{9,13},{13,9},{2,6},{6,2},{1... | collective-permute-start | bytes 1493000 | tf_op jit(solution)/shard_map/ppermute | solution.py:75
  330.2 73.0 %collective-permute-start.44 = (bf16[144,1728]{1,0:T(8,128)(2,1)S(1)}, bf16[144,1728]{1,0:T(8,128)(2,1)S(1)}, u32[]{:S(2)}, u32[]{:S(2)}) collective-permute-start(bf16[144,1728]{1,0:T(8,128)(2,1)S(1)} %get-tuple-element.125), channel_id=1, source_target_pairs={{0,4},{4,0},{8,12},{12,8},{1,5},{5,1},{9,13},{13,9},{2,6},{6,2},{1... | collective-permute-start | bytes 1493000 | tf_op jit(solution)/shard_map/ppermute | solution.py:75
  338.8 132.2 %collective-permute-start.43 = (bf16[144,1728]{1,0:T(8,128)(2,1)S(1)}, bf16[144,1728]{1,0:T(8,128)(2,1)S(1)}, u32[]{:S(2)}, u32[]{:S(2)}) collective-permute-start(bf16[144,1728]{1,0:T(8,128)(2,1)S(1)} %get-tuple-element.124), channel_id=1, source_target_pairs={{0,4},{4,0},{8,12},{12,8},{1,5},{5,1},{9,13},{13,9},{2,6},{6,2},{1... | collective-permute-start | bytes 1493000 | tf_op jit(solution)/shard_map/ppermute | solution.py:75
  361.0 40.9 %collective-permute-start.40 = (bf16[2,144,640]{2,1,0:T(8,128)(2,1)S(1)}, bf16[2,144,640]{2,1,0:T(8,128)(2,1)S(1)}, u32[]{:S(2)}, u32[]{:S(2)}) collective-permute-start(bf16[2,144,640]{2,1,0:T(8,128)(2,1)S(1)} %add_convert_fusion.6), channel_id=1, source_target_pairs={{0,4},{4,0},{8,12},{12,8},{1,5},{5,1},{9,13},{13,9},{2,6},{6,2},{1... | collective-permute-start | bytes 1105928 | tf_op jit(solution)/shard_map/ppermute | solution.py:75
  401.8 37.8 %collective-permute-start.53 = (bf16[144,1728]{1,0:T(8,128)(2,1)S(1)}, bf16[144,1728]{1,0:T(8,128)(2,1)S(1)}, u32[]{:S(2)}, u32[]{:S(2)}) collective-permute-start(bf16[144,1728]{1,0:T(8,128)(2,1)S(1)} %fusion.18), channel_id=1, source_target_pairs={{0,8},{4,12},{8,0},{12,4},{1,9},{5,13},{9,1},{13,5},{2,10},{6,14},... | collective-permute-start | bytes 1493000 | tf_op jit(solution)/shard_map/ppermute | solution.py:75
  403.2 32.0 %collective-permute-start.41 = (bf16[1,144,640]{2,1,0:T(8,128)(2,1)S(1)}, bf16[1,144,640]{2,1,0:T(8,128)(2,1)S(1)}, u32[]{:S(2)}, u32[]{:S(2)}) collective-permute-start(bf16[1,144,640]{2,1,0:T(8,128)(2,1)S(1)} %add_convert_fusion.7), channel_id=1, source_target_pairs={{0,8},{4,12},{8,0},{12,4},{1,9},{5,13},{9,1},{13,5},{2,10},{6,14},... | collective-permute-start | bytes 552968 | tf_op jit(solution)/shard_map/ppermute | solution.py:75
  435.3 34.6 %collective-permute-start.49 = (bf16[144,1728]{1,0:T(8,128)(2,1)S(1)}, bf16[144,1728]{1,0:T(8,128)(2,1)S(1)}, u32[]{:S(2)}, u32[]{:S(2)}) collective-permute-start(bf16[144,1728]{1,0:T(8,128)(2,1)S(1)} %fusion.20), channel_id=1, source_target_pairs={{0,8},{4,12},{8,0},{12,4},{1,9},{5,13},{9,1},{13,5},{2,10},{6,14},... | collective-permute-start | bytes 1493000 | tf_op jit(solution)/shard_map/ppermute | solution.py:75
  436.7 44.0 %collective-permute-start.45 = (bf16[144,1728]{1,0:T(8,128)(2,1)S(1)}, bf16[144,1728]{1,0:T(8,128)(2,1)S(1)}, u32[]{:S(2)}, u32[]{:S(2)}) collective-permute-start(bf16[144,1728]{1,0:T(8,128)(2,1)S(1)} %fusion.22), channel_id=1, source_target_pairs={{0,8},{4,12},{8,0},{12,4},{1,9},{5,13},{9,1},{13,5},{2,10},{6,14},... | collective-permute-start | bytes 1493000 | tf_op jit(solution)/shard_map/ppermute | solution.py:75
  (43 other events, 432.3 us)

commit v3 on v2

--- a/solution.py
+++ b/solution.py
@@ -277,7 +277,7 @@
         for copy in load_pieces(index_ref, ins, wd, sems):
             copy.wait()
         for at, size in spans(width, 384):
-            f_ref[:, at : at + size] = dot_nt(mix_ref[...], wd[at : at + size, :]).astype(BF)
+            f_ref[:, at : at + size] = dot_nt(wd[at : at + size, :], mix_ref[...]).T.astype(BF)
 
     return pl.pallas_call(
         body,
@@ -328,9 +328,8 @@
         for copy in copies:
             copy.wait()
         for at, size in spans(width, 384):
-            dff_ref[:, at : at + size] = (
-                dot_nt(dg_ref[...], wg[at : at + size, :]) + dot_nt(du_ref[...], wu[at : at + size, :])
-            ).astype(BF)
+            turned = dot_nt(wg[at : at + size, :], dg_ref[...]) + dot_nt(wu[at : at + size, :], du_ref[...])
+            dff_ref[:, at : at + size] = turned.T.astype(BF)
 
     return pl.pallas_call(
         body,
@@ -615,7 +614,7 @@
     gate_mine = gather_doubling(w_gate, kv_cols)
     up_mine = gather_doubling(w_up, o_part)
     o_bf = all_reduce_tp(o_part)
-    down_mine = gather_direct(w_down, o_bf)
+    down_mine = gather_doubling(w_down, o_bf)
     gate_all = in_order(with_other_core([after(p, o_part) for p in gate_mine]), index)
     up_all = in_order(with_other_core([after(p, o_part) for p in up_mine[:-1]] + [after(up_mine[-1], o_bf)]), index)
     resid, normed_ff, mixed, p1, p2 = ff_forward(

time: 485 us -> 474 us (0.977)
  waiting for transfers between devices: 237 us -> 226 us
    ppermute x57, waiting for transfers between devices: 207 us -> 197 us  [xor_swap(): return lax.ppermute(x, axis, [(i, i ^ bit) for i in range(size)])]
  transfers between devices with their start and end apart: 62 -> 62, of which waited for: 19 -> 20; matrix products, arithmetic and copies ran while one was open for 9% -> 9% of each run, Pallas kernels for 12% -> 12%
where the time goes in v3:
time: 474 us; the launch traced here: 473 us
  waiting for transfers between devices  226 us (48%)
  starting transfers between devices  81.8 us (17%)
  Pallas kernels  57 us (12%)
  blocking collectives  51.6 us (11%)
  other arithmetic  29 us (6%)
  local copies, waits for them, and re-layouts  21.3 us (4%)
    ppermute x57, waiting for transfers between devices, xor_swap(): return lax.ppermute(x, axis, [(i, i ^ bit) for i in range(size)])  197 us
    ppermute x57, starting transfers between devices, xor_swap(): return lax.ppermute(x, axis, [(i, i ^ bit) for i in range(size)])  63.4 us
    all_gather x3, blocking collectives, all_reduce_tp(): return lax.all_gather(summed, 'tp', axis=0, tiled=True)  37.5 us
    pallas_call x4, Pallas kernels, weight_grads(): pl.pallas_call(body, out_shape=out_shape, in_specs=[smem()] + [vmem()] *...  17.2 us
    all_gather x1, blocking collectives, layer(): lax.all_gather(jnp.concatenate([packed, dkv_raw, tail], axis=0), 'tp', ax...  14.1 us
    pallas_call x1, Pallas kernels, ff_backward(): pl.pallas_call(body, out_shape=(jax.ShapeDtypeStruct((rows, width), F32),...  12.6 us
    all_to_all x1, waiting for transfers between devices, layer(): kv_stack = lax.all_to_all(spread, 'tp', 0, 0)  12.4 us
    all_to_all x1, waiting for transfers between devices, layer(): dkv = lax.all_to_all(dkv, 'tp', 0, 0)  12.2 us
  transfers between devices with their start and end apart: 62, of which 20 were waited for; matrix products, arithmetic and copies ran while one was open for 9% of the time, Pallas kernels for 12%

profile of v3, /device:TPU:0, one launch (start us, length us, event | category | flops | bytes accessed | tf_op | source)
XLA Modules:
  0.0 472.6 jit_solution(8593985435910975467)
XLA Ops:
  2.5 4.1 collective-permute-start
  6.6 1.6 collective-permute-start.1
  8.2 1.9 collective-permute-start.10
  10.1 1.3 broadcast_in_dim.27.g_ref.gain_ref
  12.6 5.2 %collective-permute-done.refs_1_ = bf16[160,640]{1,0:T(8,128)(2,1)S(1)} collective-permute-done((bf16[160,640]{1,0:T(8,128)(2,1)S(1)}, bf16[160,640]{1,0:T(8,128)(2,1)S(1)}, u32[]{:S(2)}, u32[]{:S(2)}) %collective-permute-start) | collective-permute-done | bytes 204832 | tf_op jit(solution)/shard_map/ppermute | solution.py:75
  17.9 4.9 %collective-permute-done.2.refs_3_ = bf16[160,640]{1,0:T(8,128)(2,1)S(1)} collective-permute-done((bf16[160,640]{1,0:T(8,128)(2,1)S(1)}, bf16[160,640]{1,0:T(8,128)(2,1)S(1)}, u32[]{:S(2)}, u32[]{:S(2)}) %collective-permute-start.2) | collective-permute-done | bytes 204832 | tf_op jit(solution)/shard_map/ppermute | solution.py:75
  23.5 1.9 multiply_sine_fusion
  25.4 14.7 %collective-permute-start.11 = (bf16[144,1728]{1,0:T(8,128)(2,1)S(1)}, bf16[144,1728]{1,0:T(8,128)(2,1)}, u32[]{:S(2)}, u32[]{:S(2)}) collective-permute-start(bf16[144,1728]{1,0:T(8,128)(2,1)S(1)} %copy-done.11), channel_id=1, source_target_pairs={{0,4},{4,0},{8,12},{12,8},{1,5},{5,1},{9,13},{13,9},{2,6},{6,2},{1... | collective-permute-start | bytes 1493000 | tf_op jit(solution)/shard_map/ppermute | solution.py:75
  40.9 4.2 qkv_kernel.1
  46.0 1.3 collective-permute-start.7
  47.3 2.0 collective-permute-start.8
  51.5 2.2 collective-permute-done.7
  53.6 3.4 collective-permute-start.17
  57.0 6.3 %collective-permute-done.8 = bf16[256,128]{1,0:T(8,128)(2,1)S(1)} collective-permute-done((bf16[256,128]{1,0:T(8,128)(2,1)S(1)}, bf16[256,128]{1,0:T(8,128)(2,1)S(1)}, u32[]{:S(2)}, u32[]{:S(2)}) %collective-permute-start.8) | collective-permute-done | bytes 65568 | tf_op jit(solution)/shard_map/ppermute | solution.py:75
  63.3 3.6 collective-permute-start.24
  68.0 3.7 all-to-all-start
  72.9 12.4 %all-to-all-done = bf16[4,1024,128]{2,1,0:T(8,128)(2,1)S(1)} async-done(((bf16[4,1024,128]{2,1,0:T(8,128)(2,1)}), bf16[4,1024,128]{2,1,0:T(8,128)(2,1)S(1)}, u32[]{:S(2)}, u32[]{:S(2)}) %all-to-all-start) | async-done | bytes 1048608 | tf_op jit(solution)/shard_map/all_to_all | solution.py:591
  90.2 3.5 all-to-all-start.1
  94.1 16.3 %collective-permute-done.12.refs_3_ = bf16[144,1728]{1,0:T(8,128)(2,1)} collective-permute-done((bf16[144,1728]{1,0:T(8,128)(2,1)}, bf16[144,1728]{1,0:T(8,128)(2,1)}, u32[]{:S(2)}, u32[]{:S(2)}) %collective-permute-start.12) | collective-permute-done | bytes 497696 | tf_op jit(solution)/shard_map/ppermute | solution.py:75
  111.8 13.3 %all_gather.15.o_ref = bf16[256,1152]{1,0:T(8,128)(2,1)} all-gather(bf16[64,1152]{1,0:T(8,128)(2,1)} %reduce_sum.183), channel_id=1, replica_groups=mesh['shard'=2,'ctx'=4,'tp'=4] {'tp'}, dimensions={0}, use_global_device_ids=true | all-gather | bytes 737280 | tf_op jit(solution)/shard_map/all_gather | solution.py:531
  125.1 6.5 %collective-permute-done.19.refs_11_ = bf16[144,1728]{1,0:T(8,128)(2,1)S(1)} collective-permute-done((bf16[144,1728]{1,0:T(8,128)(2,1)}, bf16[144,1728]{1,0:T(8,128)(2,1)S(1)}, u32[]{:S(2)}, u32[]{:S(2)}) %collective-permute-start.19) | collective-permute-done | bytes 497696 | tf_op jit(solution)/shard_map/ppermute | solution.py:75
  133.9 12.2 %collective-permute-done.26.refs_3_.refs_19_ = bf16[144,1728]{1,0:T(8,128)(2,1)} collective-permute-done((bf16[144,1728]{1,0:T(8,128)(2,1)}, bf16[144,1728]{1,0:T(8,128)(2,1)}, u32[]{:S(2)}, u32[]{:S(2)}) %collective-permute-start.26) | collective-permute-done | bytes 497696 | tf_op jit(solution)/shard_map/ppermute | solution.py:75
  148.3 1.8 constant_dynamic-slice_fusion.1
  150.1 1.6 collective-permute-start.33
  151.7 1.5 collective-permute-start.34
  155.6 10.8 %ff_forward.1 = (f32[256,1152]{1,0:T(8,128)}, bf16[256,1152]{1,0:T(8,128)(2,1)}, bf16[256,1728]{1,0:T(8,128)(2,1)}, bf16[256,1728]{1,0:T(8,128)(2,1)}, bf16[256,1728]{1,0:T(8,128)(2,1)}) custom-call(s32[8]{0:T(128)} %get-tuple-element.113.index_ref, bf16[256,1152]{1,0:T(8,128)(2,1)} %all_gather.15.o_ref, bf16[256,1152]{1,0:T(8,128)(2,1)} %bitcast.131, ...), custom_call_target="tpu_custom_call" | custom-call | tf_op jit(solution)/shard_map/ff_forward/pallas_call | solution.py:248
  167.2 5.6 %ff_down.1 = bf16[256,1152]{1,0:T(8,128)(2,1)} custom-call(s32[8]{0:T(128)} %get-tuple-element.113.index_ref, bf16[256,1728]{1,0:T(8,128)(2,1)} %get-tuple-element.76.mix_ref.refs_1_, bf16[144,1728]{1,0:T(8,128)(2,1)} %refs_16_, bf16[144,1728]{1,0:T(8,128)(2,1)} %collective-permute-done.24.refs_1_.refs_17_, bf16[144,1728]{1,0:T(8,128)(2,1)} %copy-done.12, ...), custom_call_target="tpu_custom_call" | custom-call | tf_op jit(solution)/shard_map/ff_down/pallas_call | solution.py:282
  172.8 3.9 all-to-all-start.2
  177.9 1.7 slice.437
  179.8 4.9 %all-to-all-done.2 = bf16[4,64,1152]{2,1,0:T(8,128)(2,1)S(1)} async-done(((bf16[4,64,1152]{2,1,0:T(8,128)(2,1)}), bf16[4,64,1152]{2,1,0:T(8,128)(2,1)S(1)}, u32[]{:S(2)}, u32[]{:S(2)}) %all-to-all-start.2) | async-done | bytes 589856 | tf_op jit(solution)/shard_map/all_to_all | solution.py:529
  184.8 11.7 %all_gather.16.f_ref = bf16[256,1152]{1,0:T(8,128)(2,1)} all-gather(bf16[64,1152]{1,0:T(8,128)(2,1)S(1)} %reduce_sum.184), channel_id=1, replica_groups=mesh['shard'=2,'ctx'=4,'tp'=4] {'tp'}, dimensions={0}, use_global_device_ids=true | all-gather | bytes 737280 | tf_op jit(solution)/shard_map/all_gather | solution.py:531
  196.5 12.6 %ff_backward.1 = (f32[256,1152]{1,0:T(8,128)}, bf16[256,1152]{1,0:T(8,128)(2,1)}, f32[1,1152]{1,0:T(1,128)}, bf16[256,1728]{1,0:T(8,128)(2,1)}, bf16[256,1728]{1,0:T(8,128)(2,1)}, /*index=5*/bf16[256,1152]{1,0:T(8,128)(2,1)}) custom-call(s32[8]{0:T(128)} %get-tuple-element.113.index_ref, bf16[256,1152]{1,0:T(8,128)(2,1)} %all_gather.16.f_ref, ...), custom_call_target="tpu_custom_call" | custom-call | tf_op jit(solution)/shard_map/ff_backward/pallas_call | solution.py:334
  209.1 3.6 all-to-all-start.3
  213.1 4.7 shard_map.266
  217.8 4.7 shard_map.265
  223.3 12.6 %all_gather.17 = bf16[256,1152]{1,0:T(8,128)(2,1)S(1)} all-gather(bf16[64,1152]{1,0:T(8,128)(2,1)} %reduce_sum.187), channel_id=1, replica_groups=mesh['shard'=2,'ctx'=4,'tp'=4] {'tp'}, dimensions={0}, use_global_device_ids=true | all-gather | bytes 737280 | tf_op jit(solution)/shard_map/all_gather | solution.py:531
  243.0 3.6 all-to-all-start.4
  247.8 12.2 %all-to-all-done.4 = bf16[4,4,64,512]{3,2,1,0:T(8,128)(2,1)S(1)} async-done(((bf16[4,4,64,512]{3,2,1,0:T(8,128)(2,1)}), bf16[4,4,64,512]{3,2,1,0:T(8,128)(2,1)S(1)}, u32[]{:S(2)}, u32[]{:S(2)}) %all-to-all-start.4) | async-done | bytes 1048608 | tf_op jit(solution)/shard_map/all_to_all | solution.py:663
  260.7 4.5 collective-permute-done.31
  265.3 2.2 collective-permute-start.32
  267.7 3.5 collective-permute-done.32
  271.6 14.1 %all-gather = bf16[832,512]{1,0:T(8,128)(2,1)} all-gather(bf16[208,512]{1,0:T(8,128)(2,1)S(1)} %maximum_maximum_fusion), channel_id=2, replica_groups=mesh['shard'=2,'ctx'=4,'tp'=4] {'tp'}, dimensions={0}, use_global_device_ids=true | all-gather | bytes 1064960 | tf_op jit(solution)/shard_map/all_gather | solution.py:687
  285.7 6.6 %input_kernel.1 = (f32[256,1152]{1,0:T(8,128)}, f32[1,1152]{1,0:T(1,128)}) custom-call(s32[2]{0:T(128)} %pad_add_fusion.1.place_ref, bf16[4,208,512]{2,1,0:T(8,128)(2,1)} %bitcast.133, bf16[1152,384]{1,0:T(8,128)(2,1)} %get-tuple-element.86.own_ref, f32[256,1152]{1,0:T(8,128)} %copy-done.2, bf16[256,1152]{1,0:T(8,128)(2,1)} %bitcast.132, ...), custom_call_target="tpu_custom_call" | custom-call | tf_op jit(solution)/shard_map/input_kernel/pallas_call | solution.py:469
  295.0 4.7 shard_map.264
  301.8 3.2 collective-permute-done.55
  305.0 1.7 collective-permute-start.56
  307.3 3.2 shard_map.263
  311.9 1.6 fusion.35
  313.5 2.1 collective-permute-start.52
  315.9 2.0 collective-permute-start.48
  318.0 1.5 fusion.31
  319.5 2.0 collective-permute-start.44
  321.6 6.5 %collective-permute-done.52 = bf16[144,1728]{1,0:T(8,128)(2,1)S(1)} collective-permute-done((bf16[144,1728]{1,0:T(8,128)(2,1)S(1)}, bf16[144,1728]{1,0:T(8,128)(2,1)S(1)}, u32[]{:S(2)}, u32[]{:S(2)}) %collective-permute-start.52) | collective-permute-done | bytes 497696 | tf_op jit(solution)/shard_map/ppermute | solution.py:75
  328.2 2.0 collective-permute-start.43
  331.4 18.9 %collective-permute-done.48 = bf16[144,1728]{1,0:T(8,128)(2,1)S(1)} collective-permute-done((bf16[144,1728]{1,0:T(8,128)(2,1)S(1)}, bf16[144,1728]{1,0:T(8,128)(2,1)S(1)}, u32[]{:S(2)}, u32[]{:S(2)}) %collective-permute-start.48) | collective-permute-done | bytes 497696 | tf_op jit(solution)/shard_map/ppermute | solution.py:75
  350.3 2.0 collective-permute-start.40
  352.5 38.7 %collective-permute-done.40 = bf16[2,144,640]{2,1,0:T(8,128)(2,1)S(1)} collective-permute-done((bf16[2,144,640]{2,1,0:T(8,128)(2,1)S(1)}, bf16[2,144,640]{2,1,0:T(8,128)(2,1)S(1)}, u32[]{:S(2)}, u32[]{:S(2)}) %collective-permute-start.40) | collective-permute-done | bytes 368672 | tf_op jit(solution)/shard_map/ppermute | solution.py:75
  392.3 2.0 collective-permute-start.41
  395.5 29.1 %collective-permute-done.41 = bf16[1,144,640]{2,1,0:T(8,128)(2,1)S(1)} collective-permute-done((bf16[1,144,640]{2,1,0:T(8,128)(2,1)S(1)}, bf16[1,144,640]{2,1,0:T(8,128)(2,1)S(1)}, u32[]{:S(2)}, u32[]{:S(2)}) %collective-permute-start.41) | collective-permute-done | bytes 184352 | tf_op jit(solution)/shard_map/ppermute | solution.py:75
  426.1 2.9 collective-permute-start.45
  429.0 2.3 fusion.19
  431.3 28.1 %collective-permute-done.49 = bf16[144,1728]{1,0:T(8,128)(2,1)S(1)} collective-permute-done((bf16[144,1728]{1,0:T(8,128)(2,1)S(1)}, bf16[144,1728]{1,0:T(8,128)(2,1)S(1)}, u32[]{:S(2)}, u32[]{:S(2)}) %collective-permute-start.49) | collective-permute-done | bytes 497696 | tf_op jit(solution)/shard_map/ppermute | solution.py:75
  460.6 9.7 %collective-permute-done.45 = bf16[144,1728]{1,0:T(8,128)(2,1)S(1)} collective-permute-done((bf16[144,1728]{1,0:T(8,128)(2,1)S(1)}, bf16[144,1728]{1,0:T(8,128)(2,1)S(1)}, u32[]{:S(2)}, u32[]{:S(2)}) %collective-permute-start.45) | collective-permute-done | bytes 497696 | tf_op jit(solution)/shard_map/ppermute | solution.py:75
  470.4 2.2 fusion.23
  (292 shorter events, 49.7 us)
Async XLA Ops:
  2.5 15.4 %collective-permute-start = (bf16[160,640]{1,0:T(8,128)(2,1)S(1)}, bf16[160,640]{1,0:T(8,128)(2,1)S(1)}, u32[]{:S(2)}, u32[]{:S(2)}) collective-permute-start(bf16[160,640]{1,0:T(8,128)(2,1)S(1)} %fusion.43.refs_0_), channel_id=1, source_target_pairs={{0,8},{4,12},{8,0},{12,4},{1,9},{5,13},{9,1},{13,5},{2,10},{6,14},... | collective-permute-start | bytes 614408 | tf_op jit(solution)/shard_map/ppermute | solution.py:75
  6.6 11.2 %collective-permute-start.1 = (bf16[160,640]{1,0:T(8,128)(2,1)S(1)}, bf16[160,640]{1,0:T(8,128)(2,1)S(1)}, u32[]{:S(2)}, u32[]{:S(2)}) collective-permute-start(bf16[160,640]{1,0:T(8,128)(2,1)S(1)} %fusion.43.refs_0_), channel_id=1, source_target_pairs={{0,4},{4,0},{8,12},{12,8},{1,5},{5,1},{9,13},{13,9},{2,6},{6,2},{1... | collective-permute-start | bytes 614408 | tf_op jit(solution)/shard_map/ppermute | solution.py:75
  8.2 14.6 %collective-permute-start.2 = (bf16[160,640]{1,0:T(8,128)(2,1)S(1)}, bf16[160,640]{1,0:T(8,128)(2,1)S(1)}, u32[]{:S(2)}, u32[]{:S(2)}) collective-permute-start(bf16[160,640]{1,0:T(8,128)(2,1)S(1)} %fusion.43.refs_0_), channel_id=1, source_target_pairs={{0,12},{4,8},{8,4},{12,0},{1,13},{5,9},{9,5},{13,1},{2,14},{6,10},... | collective-permute-start | bytes 614408 | tf_op jit(solution)/shard_map/ppermute | solution.py:75
  8.2 17.2 %collective-permute-start.3 = (bf16[160,640]{1,0:T(8,128)(2,1)S(1)}, bf16[160,640]{1,0:T(8,128)(2,1)S(1)}, u32[]{:S(2)}, u32[]{:S(2)}) collective-permute-start(bf16[160,640]{1,0:T(8,128)(2,1)S(1)} %fusion.43.refs_0_), channel_id=1, source_target_pairs={{0,16},{16,0},{1,17},{17,1},{2,18},{18,2},{3,19},{19,3},{4,20},{20... | collective-permute-start | bytes 614408 | tf_op jit(solution)/shard_map/ppermute | solution.py:75
  8.2 64.6 %collective-permute-start.10 = (bf16[144,1728]{1,0:T(8,128)(2,1)}, bf16[144,1728]{1,0:T(8,128)(2,1)}, u32[]{:S(2)}, u32[]{:S(2)}) collective-permute-start(bf16[144,1728]{1,0:T(8,128)(2,1)} %refs_0_.2), channel_id=1, source_target_pairs={{0,8},{4,12},{8,0},{12,4},{1,9},{5,13},{9,1},{13,5},{2,10},{6,14},... | collective-permute-start | bytes 1493000 | tf_op jit(solution)/shard_map/ppermute | solution.py:75
  22.9 17.1 %collective-permute-start.4 = (bf16[160,640]{1,0:T(8,128)(2,1)S(1)}, bf16[160,640]{1,0:T(8,128)(2,1)S(1)}, u32[]{:S(2)}, u32[]{:S(2)}) collective-permute-start(bf16[160,640]{1,0:T(8,128)(2,1)S(1)} %collective-permute-done.refs_1_), channel_id=1, source_target_pairs={{0,16},{16,0},{1,17},{17,1},{2,18},{18,2},{3,19},{19,3},{4,20},{20... | collective-permute-start | bytes 614408 | tf_op jit(solution)/shard_map/ppermute | solution.py:75
  22.9 17.1 %collective-permute-start.5 = (bf16[160,640]{1,0:T(8,128)(2,1)S(1)}, bf16[160,640]{1,0:T(8,128)(2,1)S(1)}, u32[]{:S(2)}, u32[]{:S(2)}) collective-permute-start(bf16[160,640]{1,0:T(8,128)(2,1)S(1)} %collective-permute-done.1.refs_2_), channel_id=1, source_target_pairs={{0,16},{16,0},{1,17},{17,1},{2,18},{18,2},{3,19},{19,3},{4,20},{20... | collective-permute-start | bytes 614408 | tf_op jit(solution)/shard_map/ppermute | solution.py:75
  23.4 16.7 %collective-permute-start.6 = (bf16[160,640]{1,0:T(8,128)(2,1)S(1)}, bf16[160,640]{1,0:T(8,128)(2,1)S(1)}, u32[]{:S(2)}, u32[]{:S(2)}) collective-permute-start(bf16[160,640]{1,0:T(8,128)(2,1)S(1)} %collective-permute-done.2.refs_3_), channel_id=1, source_target_pairs={{0,16},{16,0},{1,17},{17,1},{2,18},{18,2},{3,19},{19,3},{4,20},{20... | collective-permute-start | bytes 614408 | tf_op jit(solution)/shard_map/ppermute | solution.py:75
  25.4 85.0 %collective-permute-start.11 = (bf16[144,1728]{1,0:T(8,128)(2,1)S(1)}, bf16[144,1728]{1,0:T(8,128)(2,1)}, u32[]{:S(2)}, u32[]{:S(2)}) collective-permute-start(bf16[144,1728]{1,0:T(8,128)(2,1)S(1)} %copy-done.11), channel_id=1, source_target_pairs={{0,4},{4,0},{8,12},{12,8},{1,5},{5,1},{9,13},{13,9},{2,6},{6,2},{1... | collective-permute-start | bytes 1493000 | tf_op jit(solution)/shard_map/ppermute | solution.py:75
  46.0 7.6 %collective-permute-start.7 = (bf16[256,128]{1,0:T(8,128)(2,1)S(1)}, bf16[256,128]{1,0:T(8,128)(2,1)S(1)}, u32[]{:S(2)}, u32[]{:S(2)}) collective-permute-start(bf16[256,128]{1,0:T(8,128)(2,1)S(1)} %slice.596), channel_id=1, source_target_pairs={{0,8},{4,12},{8,0},{12,4},{1,9},{5,13},{9,1},{13,5},{2,10},{6,14},... | collective-permute-start | bytes 196616 | tf_op jit(solution)/shard_map/ppermute | solution.py:75
  47.3 16.0 %collective-permute-start.8 = (bf16[256,128]{1,0:T(8,128)(2,1)S(1)}, bf16[256,128]{1,0:T(8,128)(2,1)S(1)}, u32[]{:S(2)}, u32[]{:S(2)}) collective-permute-start(bf16[256,128]{1,0:T(8,128)(2,1)S(1)} %slice.596), channel_id=1, source_target_pairs={{0,4},{4,0},{8,12},{12,8},{1,5},{5,1},{9,13},{13,9},{2,6},{6,2},{1... | collective-permute-start | bytes 196616 | tf_op jit(solution)/shard_map/ppermute | solution.py:75
  49.3 14.0 %collective-permute-start.9 = (bf16[256,128]{1,0:T(8,128)(2,1)S(1)}, bf16[256,128]{1,0:T(8,128)(2,1)S(1)}, u32[]{:S(2)}, u32[]{:S(2)}) collective-permute-start(bf16[256,128]{1,0:T(8,128)(2,1)S(1)} %slice.596), channel_id=1, source_target_pairs={{0,12},{4,8},{8,4},{12,0},{1,13},{5,9},{9,5},{13,1},{2,14},{6,10},... | collective-permute-start | bytes 196616 | tf_op jit(solution)/shard_map/ppermute | solution.py:75
  53.6 40.1 %collective-permute-start.17 = (bf16[144,1728]{1,0:T(8,128)(2,1)}, bf16[144,1728]{1,0:T(8,128)(2,1)}, u32[]{:S(2)}, u32[]{:S(2)}) collective-permute-start(bf16[144,1728]{1,0:T(8,128)(2,1)} %refs_8_.1), channel_id=1, source_target_pairs={{0,8},{4,12},{8,0},{12,4},{1,9},{5,13},{9,1},{13,5},{2,10},{6,14},... | collective-permute-start | bytes 1493000 | tf_op jit(solution)/shard_map/ppermute | solution.py:75
  63.3 47.6 %collective-permute-start.18 = (bf16[144,1728]{1,0:T(8,128)(2,1)}, bf16[144,1728]{1,0:T(8,128)(2,1)}, u32[]{:S(2)}, u32[]{:S(2)}) collective-permute-start(bf16[144,1728]{1,0:T(8,128)(2,1)} %refs_8_.1), channel_id=1, source_target_pairs={{0,4},{4,0},{8,12},{12,8},{1,5},{5,1},{9,13},{13,9},{2,6},{6,2},{1... | collective-permute-start | bytes 1493000 | tf_op jit(solution)/shard_map/ppermute | solution.py:75
  63.3 47.1 %collective-permute-start.24 = (bf16[144,1728]{1,0:T(8,128)(2,1)}, bf16[144,1728]{1,0:T(8,128)(2,1)}, u32[]{:S(2)}, u32[]{:S(2)}) collective-permute-start(bf16[144,1728]{1,0:T(8,128)(2,1)} %refs_16_), channel_id=1, source_target_pairs={{0,8},{4,12},{8,0},{12,4},{1,9},{5,13},{9,1},{13,5},{2,10},{6,14},... | collective-permute-start | bytes 1493000 | tf_op jit(solution)/shard_map/ppermute | solution.py:75
  68.0 17.2 %all-to-all-start = ((bf16[4,1024,128]{2,1,0:T(8,128)(2,1)}), bf16[4,1024,128]{2,1,0:T(8,128)(2,1)S(1)}, u32[]{:S(2)}, u32[]{:S(2)}) async-start(bf16[4,1024,128]{2,1,0:T(8,128)(2,1)} %broadcast_in_dim.28), calls=%async_computation | async-start | bytes 2097152 | tf_op jit(solution)/shard_map/all_to_all | solution.py:591
  72.8 37.6 %collective-permute-start.12 = (bf16[144,1728]{1,0:T(8,128)(2,1)}, bf16[144,1728]{1,0:T(8,128)(2,1)}, u32[]{:S(2)}, u32[]{:S(2)}) collective-permute-start(bf16[144,1728]{1,0:T(8,128)(2,1)} %collective-permute-done.10.refs_1_), channel_id=1, source_target_pairs={{0,4},{4,0},{8,12},{12,8},{1,5},{5,1},{9,13},{13,9},{2,6},{6,2},{1... | collective-permute-start | bytes 1493000 | tf_op jit(solution)/shard_map/ppermute | solution.py:75
  88.6 149.0 %copy-start.24 = (bf16[256,256]{1,0:T(8,128)(2,1)}, bf16[256,256]{1,0:T(8,128)(2,1)S(1)}, u32[]{:S(2)}) copy-start(bf16[256,256]{1,0:T(8,128)(2,1)S(1)} %fusion.12.refs_3_) | copy-start | bytes 393220
  90.2 20.8 %all-to-all-start.1 = ((bf16[4,64,1152]{2,1,0:T(8,128)(2,1)}), bf16[4,64,1152]{2,1,0:T(8,128)(2,1)S(1)}, u32[]{:S(2)}, u32[]{:S(2)}) async-start(bf16[4,64,1152]{2,1,0:T(8,128)(2,1)} %bitcast.11), calls=%async_computation.1 | async-start | bytes 1179648 | tf_op jit(solution)/shard_map/all_to_all | solution.py:529
  93.7 61.0 %copy-start.45 = (f32[1152]{0:T(1024)S(1)}, f32[1152]{0:T(1024)}, u32[]{:S(2)}) copy-start(f32[1152]{0:T(1024)} %param.32) | copy-start | bytes 13828
  93.8 31.3 %collective-permute-start.25 = (bf16[144,1728]{1,0:T(8,128)(2,1)}, bf16[144,1728]{1,0:T(8,128)(2,1)S(1)}, u32[]{:S(2)}, u32[]{:S(2)}) collective-permute-start(bf16[144,1728]{1,0:T(8,128)(2,1)} %refs_16_), channel_id=1, source_target_pairs={{0,4},{4,0},{8,12},{12,8},{1,5},{5,1},{9,13},{13,9},{2,6},{6,2},{1... | collective-permute-start | bytes 1493000 | tf_op jit(solution)/shard_map/ppermute | solution.py:75
  110.4 21.3 %collective-permute-start.19 = (bf16[144,1728]{1,0:T(8,128)(2,1)}, bf16[144,1728]{1,0:T(8,128)(2,1)S(1)}, u32[]{:S(2)}, u32[]{:S(2)}) collective-permute-start(bf16[144,1728]{1,0:T(8,128)(2,1)} %collective-permute-done.17.refs_9_), channel_id=1, source_target_pairs={{0,4},{4,0},{8,12},{12,8},{1,5},{5,1},{9,13},{13,9},{2,6},{6,2},{1... | collective-permute-start | bytes 1493000 | tf_op jit(solution)/shard_map/ppermute | solution.py:75
  110.4 21.3 %collective-permute-start.16 = (bf16[144,1728]{1,0:T(8,128)(2,1)}, bf16[144,1728]{1,0:T(8,128)(2,1)}, u32[]{:S(2)}, u32[]{:S(2)}) collective-permute-start(bf16[144,1728]{1,0:T(8,128)(2,1)} %collective-permute-done.12.refs_3_), channel_id=1, source_target_pairs={{0,16},{16,0},{1,17},{17,1},{2,18},{18,2},{3,19},{19,3},{4,20},{20... | collective-permute-start | bytes 1493000 | tf_op jit(solution)/shard_map/ppermute | solution.py:75
  110.4 21.3 %collective-permute-start.14 = (bf16[144,1728]{1,0:T(8,128)(2,1)}, bf16[144,1728]{1,0:T(8,128)(2,1)}, u32[]{:S(2)}, u32[]{:S(2)}) collective-permute-start(bf16[144,1728]{1,0:T(8,128)(2,1)} %collective-permute-done.10.refs_1_), channel_id=1, source_target_pairs={{0,16},{16,0},{1,17},{17,1},{2,18},{18,2},{3,19},{19,3},{4,20},{20... | collective-permute-start | bytes 1493000 | tf_op jit(solution)/shard_map/ppermute | solution.py:75
  110.9 21.3 %collective-permute-start.15 = (bf16[144,1728]{1,0:T(8,128)(2,1)}, bf16[144,1728]{1,0:T(8,128)(2,1)}, u32[]{:S(2)}, u32[]{:S(2)}) collective-permute-start(bf16[144,1728]{1,0:T(8,128)(2,1)} %collective-permute-done.11.refs_2_), channel_id=1, source_target_pairs={{0,16},{16,0},{1,17},{17,1},{2,18},{18,2},{3,19},{19,3},{4,20},{20... | collective-permute-start | bytes 1493000 | tf_op jit(solution)/shard_map/ppermute | solution.py:75
  125.1 7.3 %collective-permute-start.21 = (bf16[144,1728]{1,0:T(8,128)(2,1)}, bf16[144,1728]{1,0:T(8,128)(2,1)S(1)}, u32[]{:S(2)}, u32[]{:S(2)}) collective-permute-start(bf16[144,1728]{1,0:T(8,128)(2,1)} %collective-permute-done.17.refs_9_), channel_id=1, source_target_pairs={{0,16},{16,0},{1,17},{17,1},{2,18},{18,2},{3,19},{19,3},{4,20},{20... | collective-permute-start | bytes 1493000 | tf_op jit(solution)/shard_map/ppermute | solution.py:75
  131.7 2.1 collective-permute-start.22
  131.7 14.5 %collective-permute-start.26 = (bf16[144,1728]{1,0:T(8,128)(2,1)}, bf16[144,1728]{1,0:T(8,128)(2,1)}, u32[]{:S(2)}, u32[]{:S(2)}) collective-permute-start(bf16[144,1728]{1,0:T(8,128)(2,1)} %collective-permute-done.24.refs_1_.refs_17_), channel_id=1, source_target_pairs={{0,4},{4,0},{8,12},{12,8},{1,5},{5,1},{9,13},{13,9},{2,6},{6,2},{1... | collective-permute-start | bytes 1493000 | tf_op jit(solution)/shard_map/ppermute | solution.py:75
  131.8 14.4 %collective-permute-start.13 = (bf16[144,1728]{1,0:T(8,128)(2,1)S(1)}, bf16[144,1728]{1,0:T(8,128)(2,1)S(1)}, u32[]{:S(2)}, u32[]{:S(2)}) collective-permute-start(bf16[144,1728]{1,0:T(8,128)(2,1)S(1)} %copy-done.11), channel_id=1, source_target_pairs={{0,16},{16,0},{1,17},{17,1},{2,18},{18,2},{3,19},{19,3},{4,20},{20... | collective-permute-start | bytes 1493000 | tf_op jit(solution)/shard_map/ppermute | solution.py:75
  132.2 14.7 %collective-permute-start.20 = (bf16[144,1728]{1,0:T(8,128)(2,1)}, bf16[144,1728]{1,0:T(8,128)(2,1)S(1)}, u32[]{:S(2)}, u32[]{:S(2)}) collective-permute-start(bf16[144,1728]{1,0:T(8,128)(2,1)} %refs_8_.1), channel_id=1, source_target_pairs={{0,16},{16,0},{1,17},{17,1},{2,18},{18,2},{3,19},{19,3},{4,20},{20... | collective-permute-start | bytes 1493000 | tf_op jit(solution)/shard_map/ppermute | solution.py:75
  132.3 17.7 %collective-permute-start.28 = (bf16[144,1728]{1,0:T(8,128)(2,1)}, bf16[144,1728]{1,0:T(8,128)(2,1)}, u32[]{:S(2)}, u32[]{:S(2)}) collective-permute-start(bf16[144,1728]{1,0:T(8,128)(2,1)} %collective-permute-done.24.refs_1_.refs_17_), channel_id=1, source_target_pairs={{0,16},{16,0},{1,17},{17,1},{2,18},{18,2},{3,19},{19,3},{4,20},{20... | collective-permute-start | bytes 1493000 | tf_op jit(solution)/shard_map/ppermute | solution.py:75
  133.8 17.9 %collective-permute-start.29 = (bf16[144,1728]{1,0:T(8,128)(2,1)S(1)}, bf16[144,1728]{1,0:T(8,128)(2,1)}, u32[]{:S(2)}, u32[]{:S(2)}) collective-permute-start(bf16[144,1728]{1,0:T(8,128)(2,1)S(1)} %collective-permute-done.25.refs_2_.refs_18_), channel_id=1, source_target_pairs={{0,16},{16,0},{1,17},{17,1},{2,18},{18,2},{3,19},{19,3},{4,20},{20... | collective-permute-start | bytes 1493000 | tf_op jit(solution)/shard_map/ppermute | solution.py:75
  146.1 7.0 %collective-permute-start.23 = (bf16[144,1728]{1,0:T(8,128)(2,1)S(1)}, bf16[144,1728]{1,0:T(8,128)(2,1)}, u32[]{:S(2)}, u32[]{:S(2)}) collective-permute-start(bf16[144,1728]{1,0:T(8,128)(2,1)S(1)} %collective-permute-done.19.refs_11_), channel_id=1, source_target_pairs={{0,16},{16,0},{1,17},{17,1},{2,18},{18,2},{3,19},{19,3},{4,20},{20... | collective-permute-start | bytes 1493000 | tf_op jit(solution)/shard_map/ppermute | solution.py:75
  146.2 20.2 %collective-permute-start.27 = (bf16[144,1728]{1,0:T(8,128)(2,1)}, bf16[144,1728]{1,0:T(8,128)(2,1)S(1)}, u32[]{:S(2)}, u32[]{:S(2)}) collective-permute-start(bf16[144,1728]{1,0:T(8,128)(2,1)} %refs_16_), channel_id=1, source_target_pairs={{0,16},{16,0},{1,17},{17,1},{2,18},{18,2},{3,19},{19,3},{4,20},{20... | collective-permute-start | bytes 1493000 | tf_op jit(solution)/shard_map/ppermute | solution.py:75
  147.8 18.7 %collective-permute-start.30 = (bf16[144,1728]{1,0:T(8,128)(2,1)}, bf16[144,1728]{1,0:T(8,128)(2,1)}, u32[]{:S(2)}, u32[]{:S(2)}) collective-permute-start(bf16[144,1728]{1,0:T(8,128)(2,1)} %collective-permute-done.26.refs_3_.refs_19_), channel_id=1, source_target_pairs={{0,16},{16,0},{1,17},{17,1},{2,18},{18,2},{3,19},{19,3},{4,20},{20... | collective-permute-start | bytes 1493000 | tf_op jit(solution)/shard_map/ppermute | solution.py:75
  150.1 27.2 %collective-permute-start.33 = (bf16[576,384]{1,0:T(8,128)(2,1)}, bf16[576,384]{1,0:T(8,128)(2,1)}, u32[]{:S(2)}, u32[]{:S(2)}) collective-permute-start(bf16[576,384]{1,0:T(8,128)(2,1)} %constant_dynamic-slice_fusion.1), channel_id=1, source_target_pairs={{0,2},{1,3},{2,0},{3,1},{4,6},{5,7},{6,4},{7,5},{8,10},{9,11},{10,... | collective-permute-start | bytes 1327112 | tf_op jit(solution)/shard_map/ppermute | solution.py:75
  151.7 25.6 %collective-permute-start.34 = (bf16[576,384]{1,0:T(8,128)(2,1)}, bf16[576,384]{1,0:T(8,128)(2,1)}, u32[]{:S(2)}, u32[]{:S(2)}) collective-permute-start(bf16[576,384]{1,0:T(8,128)(2,1)} %constant_dynamic-slice_fusion.1), channel_id=1, source_target_pairs={{0,1},{1,0},{2,3},{3,2},{4,5},{5,4},{6,7},{7,6},{8,9},{9,8},{10,11... | collective-permute-start | bytes 1327112 | tf_op jit(solution)/shard_map/ppermute | solution.py:75
  153.2 24.6 %collective-permute-start.35 = (bf16[576,384]{1,0:T(8,128)(2,1)}, bf16[576,384]{1,0:T(8,128)(2,1)}, u32[]{:S(2)}, u32[]{:S(2)}) collective-permute-start(bf16[576,384]{1,0:T(8,128)(2,1)} %constant_dynamic-slice_fusion.1), channel_id=1, source_target_pairs={{0,3},{1,2},{2,1},{3,0},{4,7},{5,6},{6,5},{7,4},{8,11},{9,10},{10,... | collective-permute-start | bytes 1327112 | tf_op jit(solution)/shard_map/ppermute | solution.py:75
  172.8 12.0 %all-to-all-start.2 = ((bf16[4,64,1152]{2,1,0:T(8,128)(2,1)}), bf16[4,64,1152]{2,1,0:T(8,128)(2,1)S(1)}, u32[]{:S(2)}, u32[]{:S(2)}) async-start(bf16[4,64,1152]{2,1,0:T(8,128)(2,1)} %bitcast.137), calls=%async_computation.2 | async-start | bytes 1179648 | tf_op jit(solution)/shard_map/all_to_all | solution.py:529
  177.3 108.4 %collective-permute-start.36 = (bf16[576,384]{1,0:T(8,128)(2,1)}, bf16[576,384]{1,0:T(8,128)(2,1)}, u32[]{:S(2)}, u32[]{:S(2)}) collective-permute-start(bf16[576,384]{1,0:T(8,128)(2,1)} %collective-permute-done.33.refs_0_), channel_id=1, source_target_pairs={{0,16},{16,0},{1,17},{17,1},{2,18},{18,2},{3,19},{19,3},{4,20},{20... | collective-permute-start | bytes 1327112 | tf_op jit(solution)/shard_map/ppermute | solution.py:75
  177.3 108.4 %collective-permute-start.37 = (bf16[576,384]{1,0:T(8,128)(2,1)}, bf16[576,384]{1,0:T(8,128)(2,1)}, u32[]{:S(2)}, u32[]{:S(2)}) collective-permute-start(bf16[576,384]{1,0:T(8,128)(2,1)} %collective-permute-done.34.refs_1_), channel_id=1, source_target_pairs={{0,16},{16,0},{1,17},{17,1},{2,18},{18,2},{3,19},{19,3},{4,20},{20... | collective-permute-start | bytes 1327112 | tf_op jit(solution)/shard_map/ppermute | solution.py:75
  177.8 107.9 %collective-permute-start.38 = (bf16[576,384]{1,0:T(8,128)(2,1)}, bf16[576,384]{1,0:T(8,128)(2,1)}, u32[]{:S(2)}, u32[]{:S(2)}) collective-permute-start(bf16[576,384]{1,0:T(8,128)(2,1)} %collective-permute-done.35.refs_2_), channel_id=1, source_target_pairs={{0,16},{16,0},{1,17},{17,1},{2,18},{18,2},{3,19},{19,3},{4,20},{20... | collective-permute-start | bytes 1327112 | tf_op jit(solution)/shard_map/ppermute | solution.py:75
  209.1 13.4 %all-to-all-start.3 = ((bf16[4,64,1152]{2,1,0:T(8,128)(2,1)}), bf16[4,64,1152]{2,1,0:T(8,128)(2,1)S(1)}, u32[]{:S(2)}, u32[]{:S(2)}) async-start(bf16[4,64,1152]{2,1,0:T(8,128)(2,1)} %bitcast.140), calls=%async_computation.3 | async-start | bytes 1179648 | tf_op jit(solution)/shard_map/all_to_all | solution.py:529
  217.7 94.1 %collective-permute-start.50 = (bf16[4,144,1728]{2,1,0:T(8,128)(2,1)}, bf16[4,144,1728]{2,1,0:T(8,128)(2,1)}, u32[]{:S(2)}, u32[]{:S(2)}) collective-permute-start(bf16[4,144,1728]{2,1,0:T(8,128)(2,1)} %get-tuple-element.101), channel_id=1, source_target_pairs={{0,16},{16,0},{1,17},{17,1},{2,18},{18,2},{3,19},{19,3},{4,20},{20... | collective-permute-start | bytes 5971976 | tf_op jit(solution)/shard_map/ppermute | solution.py:75
  243.0 17.0 %all-to-all-start.4 = ((bf16[4,4,64,512]{3,2,1,0:T(8,128)(2,1)}), bf16[4,4,64,512]{3,2,1,0:T(8,128)(2,1)S(1)}, u32[]{:S(2)}, u32[]{:S(2)}) async-start(bf16[4,4,64,512]{3,2,1,0:T(8,128)(2,1)} %copy_bitcast_fusion), calls=%async_computation.4 | async-start | bytes 2097152 | tf_op jit(solution)/shard_map/all_to_all | solution.py:663
  260.2 5.0 %collective-permute-start.31 = (bf16[128,512]{1,0:T(8,128)(2,1)S(1)}, bf16[128,512]{1,0:T(8,128)(2,1)S(1)}, u32[]{:S(2)}, u32[]{:S(2)}) collective-permute-start(bf16[128,512]{1,0:T(8,128)(2,1)S(1)} %bitcast.142), channel_id=1, source_target_pairs={{0,4},{4,0},{8,12},{12,8},{1,5},{5,1},{9,13},{13,9},{2,6},{6,2},{1... | collective-permute-start | bytes 393224 | tf_op jit(solution)/shard_map/ppermute | solution.py:75
  265.3 5.9 %collective-permute-start.32 = (bf16[64,512]{1,0:T(8,128)(2,1)S(1)}, bf16[64,512]{1,0:T(8,128)(2,1)S(1)}, u32[]{:S(2)}, u32[]{:S(2)}) collective-permute-start(bf16[64,512]{1,0:T(8,128)(2,1)S(1)} %slice.433), channel_id=1, source_target_pairs={{0,8},{4,12},{8,0},{12,4},{1,9},{5,13},{9,1},{13,5},{2,10},{6,14},... | collective-permute-start | bytes 196616 | tf_op jit(solution)/shard_map/ppermute | solution.py:75
  271.2 44.4 %collective-permute-start.46 = (bf16[4,144,1728]{2,1,0:T(8,128)(2,1)}, bf16[4,144,1728]{2,1,0:T(8,128)(2,1)S(1)}, u32[]{:S(2)}, u32[]{:S(2)}) collective-permute-start(bf16[4,144,1728]{2,1,0:T(8,128)(2,1)} %get-tuple-element.98), channel_id=1, source_target_pairs={{0,16},{16,0},{1,17},{17,1},{2,18},{18,2},{3,19},{19,3},{4,20},{20... | collective-permute-start | bytes 5971976 | tf_op jit(solution)/shard_map/ppermute | solution.py:75
  294.9 6.4 %collective-permute-start.54 = (bf16[4,1,640]{2,0,1:T(4,128)(2,1)S(1)}, bf16[4,1,640]{2,0,1:T(4,128)(2,1)S(1)}, u32[]{:S(2)}, u32[]{:S(2)}) collective-permute-start(bf16[4,1,640]{2,0,1:T(4,128)(2,1)S(1)} %fusion.47), channel_id=1, source_target_pairs={{0,16},{16,0},{1,17},{17,1},{2,18},{18,2},{3,19},{19,3},{4,20},{20... | collective-permute-start | bytes 15368 | tf_op jit(solution)/shard_map/ppermute | solution.py:75
  299.7 18.2 %collective-permute-start.42 = (bf16[4,144,1728]{2,1,0:T(8,128)(2,1)}, bf16[4,144,1728]{2,1,0:T(8,128)(2,1)}, u32[]{:S(2)}, u32[]{:S(2)}) collective-permute-start(bf16[4,144,1728]{2,1,0:T(8,128)(2,1)} %get-tuple-element.94), channel_id=1, source_target_pairs={{0,16},{16,0},{1,17},{17,1},{2,18},{18,2},{3,19},{19,3},{4,20},{20... | collective-permute-start | bytes 5971976 | tf_op jit(solution)/shard_map/ppermute | solution.py:75
  301.3 3.7 collective-permute-start.55
  305.0 5.6 %collective-permute-start.56 = (bf16[1,1,640]{2,0,1:T(2,128)(2,1)S(1)}, bf16[1,1,640]{2,0,1:T(2,128)(2,1)S(1)}, u32[]{:S(2)}, u32[]{:S(2)}) collective-permute-start(bf16[1,1,640]{2,0,1:T(2,128)(2,1)S(1)} %fusion.51), channel_id=1, source_target_pairs={{0,8},{4,12},{8,0},{12,4},{1,9},{5,13},{9,1},{13,5},{2,10},{6,14},... | collective-permute-start | bytes 3848 | tf_op jit(solution)/shard_map/ppermute | solution.py:75
  310.5 9.0 %collective-permute-start.39 = (bf16[4,144,640]{2,1,0:T(8,128)(2,1)}, bf16[4,144,640]{2,1,0:T(8,128)(2,1)S(1)}, u32[]{:S(2)}, u32[]{:S(2)}) collective-permute-start(bf16[4,144,640]{2,1,0:T(8,128)(2,1)} %get-tuple-element.90), channel_id=1, source_target_pairs={{0,16},{16,0},{1,17},{17,1},{2,18},{18,2},{3,19},{19,3},{4,20},{20... | collective-permute-start | bytes 2211848 | tf_op jit(solution)/shard_map/ppermute | solution.py:75
  313.5 14.7 %collective-permute-start.52 = (bf16[144,1728]{1,0:T(8,128)(2,1)S(1)}, bf16[144,1728]{1,0:T(8,128)(2,1)S(1)}, u32[]{:S(2)}, u32[]{:S(2)}) collective-permute-start(bf16[144,1728]{1,0:T(8,128)(2,1)S(1)} %get-tuple-element.121), channel_id=1, source_target_pairs={{0,4},{4,0},{8,12},{12,8},{1,5},{5,1},{9,13},{13,9},{2,6},{6,2},{1... | collective-permute-start | bytes 1493000 | tf_op jit(solution)/shard_map/ppermute | solution.py:75
  315.6 110.5 %collective-permute-start.51 = (bf16[144,1728]{1,0:T(8,128)(2,1)S(1)}, bf16[144,1728]{1,0:T(8,128)(2,1)S(1)}, u32[]{:S(2)}, u32[]{:S(2)}) collective-permute-start(bf16[144,1728]{1,0:T(8,128)(2,1)S(1)} %get-tuple-element.120), channel_id=1, source_target_pairs={{0,4},{4,0},{8,12},{12,8},{1,5},{5,1},{9,13},{13,9},{2,6},{6,2},{1... | collective-permute-start | bytes 1493000 | tf_op jit(solution)/shard_map/ppermute | solution.py:75
  315.9 34.4 %collective-permute-start.48 = (bf16[144,1728]{1,0:T(8,128)(2,1)S(1)}, bf16[144,1728]{1,0:T(8,128)(2,1)S(1)}, u32[]{:S(2)}, u32[]{:S(2)}) collective-permute-start(bf16[144,1728]{1,0:T(8,128)(2,1)S(1)} %get-tuple-element.123), channel_id=1, source_target_pairs={{0,4},{4,0},{8,12},{12,8},{1,5},{5,1},{9,13},{13,9},{2,6},{6,2},{1... | collective-permute-start | bytes 1493000 | tf_op jit(solution)/shard_map/ppermute | solution.py:75
  317.9 113.4 %collective-permute-start.47 = (bf16[144,1728]{1,0:T(8,128)(2,1)S(1)}, bf16[144,1728]{1,0:T(8,128)(2,1)S(1)}, u32[]{:S(2)}, u32[]{:S(2)}) collective-permute-start(bf16[144,1728]{1,0:T(8,128)(2,1)S(1)} %get-tuple-element.122), channel_id=1, source_target_pairs={{0,4},{4,0},{8,12},{12,8},{1,5},{5,1},{9,13},{13,9},{2,6},{6,2},{1... | collective-permute-start | bytes 1493000 | tf_op jit(solution)/shard_map/ppermute | solution.py:75
  319.5 72.7 %collective-permute-start.44 = (bf16[144,1728]{1,0:T(8,128)(2,1)S(1)}, bf16[144,1728]{1,0:T(8,128)(2,1)S(1)}, u32[]{:S(2)}, u32[]{:S(2)}) collective-permute-start(bf16[144,1728]{1,0:T(8,128)(2,1)S(1)} %get-tuple-element.125), channel_id=1, source_target_pairs={{0,4},{4,0},{8,12},{12,8},{1,5},{5,1},{9,13},{13,9},{2,6},{6,2},{1... | collective-permute-start | bytes 1493000 | tf_op jit(solution)/shard_map/ppermute | solution.py:75
  328.2 132.5 %collective-permute-start.43 = (bf16[144,1728]{1,0:T(8,128)(2,1)S(1)}, bf16[144,1728]{1,0:T(8,128)(2,1)S(1)}, u32[]{:S(2)}, u32[]{:S(2)}) collective-permute-start(bf16[144,1728]{1,0:T(8,128)(2,1)S(1)} %get-tuple-element.124), channel_id=1, source_target_pairs={{0,4},{4,0},{8,12},{12,8},{1,5},{5,1},{9,13},{13,9},{2,6},{6,2},{1... | collective-permute-start | bytes 1493000 | tf_op jit(solution)/shard_map/ppermute | solution.py:75
  350.3 40.9 %collective-permute-start.40 = (bf16[2,144,640]{2,1,0:T(8,128)(2,1)S(1)}, bf16[2,144,640]{2,1,0:T(8,128)(2,1)S(1)}, u32[]{:S(2)}, u32[]{:S(2)}) collective-permute-start(bf16[2,144,640]{2,1,0:T(8,128)(2,1)S(1)} %add_convert_fusion.6), channel_id=1, source_target_pairs={{0,4},{4,0},{8,12},{12,8},{1,5},{5,1},{9,13},{13,9},{2,6},{6,2},{1... | collective-permute-start | bytes 1105928 | tf_op jit(solution)/shard_map/ppermute | solution.py:75
  391.2 37.8 %collective-permute-start.53 = (bf16[144,1728]{1,0:T(8,128)(2,1)S(1)}, bf16[144,1728]{1,0:T(8,128)(2,1)S(1)}, u32[]{:S(2)}, u32[]{:S(2)}) collective-permute-start(bf16[144,1728]{1,0:T(8,128)(2,1)S(1)} %fusion.18), channel_id=1, source_target_pairs={{0,8},{4,12},{8,0},{12,4},{1,9},{5,13},{9,1},{13,5},{2,10},{6,14},... | collective-permute-start | bytes 1493000 | tf_op jit(solution)/shard_map/ppermute | solution.py:75
  392.3 32.3 %collective-permute-start.41 = (bf16[1,144,640]{2,1,0:T(8,128)(2,1)S(1)}, bf16[1,144,640]{2,1,0:T(8,128)(2,1)S(1)}, u32[]{:S(2)}, u32[]{:S(2)}) collective-permute-start(bf16[1,144,640]{2,1,0:T(8,128)(2,1)S(1)} %add_convert_fusion.7), channel_id=1, source_target_pairs={{0,8},{4,12},{8,0},{12,4},{1,9},{5,13},{9,1},{13,5},{2,10},{6,14},... | collective-permute-start | bytes 552968 | tf_op jit(solution)/shard_map/ppermute | solution.py:75
  424.6 34.8 %collective-permute-start.49 = (bf16[144,1728]{1,0:T(8,128)(2,1)S(1)}, bf16[144,1728]{1,0:T(8,128)(2,1)S(1)}, u32[]{:S(2)}, u32[]{:S(2)}) collective-permute-start(bf16[144,1728]{1,0:T(8,128)(2,1)S(1)} %fusion.20), channel_id=1, source_target_pairs={{0,8},{4,12},{8,0},{12,4},{1,9},{5,13},{9,1},{13,5},{2,10},{6,14},... | collective-permute-start | bytes 1493000 | tf_op jit(solution)/shard_map/ppermute | solution.py:75
  426.1 44.3 %collective-permute-start.45 = (bf16[144,1728]{1,0:T(8,128)(2,1)S(1)}, bf16[144,1728]{1,0:T(8,128)(2,1)S(1)}, u32[]{:S(2)}, u32[]{:S(2)}) collective-permute-start(bf16[144,1728]{1,0:T(8,128)(2,1)S(1)} %fusion.22), channel_id=1, source_target_pairs={{0,8},{4,12},{8,0},{12,4},{1,9},{5,13},{9,1},{13,5},{2,10},{6,14},... | collective-permute-start | bytes 1493000 | tf_op jit(solution)/shard_map/ppermute | solution.py:75
  (46 other events, 483.3 us)
